TPU v7x, 32 devices: a whole 2x2x4 slice. The times are simulated.
32 devices in a mesh: section: 2 (over x), dp: 4 (over y, core), tensor: 4 (over z).
Axes of the slice: x: 2, y: 2, z: 4, core: 2. Of those that a mesh axis runs over, the one named last changes fastest.
Arguments:
- tokens: bfloat16 [8, 704, 768], P('dp', 'tensor'), may hold values from -6 to 6
- segment_ids: int32 [8, 704], P('dp'), may hold values from 0 to 3, as said below
- cotangent: bfloat16 [8, 704, 768], P('dp', 'tensor'), may hold values from -6 to 6
- norm_gain1: float32 [2, 768], P('section'), may hold values from 0.5 to 1.5
- w_in: bfloat16 [2, 768, 3, 768], P('section', None, None, 'tensor'), may hold values from -0.21875 to 0.21875
- short_taps: float32 [2, 3, 3, 768], P('section', None, None, 'tensor'), may hold values from -4 to 4
- cond_taps: float32 [2, 3, 768], P('section', None, 'tensor'), may hold values from -4 to 4
- spectrum: float32 [2, 2, 705, 768], P('section', None, None, 'tensor'), may hold values from -6 to 6
- spectral_gain: float32 [2, 2, 768], P('section', None, 'tensor'), may hold values from 0.3 to 3
- w_out: bfloat16 [2, 768, 768], P('section', 'tensor'), may hold values from -0.4375 to 0.4375
- norm_gain2: float32 [2, 768], P('section'), may hold values from 0.5 to 1.5
- w_gate_up: bfloat16 [2, 768, 2, 3072], P('section', None, None, 'tensor'), may hold values from -0.21875 to 0.21875
- w_down: bfloat16 [2, 3072, 768], P('section', 'tensor'), may hold values from -0.15625 to 0.15625
Outputs:
- layer_out: float32 [2, 8, 704, 768], P('section', 'dp', 'tensor')
- grad_in: float32 [2, 8, 704, 768], P('section', 'dp', 'tensor')
- grad_norm_gain1: float32 [2, 768], P('section')
- grad_w_in: float32 [2, 768, 3, 768], P('section', None, None, 'tensor')
- grad_short_taps: float32 [2, 3, 3, 768], P('section', None, None, 'tensor')
- grad_cond_taps: float32 [2, 3, 768], P('section', None, 'tensor')
- grad_spectrum: float32 [2, 2, 705, 768], P('section', None, None, 'tensor')
- grad_spectral_gain: float32 [2, 2, 768], P('section', None, 'tensor')
- grad_w_out: float32 [2, 768, 768], P('section', 'tensor')
- grad_norm_gain2: float32 [2, 768], P('section')
- grad_w_gate_up: float32 [2, 768, 2, 3072], P('section', None, None, 'tensor')
- grad_w_down: float32 [2, 3072, 768], P('section', 'tensor')
Inputs may be any that keep to these rules, and one draw needn't show every extreme that they name: `segment_ids`: in each pack the ids never fall along the rows, and each of the 4 ids holds one or more rows.
All inputs are finite; a program needn't handle non-finite values.
Results may differ from a plain program's by a relative error of at most 0.022.
The roundings to bfloat16 on the way count: a program that leaves them out, or rounds other values in their place, can miss the bound.
Values may be sent and summed in bfloat16 or wider, within the bound.
No kernel may reach another device: no remote copies, remote signals or barrier semaphores. Data moves between devices by JAX's collectives and lax.ppermute only.
A program may use at most 192 MiB of HBM per device.

v0:
```python
from functools import partial
import math

import jax
import jax.numpy as jnp
from jax import lax
from jax.sharding import PartitionSpec as P

SEGS = 4


highest = lax.Precision.HIGHEST


def from_behind(shard, axis, by):
    peers = lax.axis_size(axis)
    pairs = [(i, i + by) for i in range(peers) if 0 <= i + by < peers]
    return lax.ppermute(shard, axis, pairs)


def layer_norm(values, gain):
    row_mean = jnp.mean(values, axis=-1, keepdims=True)
    centred = values - row_mean
    variance = jnp.mean(centred * centred, axis=-1, keepdims=True)
    return centred * lax.rsqrt(variance + 1e-05) * gain


def neighbours(segments):
    equal = (segments[1:] == segments[:-1]).astype(jnp.float32)
    blank = jnp.zeros((1,), jnp.float32)
    return (jnp.concatenate([blank, equal]), jnp.concatenate([equal, blank]))


def masked_short(values, taps, same_prev, same_next):
    blank = jnp.zeros((1, values.shape[1]), values.dtype)
    before = jnp.concatenate([blank, values[:-1]], axis=0) * same_prev[:, None]
    after = jnp.concatenate([values[1:], blank], axis=0) * same_next[:, None]
    return taps[0] * before + taps[1] * values + taps[2] * after


def spectral_tables(pack_len):
    period = 2 * pack_len
    freq_index = lax.broadcasted_iota(jnp.int32, (pack_len + 1, pack_len), 0)
    place_index = lax.broadcasted_iota(jnp.int32, (pack_len + 1, pack_len), 1)
    angle = (freq_index * place_index % period).astype(jnp.float32) * (2.0 * math.pi / period)
    cosine = jnp.cos(angle)
    sine = jnp.sin(angle)
    forward_table = jnp.concatenate([cosine, -sine], axis=0)
    freq_column = freq_index[:, :1]
    column_weight = jnp.where((freq_column == 0) | (freq_column == pack_len), 1.0, 2.0) / period
    inverse_table = jnp.concatenate([cosine * column_weight, -sine * column_weight], axis=0).T
    return (forward_table, inverse_table)


def orchid_mix(proj, short_taps, cond_taps, spectrum, spectral_gain, segments, tables):
    forward_table, inverse_table = tables
    pack_len = proj.shape[0]
    channels = proj.shape[1] // 3
    freqs = pack_len + 1
    same_prev, same_next = neighbours(segments)
    shorted = masked_short(proj, short_taps, same_prev, same_next)
    query = shorted[:, :channels]
    key_part = shorted[:, channels : 2 * channels]
    value_part = shorted[:, 2 * channels :]
    condition = masked_short(key_part, cond_taps, same_prev, same_next)
    cond_hat = jnp.dot(forward_table, condition, precision=highest)
    scale_in = spectral_gain[0] / math.sqrt(pack_len)
    filt_re = spectrum[0] + spectral_gain[1] * jnp.tanh(scale_in * cond_hat[:freqs])
    filt_im = spectrum[1] + spectral_gain[1] * jnp.tanh(scale_in * cond_hat[freqs:])
    masks = (segments[:, None] == jnp.arange(SEGS, dtype=jnp.int32)[None, :]).astype(jnp.float32)
    pieces = (masks[:, :, None] * value_part[:, None, :]).reshape(pack_len, SEGS * channels)
    piece_hat = jnp.dot(forward_table, pieces, precision=highest).reshape(2, freqs, SEGS, channels)
    real_part = piece_hat[0] * filt_re[:, None, :] - piece_hat[1] * filt_im[:, None, :]
    imag_part = piece_hat[0] * filt_im[:, None, :] + piece_hat[1] * filt_re[:, None, :]
    joined = jnp.concatenate([real_part, imag_part], axis=0).reshape(2 * freqs, SEGS * channels)
    conv = jnp.dot(inverse_table, joined, precision=highest).reshape(pack_len, SEGS, channels)
    mixed = jnp.sum(conv * masks[:, :, None], axis=1)
    return query * mixed


def glu_act(both_parts):
    half_width = both_parts.shape[1] // 2
    return jax.nn.silu(both_parts[:, :half_width]) * both_parts[:, half_width:]


def mixer_local(gathered, segments, params, tables):
    (
        gain_one,
        w_in,
        short_taps,
        cond_taps,
        spectrum,
        spectral_gain,
        w_out,
        gain_two,
        w_gate_up,
        w_down,
    ) = params
    proj = jnp.dot(gathered, w_in, preferred_element_type=jnp.float32)
    mixer = partial(orchid_mix, segments=segments, tables=tables)
    mixed, mix_pull = jax.vjp(mixer, proj, short_taps, cond_taps, spectrum, spectral_gain)
    return (mixed.astype(jnp.bfloat16), mix_pull)


def glu_local(gathered_two, w_gate_up):
    both_parts = jnp.dot(gathered_two, w_gate_up, preferred_element_type=jnp.float32)
    act, act_pull = jax.vjp(glu_act, both_parts)
    return (act.astype(jnp.bfloat16), act_pull)


def run_layer(layer_input, segments, params, tables, finish):
    (
        gain_one,
        w_in,
        short_taps,
        cond_taps,
        spectrum,
        spectral_gain,
        w_out,
        gain_two,
        w_gate_up,
        w_down,
    ) = params
    normed, norm_pull = jax.vjp(layer_norm, layer_input, gain_one)
    gathered = lax.all_gather(normed.astype(jnp.bfloat16), "tensor", axis=0, tiled=True)
    mixed_low, mix_pull = mixer_local(gathered, segments, params, tables)
    hidden = layer_input + lax.psum_scatter(
        jnp.dot(mixed_low, w_out, preferred_element_type=jnp.float32),
        "tensor",
        scatter_dimension=0,
        tiled=True,
    )
    normed_two, norm_pull_two = jax.vjp(layer_norm, hidden, gain_two)
    gathered_two = lax.all_gather(normed_two.astype(jnp.bfloat16), "tensor", axis=0, tiled=True)
    act_low, act_pull = glu_local(gathered_two, w_gate_up)
    saved = (
        norm_pull,
        gathered,
        mixed_low,
        mix_pull,
        norm_pull_two,
        gathered_two,
        act_pull,
        act_low,
    )
    front_rows = (gathered, hidden, gathered_two)
    if finish:
        return (
            hidden
            + lax.psum_scatter(
                jnp.dot(act_low, w_down, preferred_element_type=jnp.float32),
                "tensor",
                scatter_dimension=0,
                tiled=True,
            ),
            saved,
            front_rows,
        )
    return (hidden, saved, front_rows)


def back_layer(layer_input, segments, params, tables, grad_out):
    (
        gain_one,
        w_in,
        short_taps,
        cond_taps,
        spectrum,
        spectral_gain,
        w_out,
        gain_two,
        w_gate_up,
        w_down,
    ) = params
    hidden, saved, front_rows = run_layer(layer_input, segments, params, tables, False)
    norm_pull, gathered, mixed_low, mix_pull, norm_pull_two, gathered_two, act_pull, act_low = saved
    grad_rows = lax.all_gather(grad_out.astype(jnp.bfloat16), "tensor", axis=0, tiled=True)
    grad_act = jnp.einsum("ld,fd->lf", grad_rows, w_down, preferred_element_type=jnp.float32)
    grad_down = jnp.einsum("lf,ld->fd", act_low, grad_rows, preferred_element_type=jnp.float32)
    grad_both = act_pull(grad_act)[0].astype(jnp.bfloat16)
    grad_gate_up = jnp.einsum(
        "ld,lf->df", gathered_two, grad_both, preferred_element_type=jnp.float32
    )
    piece = grad_both
    grad_normed_two = lax.psum_scatter(
        jnp.einsum("lf,df->ld", piece, w_gate_up, preferred_element_type=jnp.float32),
        "tensor",
        scatter_dimension=0,
        tiled=True,
    )
    grad_hidden_part, grad_gain_two = norm_pull_two(grad_normed_two)
    grad_hidden = grad_out + grad_hidden_part
    grad_mix_rows = lax.all_gather(grad_hidden.astype(jnp.bfloat16), "tensor", axis=0, tiled=True)
    grad_mixed = jnp.einsum("ld,cd->lc", grad_mix_rows, w_out, preferred_element_type=jnp.float32)
    grad_w_out = jnp.einsum(
        "lc,ld->cd", mixed_low, grad_mix_rows, preferred_element_type=jnp.float32
    )
    grad_proj, grad_short, grad_cond, grad_spectrum, grad_spectral = mix_pull(grad_mixed)
    grad_proj_low = grad_proj.astype(jnp.bfloat16)
    grad_w_in = jnp.einsum("ld,lc->dc", gathered, grad_proj_low, preferred_element_type=jnp.float32)
    piece = grad_proj_low
    grad_normed = lax.psum_scatter(
        jnp.einsum("lc,dc->ld", piece, w_in, preferred_element_type=jnp.float32),
        "tensor",
        scatter_dimension=0,
        tiled=True,
    )
    grad_input_part, grad_gain_one = norm_pull(grad_normed)
    grad_input = grad_hidden + grad_input_part
    weight_terms = (
        grad_w_in,
        grad_short,
        grad_cond,
        grad_spectrum,
        grad_spectral,
        grad_w_out,
        grad_gate_up,
        grad_down,
    )
    return (grad_input, (grad_gain_one, grad_gain_two), weight_terms)


def per_device(
    tokens,
    segment_ids,
    cotangent,
    norm_gain1,
    w_in,
    short_taps,
    cond_taps,
    spectrum,
    spectral_gain,
    w_out,
    norm_gain2,
    w_gate_up,
    w_down,
):
    pack_count, row_count, model_width = tokens.shape
    pack_len = segment_ids.shape[1]
    channels = w_in.shape[3]
    hidden_cols = w_gate_up.shape[3]
    params = (
        norm_gain1[0],
        w_in[0].reshape(model_width, 3 * channels),
        short_taps[0].reshape(3, 3 * channels),
        cond_taps[0],
        spectrum[0],
        spectral_gain[0],
        w_out[0],
        norm_gain2[0],
        w_gate_up[0].reshape(model_width, 2 * hidden_cols),
        w_down[0],
    )
    tables = spectral_tables(pack_len)
    section_index = lax.axis_index("section")
    last_section = lax.axis_size("section") - 1
    step_count = pack_count + last_section

    def forward_step(loop_state, step_index):
        sent, kept_in, kept_out, kept_extra = loop_state
        received = from_behind(sent, "section", 1)
        micro = step_index - section_index
        is_valid = (micro >= 0) & (micro < pack_count)
        slot_index = jnp.clip(micro, 0, pack_count - 1)
        own_rows = lax.dynamic_index_in_dim(tokens, slot_index, 0, keepdims=False).astype(
            jnp.float32
        )
        layer_input = jnp.where(section_index == 0, own_rows, received)
        segments = lax.dynamic_index_in_dim(segment_ids, slot_index, 0, keepdims=False)
        result, unused_saved, front_rows = run_layer(layer_input, segments, params, tables, True)
        kept_in = jnp.where(
            is_valid, lax.dynamic_update_index_in_dim(kept_in, layer_input, slot_index, 0), kept_in
        )
        kept_out = jnp.where(
            is_valid, lax.dynamic_update_index_in_dim(kept_out, result, slot_index, 0), kept_out
        )
        return ((result, kept_in, kept_out, kept_extra), None)

    extra_start = ()
    start_state = (
        jnp.zeros((row_count, model_width), jnp.float32),
        jnp.zeros((pack_count, row_count, model_width), jnp.float32),
        jnp.zeros((pack_count, row_count, model_width), jnp.float32),
        extra_start,
    )
    (unused_rows, kept_in, kept_out, kept_extra), unused_steps = lax.scan(
        forward_step, start_state, jnp.arange(step_count)
    )
    weight_shapes = (
        params[1],
        params[2],
        params[3],
        params[4],
        params[5],
        params[6],
        params[8],
        params[9],
    )
    zero_weights = tuple((jnp.zeros(array.shape, jnp.float32) for array in weight_shapes))
    zero_gains = (jnp.zeros((model_width,), jnp.float32), jnp.zeros((model_width,), jnp.float32))

    def backward_step(loop_state, step_index):
        sent, kept_grad, gain_totals, weight_totals = loop_state
        received = from_behind(sent, "section", -1)
        micro = step_index - (last_section - section_index)
        is_valid = (micro >= 0) & (micro < pack_count)
        slot_index = jnp.clip(micro, 0, pack_count - 1)
        own_grad = lax.dynamic_index_in_dim(cotangent, slot_index, 0, keepdims=False).astype(
            jnp.float32
        )
        grad_out = jnp.where(section_index == last_section, own_grad, received)
        layer_input = lax.dynamic_index_in_dim(kept_in, slot_index, 0, keepdims=False)
        segments = lax.dynamic_index_in_dim(segment_ids, slot_index, 0, keepdims=False)
        grad_input, gain_terms, weight_terms = back_layer(
            layer_input, segments, params, tables, grad_out
        )
        gain_terms = tuple((jnp.where(is_valid, term, 0.0) for term in gain_terms))
        term_in, term_short, term_cond, term_spec, term_gain, term_out, term_gate_up, term_down = (
            tuple((jnp.where(is_valid, term, 0.0) for term in weight_terms))
        )
        new_terms = (
            term_in,
            term_short,
            term_cond,
            term_spec,
            term_gain,
            term_out,
            term_gate_up,
            term_down,
        )
        weight_totals = tuple((total + term for total, term in zip(weight_totals, new_terms)))
        gain_totals = tuple((total + term for total, term in zip(gain_totals, gain_terms)))
        kept_grad = jnp.where(
            is_valid,
            lax.dynamic_update_index_in_dim(kept_grad, grad_input, slot_index, 0),
            kept_grad,
        )
        return ((grad_input, kept_grad, gain_totals, weight_totals), None)

    back_start = (
        jnp.zeros((row_count, model_width), jnp.float32),
        jnp.zeros((pack_count, row_count, model_width), jnp.float32),
        zero_gains,
        zero_weights,
    )
    (unused_grad, kept_grad, gain_totals, weight_totals), unused_back = lax.scan(
        backward_step, back_start, jnp.arange(step_count)
    )
    sum_in, sum_short, sum_cond, sum_spec, sum_gain, sum_out, sum_gate_up, sum_down = weight_totals
    sum_in, sum_short, sum_cond, sum_spec, sum_gain, sum_out, sum_gate_up, sum_down = lax.psum(
        (sum_in, sum_short, sum_cond, sum_spec, sum_gain, sum_out, sum_gate_up, sum_down), "dp"
    )
    gain_first, gain_second = gain_totals
    gain_first, gain_second = lax.psum((gain_first, gain_second), ("dp", "tensor"))
    return (
        kept_out[None],
        kept_grad[None],
        gain_first[None],
        sum_in.reshape(1, model_width, 3, channels),
        sum_short.reshape(1, 3, 3, channels),
        sum_cond[None],
        sum_spec[None],
        sum_gain[None],
        sum_out[None],
        gain_second[None],
        sum_gate_up.reshape(1, model_width, 2, hidden_cols),
        sum_down[None],
    )


def solution(mesh):
    return jax.shard_map(
        per_device,
        mesh=mesh,
        in_specs=(
            P("dp", "tensor", None),
            P("dp", None),
            P("dp", "tensor", None),
            P("section", None),
            P("section", None, None, "tensor"),
            P("section", None, None, "tensor"),
            P("section", None, "tensor"),
            P("section", None, None, "tensor"),
            P("section", None, "tensor"),
            P("section", "tensor", None),
            P("section", None),
            P("section", None, None, "tensor"),
            P("section", "tensor", None),
        ),
        out_specs=(
            P("section", "dp", "tensor", None),
            P("section", "dp", "tensor", None),
            P("section", None),
            P("section", None, None, "tensor"),
            P("section", None, None, "tensor"),
            P("section", None, "tensor"),
            P("section", None, None, "tensor"),
            P("section", None, "tensor"),
            P("section", "tensor", None),
            P("section", None),
            P("section", None, None, "tensor"),
            P("section", "tensor", None),
        ),
        check_vma=False,
    )
```

profile of v0, /device:TPU:0, one launch (start us, length us, event | category | flops | bytes accessed | tf_op | source)
XLA Modules:
  0.0 2237.0 jit_solution(2906031752056489237)
XLA Ops:
  48.2 704.4 %while.51 = (s32[]{:T(128)}, f32[176,768]{1,0:T(8,128)S(1)}, f32[2,176,768]{2,1,0:T(8,128)S(1)}, f32[2,176,768]{2,1,0:T(8,128)}, pred[]{:T(512)}, /*index=5*/s32...) while((s32[]{:T(128)}, f32[176,768]{1,0:T(8,128)S(1)}, ...), condition=%wide.region_8.9_spmd.clone, body=%wide.region_0.8_spmd.clone.sunk | while | flops 23922319360 | bytes 190306960 | solution.py:286
  67.5 30.6 %all-gather.7.cloned.1.call-done = bf16[704,768]{1,0:T(8,128)(2,1)} async-done(((bf16[176,768]{1,0:T(8,128)(2,1)}), bf16[704,768]{1,0:T(8,128)(2,1)}) %all-gather.7.cloned.1.call-update) | async-done | bytes 1081360 | tf_op jit(solution)/shard_map/while/body/eval_jaxpr/all_gather | solution.py:125
  157.9 43.8 %reduce-scatter.6.cloned.1.call-done = f32[176,768]{1,0:T(8,128)} async-done(((f32[704,768]{1,0:T(8,128)}), f32[176,768]{1,0:T(8,128)}) %reduce-scatter.6.cloned.1.call-update) | async-done | bytes 540688 | tf_op jit(solution)/shard_map/while/body/eval_jaxpr/reduce_scatter | solution.py:127
  204.0 28.0 %all-gather.9.cloned.1.call-done = bf16[704,768]{1,0:T(8,128)(2,1)} async-done(((bf16[176,768]{1,0:T(8,128)(2,1)}), bf16[704,768]{1,0:T(8,128)(2,1)}) %all-gather.9.cloned.1.call-update) | async-done | bytes 1081360 | tf_op jit(solution)/shard_map/while/body/eval_jaxpr/all_gather | solution.py:134
  238.6 44.6 %reduce-scatter.8.cloned.1.call-done = f32[176,768]{1,0:T(8,128)} async-done(((f32[704,768]{1,0:T(8,128)}), f32[176,768]{1,0:T(8,128)}) %reduce-scatter.8.cloned.1.call-update) | async-done | bytes 540688 | tf_op jit(solution)/shard_map/while/body/eval_jaxpr/reduce_scatter | solution.py:150
  302.8 28.9 %all-gather.7.cloned.1.call-done = bf16[704,768]{1,0:T(8,128)(2,1)} async-done(((bf16[176,768]{1,0:T(8,128)(2,1)}), bf16[704,768]{1,0:T(8,128)(2,1)}) %all-gather.7.cloned.1.call-update) | async-done | bytes 1081360 | tf_op jit(solution)/shard_map/while/body/eval_jaxpr/all_gather | solution.py:125
  391.5 43.8 %reduce-scatter.6.cloned.1.call-done = f32[176,768]{1,0:T(8,128)} async-done(((f32[704,768]{1,0:T(8,128)}), f32[176,768]{1,0:T(8,128)}) %reduce-scatter.6.cloned.1.call-update) | async-done | bytes 540688 | tf_op jit(solution)/shard_map/while/body/eval_jaxpr/reduce_scatter | solution.py:127
  437.7 28.0 %all-gather.9.cloned.1.call-done = bf16[704,768]{1,0:T(8,128)(2,1)} async-done(((bf16[176,768]{1,0:T(8,128)(2,1)}), bf16[704,768]{1,0:T(8,128)(2,1)}) %all-gather.9.cloned.1.call-update) | async-done | bytes 1081360 | tf_op jit(solution)/shard_map/while/body/eval_jaxpr/all_gather | solution.py:134
  472.2 44.6 %reduce-scatter.8.cloned.1.call-done = f32[176,768]{1,0:T(8,128)} async-done(((f32[704,768]{1,0:T(8,128)}), f32[176,768]{1,0:T(8,128)}) %reduce-scatter.8.cloned.1.call-update) | async-done | bytes 540688 | tf_op jit(solution)/shard_map/while/body/eval_jaxpr/reduce_scatter | solution.py:150
  536.4 28.9 %all-gather.7.cloned.1.call-done = bf16[704,768]{1,0:T(8,128)(2,1)} async-done(((bf16[176,768]{1,0:T(8,128)(2,1)}), bf16[704,768]{1,0:T(8,128)(2,1)}) %all-gather.7.cloned.1.call-update) | async-done | bytes 1081360 | tf_op jit(solution)/shard_map/while/body/eval_jaxpr/all_gather | solution.py:125
  625.1 43.8 %reduce-scatter.6.cloned.1.call-done = f32[176,768]{1,0:T(8,128)} async-done(((f32[704,768]{1,0:T(8,128)}), f32[176,768]{1,0:T(8,128)}) %reduce-scatter.6.cloned.1.call-update) | async-done | bytes 540688 | tf_op jit(solution)/shard_map/while/body/eval_jaxpr/reduce_scatter | solution.py:127
  671.3 28.0 %all-gather.9.cloned.1.call-done = bf16[704,768]{1,0:T(8,128)(2,1)} async-done(((bf16[176,768]{1,0:T(8,128)(2,1)}), bf16[704,768]{1,0:T(8,128)(2,1)}) %all-gather.9.cloned.1.call-update) | async-done | bytes 1081360 | tf_op jit(solution)/shard_map/while/body/eval_jaxpr/all_gather | solution.py:134
  705.8 44.6 %reduce-scatter.8.cloned.1.call-done = f32[176,768]{1,0:T(8,128)} async-done(((f32[704,768]{1,0:T(8,128)}), f32[176,768]{1,0:T(8,128)}) %reduce-scatter.8.cloned.1.call-update) | async-done | bytes 540688 | tf_op jit(solution)/shard_map/while/body/eval_jaxpr/reduce_scatter | solution.py:150
  753.6 1268.6 %while.52 = (s32[]{:T(128)}, f32[176,768]{1,0:T(8,128)}, f32[2,176,768]{2,1,0:T(8,128)}, f32[768]{0:T(1024)}, f32[768]{0:T(1024)}, /*index=5*/f32[768,576]{0,1:T...) while((s32[]{:T(128)}, f32[176,768]{1,0:T(8,128)}, ...), condition=%wide.region_39.40_spmd.clone, body=%wide.region_9.39_spmd.clone.sunk | while | flops 50368700416 | bytes 605911616 | solution.py:346
  759.0 25.9 %all-gather.11.cloned.1.call-done = bf16[704,768]{1,0:T(8,128)(2,1)} async-done(((bf16[176,768]{1,0:T(8,128)(2,1)}), bf16[704,768]{1,0:T(8,128)(2,1)}) %all-gather.11.cloned.1.call-update) | async-done | bytes 1081360 | tf_op jit(solution)/shard_map/while/body/eval_jaxpr/all_gather | solution.py:125
  850.3 43.2 %reduce-scatter.10.cloned.1.call-done = f32[176,768]{1,0:T(8,128)} async-done(((f32[704,768]{1,0:T(8,128)}), f32[176,768]{1,0:T(8,128)}) %reduce-scatter.10.cloned.1.call-update) | async-done | bytes 540688 | tf_op jit(solution)/shard_map/while/body/eval_jaxpr/reduce_scatter | solution.py:127
  931.1 23.5 %all-gather.15.cloned.1.call-done = bf16[704,768]{1,0:T(8,128)(2,1)} async-done(((bf16[176,768]{1,0:T(8,128)(2,1)}), bf16[704,768]{1,0:T(8,128)(2,1)}) %all-gather.15.cloned.1.call-update) | async-done | bytes 1081360 | tf_op jit(solution)/shard_map/while/body/eval_jaxpr/all_gather | solution.py:177
  964.5 44.5 %reduce-scatter.12.cloned.1.call-done = f32[176,768]{1,0:T(8,128)} async-done(((f32[704,768]{1,0:T(8,128)}), f32[176,768]{1,0:T(8,128)}) %reduce-scatter.12.cloned.1.call-update) | async-done | bytes 540688 | tf_op jit(solution)/shard_map/while/body/eval_jaxpr/reduce_scatter | solution.py:185
  1144.2 26.5 %reduce-scatter.14.cloned.1.call-done = f32[176,768]{1,0:T(8,128)} async-done(((f32[704,768]{1,0:T(8,128)}), f32[176,768]{1,0:T(8,128)}) %reduce-scatter.14.cloned.1.call-update) | async-done | bytes 540688 | tf_op jit(solution)/shard_map/while/body/eval_jaxpr/reduce_scatter | solution.py:202
  1181.1 25.9 %all-gather.11.cloned.1.call-done = bf16[704,768]{1,0:T(8,128)(2,1)} async-done(((bf16[176,768]{1,0:T(8,128)(2,1)}), bf16[704,768]{1,0:T(8,128)(2,1)}) %all-gather.11.cloned.1.call-update) | async-done | bytes 1081360 | tf_op jit(solution)/shard_map/while/body/eval_jaxpr/all_gather | solution.py:125
  1272.3 43.3 %reduce-scatter.10.cloned.1.call-done = f32[176,768]{1,0:T(8,128)} async-done(((f32[704,768]{1,0:T(8,128)}), f32[176,768]{1,0:T(8,128)}) %reduce-scatter.10.cloned.1.call-update) | async-done | bytes 540688 | tf_op jit(solution)/shard_map/while/body/eval_jaxpr/reduce_scatter | solution.py:127
  1353.2 23.7 %all-gather.15.cloned.1.call-done = bf16[704,768]{1,0:T(8,128)(2,1)} async-done(((bf16[176,768]{1,0:T(8,128)(2,1)}), bf16[704,768]{1,0:T(8,128)(2,1)}) %all-gather.15.cloned.1.call-update) | async-done | bytes 1081360 | tf_op jit(solution)/shard_map/while/body/eval_jaxpr/all_gather | solution.py:177
  1386.7 44.5 %reduce-scatter.12.cloned.1.call-done = f32[176,768]{1,0:T(8,128)} async-done(((f32[704,768]{1,0:T(8,128)}), f32[176,768]{1,0:T(8,128)}) %reduce-scatter.12.cloned.1.call-update) | async-done | bytes 540688 | tf_op jit(solution)/shard_map/while/body/eval_jaxpr/reduce_scatter | solution.py:185
  1445.3 20.0 all-gather.17.cloned.1.call-done
  1569.3 23.5 %reduce-scatter.14.cloned.1.call-done = f32[176,768]{1,0:T(8,128)} async-done(((f32[704,768]{1,0:T(8,128)}), f32[176,768]{1,0:T(8,128)}) %reduce-scatter.14.cloned.1.call-update) | async-done | bytes 540688 | tf_op jit(solution)/shard_map/while/body/eval_jaxpr/reduce_scatter | solution.py:202
  1603.3 25.9 %all-gather.11.cloned.1.call-done = bf16[704,768]{1,0:T(8,128)(2,1)} async-done(((bf16[176,768]{1,0:T(8,128)(2,1)}), bf16[704,768]{1,0:T(8,128)(2,1)}) %all-gather.11.cloned.1.call-update) | async-done | bytes 1081360 | tf_op jit(solution)/shard_map/while/body/eval_jaxpr/all_gather | solution.py:125
  1694.5 43.2 %reduce-scatter.10.cloned.1.call-done = f32[176,768]{1,0:T(8,128)} async-done(((f32[704,768]{1,0:T(8,128)}), f32[176,768]{1,0:T(8,128)}) %reduce-scatter.10.cloned.1.call-update) | async-done | bytes 540688 | tf_op jit(solution)/shard_map/while/body/eval_jaxpr/reduce_scatter | solution.py:127
  1775.4 23.5 %all-gather.15.cloned.1.call-done = bf16[704,768]{1,0:T(8,128)(2,1)} async-done(((bf16[176,768]{1,0:T(8,128)(2,1)}), bf16[704,768]{1,0:T(8,128)(2,1)}) %all-gather.15.cloned.1.call-update) | async-done | bytes 1081360 | tf_op jit(solution)/shard_map/while/body/eval_jaxpr/all_gather | solution.py:177
  1808.7 44.5 %reduce-scatter.12.cloned.1.call-done = f32[176,768]{1,0:T(8,128)} async-done(((f32[704,768]{1,0:T(8,128)}), f32[176,768]{1,0:T(8,128)}) %reduce-scatter.12.cloned.1.call-update) | async-done | bytes 540688 | tf_op jit(solution)/shard_map/while/body/eval_jaxpr/reduce_scatter | solution.py:185
  1991.4 23.5 %reduce-scatter.14.cloned.1.call-done = f32[176,768]{1,0:T(8,128)} async-done(((f32[704,768]{1,0:T(8,128)}), f32[176,768]{1,0:T(8,128)}) %reduce-scatter.14.cloned.1.call-update) | async-done | bytes 540688 | tf_op jit(solution)/shard_map/while/body/eval_jaxpr/reduce_scatter | solution.py:202
  2029.7 33.8 %all-reduce.34 = (f32[1,768]{1,0:T(1,128)}, f32[1,768]{1,0:T(1,128)}) all-reduce(f32[1,768]{1,0:T(1,128)S(1)} %broadcast_in_dim.232, f32[1,768]{1,0:T(1,128)S(1)} %broadcast_in_dim.237), channel_id=1, replica_groups=mesh['section'=2,'dp'=4,'tensor'=4] {'dp','tensor'}, use_global_device_ids=true, to_apply=%region_40.41 | all-reduce | flops 1536 | bytes 12288 | tf_op jit(solution)/shard_map/psum | solution.py:354
  2075.9 143.5 %all-reduce.39.cloned.1.call-done = (f32[1,768,3,192]{1,3,2,0:T(8,128)}, f32[1,2,705,192]{2,3,1,0:T(8,128)}, f32[1,192,768]{2,1,0:T(8,128)}, f32[1,768,2,768]{3,2,1,0:T(2,128)}, f32[1,768,768]{2,1,0:T(8,128)}) async-done(((f32[1,768,3,192]{1,3,2,0:T(8,128)}, f32[1,2,705,192]{2,3,1,0:T(8,128)}, f32[1,192,768]{2,1,0:T(8,128)}, f32[1,768,2,768]{3,2,1,0:T(2,128)}, f32[1,768,768]{2,1,0:T(8,128)}), ...) | async-done | bytes 10520080 | tf_op jit(solution)/shard_map/psum | solution.py:350
  (1323 shorter events, 1087.5 us)
Async XLA Ops:
  48.4 49.6 %all-gather.7.cloned.1.call-start = ((), (), s32[]{:S(2)}) async-start(), calls=%async_computation.6 | async-start | bytes 1351680 | tf_op jit(solution)/shard_map/while/body/eval_jaxpr/all_gather | solution.py:125
  67.2 134.5 %reduce-scatter.6.cloned.1.call-start = ((), (), s32[]{:S(2)}) async-start(), calls=%async_computation.7 | async-start | bytes 2703360 | tf_op jit(solution)/shard_map/while/body/eval_jaxpr/reduce_scatter | solution.py:127
  157.1 74.9 %all-gather.9.cloned.1.call-start = ((), (), s32[]{:S(2)}) async-start(), calls=%async_computation.8 | async-start | bytes 1351680 | tf_op jit(solution)/shard_map/while/body/eval_jaxpr/all_gather | solution.py:134
  204.0 79.2 %reduce-scatter.8.cloned.1.call-start = ((), (), s32[]{:S(2)}) async-start(), calls=%async_computation.9 | async-start | bytes 2703360 | tf_op jit(solution)/shard_map/while/body/eval_jaxpr/reduce_scatter | solution.py:150
  285.4 46.3 %all-gather.7.cloned.1.call-start = ((), (), s32[]{:S(2)}) async-start(), calls=%async_computation.6 | async-start | bytes 1351680 | tf_op jit(solution)/shard_map/while/body/eval_jaxpr/all_gather | solution.py:125
  302.5 132.9 %reduce-scatter.6.cloned.1.call-start = ((), (), s32[]{:S(2)}) async-start(), calls=%async_computation.7 | async-start | bytes 2703360 | tf_op jit(solution)/shard_map/while/body/eval_jaxpr/reduce_scatter | solution.py:127
  390.7 74.9 %all-gather.9.cloned.1.call-start = ((), (), s32[]{:S(2)}) async-start(), calls=%async_computation.8 | async-start | bytes 1351680 | tf_op jit(solution)/shard_map/while/body/eval_jaxpr/all_gather | solution.py:134
  437.6 79.2 %reduce-scatter.8.cloned.1.call-start = ((), (), s32[]{:S(2)}) async-start(), calls=%async_computation.9 | async-start | bytes 2703360 | tf_op jit(solution)/shard_map/while/body/eval_jaxpr/reduce_scatter | solution.py:150
  519.0 46.3 %all-gather.7.cloned.1.call-start = ((), (), s32[]{:S(2)}) async-start(), calls=%async_computation.6 | async-start | bytes 1351680 | tf_op jit(solution)/shard_map/while/body/eval_jaxpr/all_gather | solution.py:125
  536.1 132.9 %reduce-scatter.6.cloned.1.call-start = ((), (), s32[]{:S(2)}) async-start(), calls=%async_computation.7 | async-start | bytes 2703360 | tf_op jit(solution)/shard_map/while/body/eval_jaxpr/reduce_scatter | solution.py:127
  624.3 74.9 %all-gather.9.cloned.1.call-start = ((), (), s32[]{:S(2)}) async-start(), calls=%async_computation.8 | async-start | bytes 1351680 | tf_op jit(solution)/shard_map/while/body/eval_jaxpr/all_gather | solution.py:134
  671.2 79.2 %reduce-scatter.8.cloned.1.call-start = ((), (), s32[]{:S(2)}) async-start(), calls=%async_computation.9 | async-start | bytes 2703360 | tf_op jit(solution)/shard_map/while/body/eval_jaxpr/reduce_scatter | solution.py:150
  754.2 30.8 %all-gather.11.cloned.1.call-start = ((), (), s32[]{:S(2)}) async-start(), calls=%async_computation.10 | async-start | bytes 1351680 | tf_op jit(solution)/shard_map/while/body/eval_jaxpr/all_gather | solution.py:125
  756.9 136.6 %reduce-scatter.10.cloned.1.call-start = ((), (), s32[]{:S(2)}) async-start(), calls=%async_computation.11 | async-start | bytes 2703360 | tf_op jit(solution)/shard_map/while/body/eval_jaxpr/reduce_scatter | solution.py:127
  849.0 76.2 %all-gather.13.cloned.1.call-start = ((), (), s32[]{:S(2)}) async-start(), calls=%async_computation.12 | async-start | bytes 1351680 | tf_op jit(solution)/shard_map/while/body/eval_jaxpr/all_gather | solution.py:134
  897.2 57.4 %all-gather.15.cloned.1.call-start = ((), (), s32[]{:S(2)}) async-start(), calls=%async_computation.13 | async-start | bytes 1351680 | tf_op jit(solution)/shard_map/while/body/eval_jaxpr/all_gather | solution.py:177
  915.6 93.4 %reduce-scatter.12.cloned.1.call-start = ((), (), s32[]{:S(2)}) async-start(), calls=%async_computation.14 | async-start | bytes 2703360 | tf_op jit(solution)/shard_map/while/body/eval_jaxpr/reduce_scatter | solution.py:185
  964.5 78.6 %all-gather.17.cloned.1.call-start = ((), (), s32[]{:S(2)}) async-start(), calls=%async_computation.15 | async-start | bytes 1351680 | tf_op jit(solution)/shard_map/while/body/eval_jaxpr/all_gather | solution.py:193
  1015.1 155.6 %reduce-scatter.14.cloned.1.call-start = ((), (), s32[]{:S(2)}) async-start(), calls=%async_computation.16 | async-start | bytes 2703360 | tf_op jit(solution)/shard_map/while/body/eval_jaxpr/reduce_scatter | solution.py:202
  1179.0 136.6 %reduce-scatter.10.cloned.1.call-start = ((), (), s32[]{:S(2)}) async-start(), calls=%async_computation.11 | async-start | bytes 2703360 | tf_op jit(solution)/shard_map/while/body/eval_jaxpr/reduce_scatter | solution.py:127
  1271.0 76.3 %all-gather.13.cloned.1.call-start = ((), (), s32[]{:S(2)}) async-start(), calls=%async_computation.12 | async-start | bytes 1351680 | tf_op jit(solution)/shard_map/while/body/eval_jaxpr/all_gather | solution.py:134
  1319.3 57.6 %all-gather.15.cloned.1.call-start = ((), (), s32[]{:S(2)}) async-start(), calls=%async_computation.13 | async-start | bytes 1351680 | tf_op jit(solution)/shard_map/while/body/eval_jaxpr/all_gather | solution.py:177
  1338.7 92.5 %reduce-scatter.12.cloned.1.call-start = ((), (), s32[]{:S(2)}) async-start(), calls=%async_computation.14 | async-start | bytes 2703360 | tf_op jit(solution)/shard_map/while/body/eval_jaxpr/reduce_scatter | solution.py:185
  1386.6 78.6 %all-gather.17.cloned.1.call-start = ((), (), s32[]{:S(2)}) async-start(), calls=%async_computation.15 | async-start | bytes 1351680 | tf_op jit(solution)/shard_map/while/body/eval_jaxpr/all_gather | solution.py:193
  1437.3 155.6 %reduce-scatter.14.cloned.1.call-start = ((), (), s32[]{:S(2)}) async-start(), calls=%async_computation.16 | async-start | bytes 2703360 | tf_op jit(solution)/shard_map/while/body/eval_jaxpr/reduce_scatter | solution.py:202
  1601.2 136.6 %reduce-scatter.10.cloned.1.call-start = ((), (), s32[]{:S(2)}) async-start(), calls=%async_computation.11 | async-start | bytes 2703360 | tf_op jit(solution)/shard_map/while/body/eval_jaxpr/reduce_scatter | solution.py:127
  1693.2 76.2 %all-gather.13.cloned.1.call-start = ((), (), s32[]{:S(2)}) async-start(), calls=%async_computation.12 | async-start | bytes 1351680 | tf_op jit(solution)/shard_map/while/body/eval_jaxpr/all_gather | solution.py:134
  1741.4 57.4 %all-gather.15.cloned.1.call-start = ((), (), s32[]{:S(2)}) async-start(), calls=%async_computation.13 | async-start | bytes 1351680 | tf_op jit(solution)/shard_map/while/body/eval_jaxpr/all_gather | solution.py:177
  1760.9 92.4 %reduce-scatter.12.cloned.1.call-start = ((), (), s32[]{:S(2)}) async-start(), calls=%async_computation.14 | async-start | bytes 2703360 | tf_op jit(solution)/shard_map/while/body/eval_jaxpr/reduce_scatter | solution.py:185
  1808.7 78.6 %all-gather.17.cloned.1.call-start = ((), (), s32[]{:S(2)}) async-start(), calls=%async_computation.15 | async-start | bytes 1351680 | tf_op jit(solution)/shard_map/while/body/eval_jaxpr/all_gather | solution.py:193
  1859.3 155.6 %reduce-scatter.14.cloned.1.call-start = ((), (), s32[]{:S(2)}) async-start(), calls=%async_computation.16 | async-start | bytes 2703360 | tf_op jit(solution)/shard_map/while/body/eval_jaxpr/reduce_scatter | solution.py:202
  2022.2 197.2 %all-reduce.39.cloned.1.call-start = ((), (), s32[]{:S(2)}) async-start(), calls=%async_computation.5 | async-start | bytes 21233664 | tf_op jit(solution)/shard_map/psum | solution.py:350
  (402 other events, 3036.8 us)
Sparse Core Ops, SparseCore 0:
  67.3 30.7 all-gather.6
  157.2 44.4 reduce-scatter.5
  204.1 27.8 all-gather.8
  238.7 44.4 reduce-scatter.7
  302.6 29.0 all-gather.6
  390.9 44.4 reduce-scatter.5
  437.7 27.8 all-gather.8
  472.3 44.4 reduce-scatter.7
  536.2 29.0 all-gather.6
  624.5 44.4 reduce-scatter.5
  671.3 27.8 all-gather.8
  706.0 44.4 reduce-scatter.7
  757.0 27.8 all-gather.10
  849.1 44.4 reduce-scatter.9
  897.3 27.8 all-gather.12
  926.6 27.9 all-gather.14
  964.6 44.4 reduce-scatter.11
  1015.2 27.8 all-gather.16
  1126.2 44.4 reduce-scatter.13
  1271.1 44.4 reduce-scatter.9
  1319.4 27.8 all-gather.12
  1348.8 27.9 all-gather.14
  1386.8 44.4 reduce-scatter.11
  1437.4 27.8 all-gather.16
  1548.4 44.4 reduce-scatter.13
  1601.3 27.8 all-gather.10
  1693.3 44.4 reduce-scatter.9
  1741.6 27.8 all-gather.12
  1770.9 27.9 all-gather.14
  1808.8 44.4 reduce-scatter.11
  1859.4 27.8 all-gather.16
  1970.4 44.4 reduce-scatter.13
  (1 shorter events, 27.8 us)
Sparse Core Ops, SparseCore 1:
  2029.0 190.3 all-reduce.38
where the time goes:
time: 2250 us; the launch traced here: 2240 us
  waiting for transfers between devices  1230 us (55%)
  matrix products  430 us (19%)
  local copies, waits for them, and re-layouts  279 us (12%)
  other arithmetic  208 us (9%)
  blocking collectives  46.2 us (2%)
    reduce_scatter x6, waiting for transfers between devices, run_layer(): lax.psum_scatter(jnp.dot(mixed_low, w_out, preferred_element_type=jnp.flo...  261 us
    all_gather x6, waiting for transfers between devices, run_layer(): lax.all_gather(normed.astype(jnp.bfloat16), 'tensor', axis=0, tiled=True)  166 us
    psum x1, waiting for transfers between devices, per_device(): lax.psum((sum_in, sum_short, sum_cond, sum_spec, sum_gain, sum_out, sum_g...  143 us
    reduce_scatter x3, waiting for transfers between devices, run_layer(): lax.psum_scatter(jnp.dot(act_low, w_down, preferred_element_type=jnp.floa...  134 us
    reduce_scatter x3, waiting for transfers between devices, back_layer(): lax.psum_scatter(jnp.einsum('lf,df->ld', piece, w_gate_up, preferred_elem...  134 us
    dot_general x9, matrix products, orchid_mix(): jnp.dot(inverse_table, joined, precision=highest)  124 us
    dot_general x9, matrix products, orchid_mix(): jnp.dot(forward_table, pieces, precision=highest)  123 us
    all_gather x6, waiting for transfers between devices, run_layer(): lax.all_gather(normed_two.astype(jnp.bfloat16), 'tensor', axis=0, tiled=T...  110 us
  transfers between devices with their start and end apart: 40, of which 40 were waited for; matrix products, arithmetic and copies ran while one was open for 5% of the time, Pallas kernels for 0%

commit v1 on v0

v1 whole, which is shorter than its diff:
```python
from functools import partial
import math

import jax
import jax.numpy as jnp
from jax import lax
from jax.sharding import Mesh
from jax.sharding import PartitionSpec as P

SEGS = 4

high = lax.Precision.HIGH

ALL_AXES = ("section", "dq", "core", "th", "tl")


def permute(values, axes, mapping):
    sizes = [lax.axis_size(a) for a in axes]
    pairs = []
    total = math.prod(sizes)
    for source in range(total):
        place = []
        rest = source
        for size in reversed(sizes):
            place.append(rest % size)
            rest //= size
        place = tuple(reversed(place))
        target = mapping(*place)
        if target is None:
            continue
        flat = 0
        for size, at in zip(sizes, target):
            flat = flat * size + at
        pairs.append((source, flat))
    return lax.ppermute(values, axes if len(axes) > 1 else axes[0], pairs)


def swap_core(values):
    return permute(values, ("core",), lambda c: (1 - c,))


def swap_section(values):
    return permute(values, ("section",), lambda s: (1 - s,))


def shift(values, axis, by):
    size = lax.axis_size(axis)
    return permute(values, (axis,), lambda j: ((j + by) % size,))


def transposed(values):
    return permute(values, ("core", "th"), lambda c, h: (h, c))


def gather_rows(rows):
    peers = lax.axis_size("tl")
    blocks = [rows] + [shift(rows, "tl", k) for k in range(1, peers)]
    others = [swap_core(block) for block in blocks]
    return jnp.concatenate(blocks + others, axis=0)


def scatter_rows(partial_rows):
    peers = lax.axis_size("tl")
    count = partial_rows.shape[0] // (2 * peers)
    blocks = partial_rows.reshape(2, peers, count, partial_rows.shape[1])
    total = None
    for k in list(range(1, peers)) + [0]:
        block = blocks[0, k] + swap_core(blocks[1, k])
        if k:
            block = shift(block, "tl", -k)
        total = block if total is None else total + block
    return total


def reorder(rows, core, low):
    peers = lax.axis_size("tl")
    count = rows.shape[0] // (2 * peers)
    blocks = rows.reshape(2, peers, count, rows.shape[1])
    picked = []
    for c in range(2):
        for t in range(peers):
            picked.append(blocks[jnp.bitwise_xor(core, c), (low - t) % peers])
    return jnp.concatenate(picked, axis=0)


def layer_norm(values, gain):
    row_mean = jnp.mean(values, axis=-1, keepdims=True)
    centred = values - row_mean
    variance = jnp.mean(centred * centred, axis=-1, keepdims=True)
    return centred * lax.rsqrt(variance + 1e-05) * gain


def neighbours(segments):
    equal = (segments[1:] == segments[:-1]).astype(jnp.float32)
    blank = jnp.zeros((1,), jnp.float32)
    return (jnp.concatenate([blank, equal]), jnp.concatenate([equal, blank]))


def masked_short(values, taps, same_prev, same_next):
    blank = jnp.zeros((1, values.shape[1]), values.dtype)
    before = jnp.concatenate([blank, values[:-1]], axis=0) * same_prev[:, None]
    after = jnp.concatenate([values[1:], blank], axis=0) * same_next[:, None]
    return taps[0] * before + taps[1] * values + taps[2] * after


def spectral_tables(pack_len):
    period = 2 * pack_len
    freq_index = lax.broadcasted_iota(jnp.int32, (pack_len + 1, pack_len), 0)
    place_index = lax.broadcasted_iota(jnp.int32, (pack_len + 1, pack_len), 1)
    angle = (freq_index * place_index % period).astype(jnp.float32) * (2.0 * math.pi / period)
    cosine = jnp.cos(angle)
    sine = jnp.sin(angle)
    forward_table = jnp.concatenate([cosine, -sine], axis=0)
    freq_column = freq_index[:, :1]
    column_weight = jnp.where((freq_column == 0) | (freq_column == pack_len), 1.0, 2.0) / period
    inverse_table = jnp.concatenate([cosine * column_weight, -sine * column_weight], axis=0).T
    return (forward_table, inverse_table)


def orchid_mix(proj, short_taps, cond_taps, spectrum, spectral_gain, segments, tables):
    forward_table, inverse_table = tables
    pack_len = proj.shape[0]
    channels = proj.shape[1] // 3
    freqs = pack_len + 1
    same_prev, same_next = neighbours(segments)
    shorted = masked_short(proj, short_taps, same_prev, same_next)
    query = shorted[:, :channels]
    key_part = shorted[:, channels : 2 * channels]
    value_part = shorted[:, 2 * channels :]
    condition = masked_short(key_part, cond_taps, same_prev, same_next)
    cond_hat = jnp.dot(forward_table, condition, precision=high)
    scale_in = spectral_gain[0] / math.sqrt(pack_len)
    filt_re = spectrum[0] + spectral_gain[1] * jnp.tanh(scale_in * cond_hat[:freqs])
    filt_im = spectrum[1] + spectral_gain[1] * jnp.tanh(scale_in * cond_hat[freqs:])
    masks = (segments[:, None] == jnp.arange(SEGS, dtype=jnp.int32)[None, :]).astype(jnp.float32)
    pieces = (masks[:, :, None] * value_part[:, None, :]).reshape(pack_len, SEGS * channels)
    piece_hat = jnp.dot(forward_table, pieces, precision=high).reshape(2, freqs, SEGS, channels)
    real_part = piece_hat[0] * filt_re[:, None, :] - piece_hat[1] * filt_im[:, None, :]
    imag_part = piece_hat[0] * filt_im[:, None, :] + piece_hat[1] * filt_re[:, None, :]
    joined = jnp.concatenate([real_part, imag_part], axis=0).reshape(2 * freqs, SEGS * channels)
    conv = jnp.dot(inverse_table, joined, precision=high).reshape(pack_len, SEGS, channels)
    mixed = jnp.sum(conv * masks[:, :, None], axis=1)
    return query * mixed


def glu_act(both_parts):
    half_width = both_parts.shape[1] // 2
    return jax.nn.silu(both_parts[:, :half_width]) * both_parts[:, half_width:]


def dot32(spec, a, b):
    return jnp.einsum(spec, a, b, preferred_element_type=jnp.float32)


def forward_layer(rows, segments, params, tables, place):
    w_in, short_taps, cond_taps, spectrum, spectral_gain, w_out, gate_up, down, gain1, gain2 = params
    core, low = place
    normed, norm_pull = jax.vjp(layer_norm, rows, gain1)
    gathered = reorder(gather_rows(normed.astype(jnp.bfloat16)), core, low)
    proj = dot32("ld,dc->lc", gathered, w_in)
    mixer = partial(orchid_mix, segments=segments, tables=tables)
    mixed, mix_pull = jax.vjp(mixer, proj, short_taps, cond_taps, spectrum, spectral_gain)
    mixed_low = mixed.astype(jnp.bfloat16)
    hidden = rows + scatter_rows(dot32("lc,cd->ld", reorder(mixed_low, core, low), w_out))
    normed_two, norm_pull_two = jax.vjp(layer_norm, hidden, gain2)
    gathered_two = gather_rows(normed_two.astype(jnp.bfloat16))
    act, act_pull = jax.vjp(glu_act, dot32("ld,df->lf", gathered_two, gate_up))
    act_low = act.astype(jnp.bfloat16)
    result = hidden + scatter_rows(dot32("lf,fd->ld", act_low, down))
    return result, (norm_pull, gathered, mixed_low, mix_pull, norm_pull_two, gathered_two, act_pull, act_low)


def backward_layer(grad_out, params, saved, place):
    w_in, short_taps, cond_taps, spectrum, spectral_gain, w_out, gate_up, down, gain1, gain2 = params
    norm_pull, gathered, mixed_low, mix_pull, norm_pull_two, gathered_two, act_pull, act_low = saved
    core, low = place
    grad_rows = gather_rows(grad_out.astype(jnp.bfloat16))
    grad_act = dot32("ld,fd->lf", grad_rows, down)
    grad_both = act_pull(grad_act)[0].astype(jnp.bfloat16)
    grad_normed_two = scatter_rows(dot32("lf,df->ld", grad_both, gate_up))
    grad_down = dot32("lf,ld->fd", act_low, grad_rows)
    grad_gate_up = dot32("ld,lf->df", gathered_two, grad_both)
    grad_hidden_part, grad_gain2 = norm_pull_two(grad_normed_two)
    grad_hidden = grad_out + grad_hidden_part
    mix_rows = reorder(gather_rows(grad_hidden.astype(jnp.bfloat16)), core, low)
    grad_mixed = dot32("ld,cd->lc", mix_rows, w_out)
    grad_w_out = dot32("lc,ld->cd", mixed_low, mix_rows)
    grad_proj, grad_short, grad_cond, grad_spectrum, grad_spectral = mix_pull(grad_mixed)
    grad_proj_low = grad_proj.astype(jnp.bfloat16)
    grad_normed = scatter_rows(dot32("lc,dc->ld", reorder(grad_proj_low, core, low), w_in))
    grad_w_in = dot32("ld,lc->dc", gathered, grad_proj_low)
    grad_input_part, grad_gain1 = norm_pull(grad_normed)
    large = (grad_w_in, grad_spectrum, grad_w_out, grad_gate_up, grad_down)
    small = (grad_short, grad_cond, grad_spectral)
    return grad_hidden + grad_input_part, large, small, (grad_gain1, grad_gain2)


def parts_of(values):
    unit = 32 * lax.axis_size("dq")
    rows = values.shape[0]
    padded = -(-rows // unit) * unit
    if padded != rows:
        values = jnp.pad(values, ((0, padded - rows), (0, 0)))
    return values.reshape(lax.axis_size("dq"), padded // lax.axis_size("dq"), values.shape[1])


def join_dq(part, dq, mapping_ok=None):
    peers = lax.axis_size("dq")
    got = [part]
    for k in range(1, peers):
        if mapping_ok is None:
            got.append(shift(part, "dq", k))
        else:
            got.append(
                permute(
                    part,
                    ("dq", "core", "th"),
                    lambda d, c, h: ((d + k) % peers, c, h) if mapping_ok(c, h) else None,
                )
            )
    stack = jnp.stack(got)
    return jnp.concatenate([stack[(dq - d) % peers] for d in range(peers)], axis=0)


def fetch(own, place5):
    section, dq, core, high_part, low = place5
    rows = own.shape[0]
    parts = parts_of(own)
    own_part = parts[dq]
    crossed = lambda c, h: c != h
    moved_part = permute(
        own_part, ("core", "th"), lambda c, h: (h, c) if c != h else None
    )
    stays = core == high_part
    part = jnp.where(stays, own_part, moved_part)
    other_part = swap_section(part)
    moved = join_dq(moved_part, dq, crossed)[:rows]
    mine = jnp.where(stays, own, moved)
    other = join_dq(other_part, dq)[:rows]
    first = section == 0
    return jnp.where(first, mine, other), jnp.where(first, other, mine)


def reduce_large(first, second, place5):
    section, dq, core, high_part, low = place5
    low_type = jnp.bfloat16
    rows = first.shape[0]
    peers = lax.axis_size("dq")

    def over_dq(grad):
        parts = parts_of(grad)
        total = parts[dq]
        for k in range(1, peers):
            total = total + shift(parts[(dq + k) % peers].astype(low_type), "dq", k).astype(
                jnp.float32
            )
        return total

    first, second = over_dq(first), over_dq(second)
    is_first = section == 0
    total = jnp.where(is_first, first, second) + swap_section(
        jnp.where(is_first, second, first).astype(low_type)
    ).astype(jnp.float32)
    other = permute(
        total.astype(low_type), ("core", "th"), lambda c, h: (c, 1 - h) if c != h else None
    )
    total = (total + other.astype(jnp.float32)).astype(low_type)
    half = total.shape[0] // 2
    halves = total.reshape(2, half, total.shape[1])
    got = permute(total, ("core", "th"), lambda c, h: (1 - c, h) if c == h else None)
    total = jnp.where(core == high_part, total, got)
    mine = total.reshape(2, half, total.shape[1])[core]
    joined = [mine] + [shift(mine, "dq", k) for k in range(1, peers)]
    stack = jnp.stack(joined)
    across = swap_core(stack)
    both = jnp.stack([stack, across])
    ordered = []
    for d in range(peers):
        for c in range(2):
            ordered.append(both[jnp.bitwise_xor(core, c), (dq - d) % peers])
    return jnp.concatenate(ordered, axis=0)[:rows].astype(jnp.float32)


def reduce_small(values):
    for k in range(1, 2):
        values = values + swap_section(values)
    total = values
    for k in range(1, lax.axis_size("dq")):
        total = total + shift(values, "dq", k)
    total = total + permute(total, ("th",), lambda h: (1 - h,))
    return total


def per_device(
    tokens,
    segment_ids,
    cotangent,
    norm_gain1,
    w_in,
    short_taps,
    cond_taps,
    spectrum,
    spectral_gain,
    w_out,
    norm_gain2,
    w_gate_up,
    w_down,
):
    slots, row_count, width = tokens.shape
    pack_len = segment_ids.shape[1]
    channels = w_in.shape[3]
    hidden_cols = w_gate_up.shape[3]
    place5 = tuple(lax.axis_index(a) for a in ALL_AXES)
    section, dq, core, high_part, low = place5
    place = (core, low)
    packs = slots // 2

    tables = spectral_tables(pack_len)

    def own_slots(array):
        return lax.dynamic_slice_in_dim(array, section * packs, packs, 0)

    rows_in = transposed(own_slots(tokens))
    ids_both = jnp.stack([segment_ids, permute(segment_ids.astype(jnp.float32), ("core",), lambda c: (1 - c,)).astype(jnp.int32)])
    segments = own_slots(ids_both[jnp.bitwise_xor(core, high_part)])

    freqs = spectrum.shape[2]
    flat = {
        "w_in": w_in[0].reshape(width, 3 * channels),
        "spectrum": spectrum[0].reshape(2 * freqs, channels),
        "w_out": w_out[0],
        "gate_up": w_gate_up[0].reshape(width, 2 * hidden_cols),
        "down": w_down[0],
    }
    taps = jnp.concatenate(
        [short_taps[0].reshape(9, channels), cond_taps[0], spectral_gain[0]], axis=0
    )
    taps_t = transposed(taps)
    taps_o = swap_section(taps_t)
    gains = jnp.concatenate([norm_gain1, norm_gain2], axis=0)
    gains_o = swap_section(gains)
    first = section == 0
    taps_l = (jnp.where(first, taps_t, taps_o), jnp.where(first, taps_o, taps_t))
    gains_l = (jnp.where(first, gains, gains_o), jnp.where(first, gains_o, gains))
    fetched = {name: fetch(flat[name], place5) for name in ("w_in", "spectrum", "w_out", "gate_up", "down")}
    cot_in = transposed(own_slots(cotangent))

    def params_of(layer):
        t = taps_l[layer]
        short = t[:9].reshape(3, 3, channels).reshape(3, 3 * channels)
        return (
            fetched["w_in"][layer],
            short,
            t[9:12],
            fetched["spectrum"][layer].reshape(2, freqs, channels),
            t[12:14],
            fetched["w_out"][layer],
            fetched["gate_up"][layer],
            fetched["down"][layer],
            gains_l[layer][0],
            gains_l[layer][1],
        )

    params = (params_of(0), params_of(1))
    results = [[], []]
    saved = [[], []]
    for pack in range(packs):
        state = rows_in[pack].astype(jnp.float32)
        for layer in range(2):
            state, kept = forward_layer(state, segments[pack], params[layer], tables, place)
            results[layer].append(state)
            saved[layer].append(kept)
    grads_in = [[], []]
    large_sum = [None, None]
    small_sum = [None, None]
    gain_sum = [None, None]

    def add(old, new):
        return new if old is None else jax.tree.map(jnp.add, old, new)

    for pack in range(packs):
        state = cot_in[pack].astype(jnp.float32)
        for layer in (1, 0):
            state, large, small, gain = backward_layer(
                state, params[layer], saved[layer][pack], place
            )
            grads_in[layer].append(state)
            large_sum[layer] = add(large_sum[layer], large)
            small_sum[layer] = add(small_sum[layer], small)
            gain_sum[layer] = add(gain_sum[layer], gain)

    def deliver(by_layer):
        zero, one = jnp.stack(by_layer[0]), jnp.stack(by_layer[1])
        keep = transposed(jnp.where(first, zero, one))
        given = permute(
            jnp.where(first, one, zero),
            ("section", "core", "th"),
            lambda s, c, h: (1 - s, h, c),
        )
        lead = jnp.where(first, keep, given)
        trail = jnp.where(first, given, keep)
        return jnp.concatenate([lead, trail], axis=0)

    layer_out = deliver(results)
    grad_in = deliver(grads_in)

    names = ("w_in", "spectrum", "w_out", "gate_up", "down")
    large_first = dict(zip(names, large_sum[0]))
    large_second = dict(zip(names, large_sum[1]))
    for d in (large_first, large_second):
        d["spectrum"] = d["spectrum"].reshape(2 * freqs, channels)
    reduced = {n: reduce_large(large_first[n], large_second[n], place5) for n in names}

    def small_pack(small):
        short, cond, spectral = small
        return jnp.concatenate([short.reshape(9, channels), cond, spectral], axis=0)

    small_both = jnp.stack([small_pack(small_sum[0]), small_pack(small_sum[1])])
    small_both = transposed(reduce_small(small_both))
    small_mine = small_both[section]
    gain_both = jnp.stack([jnp.stack(gain_sum[0]), jnp.stack(gain_sum[1])])
    gain_both = lax.psum(gain_both, ALL_AXES)
    gain_mine = gain_both[section]
    return (
        layer_out[None],
        grad_in[None],
        gain_mine[0][None],
        reduced["w_in"].reshape(1, width, 3, channels),
        small_mine[:9].reshape(1, 3, 3, channels),
        small_mine[9:12][None],
        reduced["spectrum"].reshape(1, 2, freqs, channels),
        small_mine[12:14][None],
        reduced["w_out"][None],
        gain_mine[1][None],
        reduced["gate_up"].reshape(1, width, 2, hidden_cols),
        reduced["down"][None],
    )


def solution(mesh):
    sections, dps, tensors = (mesh.shape[a] for a in ("section", "dp", "tensor"))
    devices = mesh.devices.reshape(sections, dps // 2, 2, 2, tensors // 2)
    fine = Mesh(devices, ALL_AXES)
    dp = ("dq", "core")
    tensor = ("th", "tl")
    return jax.shard_map(
        per_device,
        mesh=fine,
        in_specs=(
            P(dp, tensor, None),
            P(dp, None),
            P(dp, tensor, None),
            P("section", None),
            P("section", None, None, tensor),
            P("section", None, None, tensor),
            P("section", None, tensor),
            P("section", None, None, tensor),
            P("section", None, tensor),
            P("section", tensor, None),
            P("section", None),
            P("section", None, None, tensor),
            P("section", tensor, None),
        ),
        out_specs=(
            P("section", dp, tensor, None),
            P("section", dp, tensor, None),
            P("section", None),
            P("section", None, None, tensor),
            P("section", None, None, tensor),
            P("section", None, tensor),
            P("section", None, None, tensor),
            P("section", None, tensor),
            P("section", tensor, None),
            P("section", None),
            P("section", None, None, tensor),
            P("section", tensor, None),
        ),
        check_vma=False,
    )
```

time: 2250 us -> 1070 us (0.48)
  waiting for transfers between devices: 1230 us -> 206 us
  matrix products: 430 us -> 149 us
  starting transfers between devices: 17 us -> 205 us
  local copies, waits for them, and re-layouts: 279 us -> 253 us
    reduce_scatter x15 -> x0, waiting for transfers between devices: 602 us -> none  [the longest x6 261 us: run_layer(): lax.psum_scatter(jnp.dot(mixed_low, w_out, preferred_element_type=jnp.flo...]
    all_gather x18 -> x0, waiting for transfers between devices: 407 us -> none  [the longest x6 166 us: run_layer(): lax.all_gather(normed.astype(jnp.bfloat16), 'tensor', axis=0, tiled=True)]
    dot_general x72 -> x36, matrix products: 430 us -> 149 us  [the longest x24 50.6 us: dot32(): return jnp.einsum(spec, a, b, preferred_element_type=jnp.float32)]
    ppermute x6 -> x117, starting transfers between devices: 15.6 us -> 205 us  [permute(): return lax.ppermute(values, axes if len(axes) > 1 else axes[0], pairs)]
    psum x1 -> x0, waiting for transfers between devices: 143 us -> none  [per_device(): lax.psum((sum_in, sum_short, sum_cond, sum_spec, sum_gain, sum_out, sum_g...]
    ppermute x6 -> x117, waiting for transfers between devices: 73.7 us -> 206 us  [permute(): return lax.ppermute(values, axes if len(axes) > 1 else axes[0], pairs)]
    while x750 -> x0, local copies, waits for them, and re-layouts: 61.9 us -> none
    convert_element_type x21 -> x32, other arithmetic: 18.2 us -> 50.9 us  [the longest x4 15.9 us: reduce_large(): return jnp.concatenate(ordered, axis=0)[:rows].astype(jnp.float32)]
  transfers between devices with their start and end apart: 40 -> 117, of which waited for: 40 -> 30; matrix products, arithmetic and copies ran while one was open for 5% -> 45% of each run, Pallas kernels for 0% -> 0%
where the time goes in v1:
time: 1070 us; the launch traced here: 1060 us
  local copies, waits for them, and re-layouts  253 us (24%)
  waiting for transfers between devices  206 us (19%)
  starting transfers between devices  205 us (19%)
  other arithmetic  201 us (19%)
  matrix products  149 us (14%)
  blocking collectives  37 us (3%)
    ppermute x117, waiting for transfers between devices, permute(): return lax.ppermute(values, axes if len(axes) > 1 else axes[0], pairs)  206 us
    ppermute x117, starting transfers between devices, permute(): return lax.ppermute(values, axes if len(axes) > 1 else axes[0], pairs)  205 us
    dot_general x24, matrix products, dot32(): return jnp.einsum(spec, a, b, preferred_element_type=jnp.float32)  50.6 us
    dot_general x4, matrix products, orchid_mix(): jnp.dot(forward_table, pieces, precision=high)  45.1 us
    unnamed x612, local copies, waits for them, and re-layouts  44.9 us
    dot_general x4, matrix products, orchid_mix(): jnp.dot(inverse_table, joined, precision=high)  44.1 us
    psum x1, blocking collectives, per_device(): gain_both = lax.psum(gain_both, ALL_AXES)  37 us
  transfers between devices with their start and end apart: 117, of which 30 were waited for; matrix products, arithmetic and copies ran while one was open for 45% of the time, Pallas kernels for 0%

profile of v1, /device:TPU:0, one launch (start us, length us, event | category | flops | bytes accessed | tf_op | source)
XLA Modules:
  0.0 1056.9 jit_solution(16371263430732235881)
XLA Ops:
  26.5 8.2 sine_negate_fusion
  34.7 9.2 fusion.28
  44.0 10.1 broadcast_multiply_fusion.11
  88.7 12.2 %collective-permute-start.5 = (bf16[176,768]{1,0:T(8,128)(2,1)S(1)}, bf16[176,768]{1,0:T(8,128)(2,1)S(1)}, u32[]{:S(2)}, u32[]{:S(2)}) collective-permute-start(bf16[176,768]{1,0:T(8,128)(2,1)S(1)} %fusion.125), channel_id=1, source_target_pairs={{0,4},{4,0},{1,5},{5,1},{2,6},{6,2},{3,7},{7,3},{8,12},{12,8},{9,1... | collective-permute-start | bytes 811016 | tf_op jit(solution)/shard_map/ppermute | solution.py:35
  134.7 14.3 %fusion.279 = f32[1410,768]{1,0:T(8,128)} fusion(f32[704,768]{0,1:T(8,128)S(1)} %bitcast.790, f32[705,704]{0,1:T(8,128)S(1)} %sine_negate_fusion, f32[705,704]{0,1:T(8,128)S(1)} %copy-done.2), kind=kOutput, calls=%fused_computation.736 | convolution fusion | flops 4575077888 | bytes 10464768 | tf_op jit(solution)/shard_map/jvp()/dot_general | solution.py:137
  176.0 9.4 multiply_reduce_fusion.11
  190.1 22.7 %collective-permute-start.20 = (f32[176,768]{1,0:T(8,128)S(1)}, f32[176,768]{1,0:T(8,128)S(1)}, u32[]{:S(2)}, u32[]{:S(2)}) collective-permute-start(f32[176,768]{1,0:T(8,128)S(1)} %get-tuple-element.187), channel_id=1, source_target_pairs={{0,4},{4,0},{1,5},{5,1},{2,6},{6,2},{3,7},{7,3},{8,12},{12,8},{9,1... | collective-permute-start | bytes 1622024 | tf_op jit(solution)/shard_map/ppermute | solution.py:35
  230.0 10.5 collective-permute-done.28
  248.1 9.1 collective-permute-start.24
  257.2 12.2 %collective-permute-done.29 = bf16[384,1536]{1,0:T(8,128)(2,1)S(1)} collective-permute-done((bf16[384,1536]{1,0:T(8,128)(2,1)S(1)}, bf16[384,1536]{1,0:T(8,128)(2,1)S(1)}, u32[]{:S(2)}, u32[]{:S(2)}) %collective-permute-start.29) | collective-permute-done | bytes 1179680 | tf_op jit(solution)/shard_map/ppermute | solution.py:35
  284.9 12.8 %collective-permute-done.35 = f32[176,768]{1,0:T(8,128)S(1)} collective-permute-done((f32[176,768]{1,0:T(8,128)S(1)}, f32[176,768]{1,0:T(8,128)S(1)}, u32[]{:S(2)}, u32[]{:S(2)}) %collective-permute-start.35) | collective-permute-done | bytes 540704 | tf_op jit(solution)/shard_map/ppermute | solution.py:35
  300.7 6.4 collective-permute-done.37
  333.4 12.3 %fusion.278 = f32[1410,768]{1,0:T(8,128)S(1)} fusion(f32[704,768]{0,1:T(8,128)S(1)} %bitcast.792, f32[705,704]{0,1:T(8,128)S(1)} %sine_negate_fusion, f32[705,704]{0,1:T(8,128)S(1)} %copy-done.4), kind=kOutput, calls=%fused_computation.735 | convolution fusion | flops 4575077888 | bytes 10464768 | tf_op jit(solution)/shard_map/jvp()/dot_general | solution.py:137
  357.2 9.5 multiply_reduce_fusion.10
  384.5 15.3 %collective-permute-done.52 = bf16[176,768]{1,0:T(8,128)(2,1)} collective-permute-done((bf16[176,768]{1,0:T(8,128)(2,1)}, bf16[176,768]{1,0:T(8,128)(2,1)}, u32[]{:S(2)}, u32[]{:S(2)}) %collective-permute-start.52) | collective-permute-done | bytes 270368 | tf_op jit(solution)/shard_map/ppermute | solution.py:35
  420.5 6.8 collective-permute-done.43
  427.4 10.0 broadcast_select_fusion.1
  508.8 12.7 %fusion.30 = f32[1410,768]{1,0:T(8,128)S(1)} fusion(f32[704,768]{0,1:T(8,128)S(1)} %bitcast.793, f32[705,704]{0,1:T(8,128)S(1)} %copy-done.110, f32[705,704]{0,1:T(8,128)S(1)} %copy-done.108), kind=kOutput, calls=%fused_computation.94 | convolution fusion | flops 4575077888 | bytes 10464768 | tf_op jit(solution)/shard_map/transpose(jvp())/dot_general | solution.py:141
  539.8 7.2 reshape.1001
  547.0 9.1 multiply_reduce_fusion.9
  659.9 11.1 %collective-permute-done.110 = bf16[384,768]{1,0:T(8,128)(2,1)S(1)} collective-permute-done((bf16[384,768]{1,0:T(8,128)(2,1)S(1)}, bf16[384,768]{1,0:T(8,128)(2,1)S(1)}, u32[]{:S(2)}, u32[]{:S(2)}) %collective-permute-start.110) | collective-permute-done | bytes 589856 | tf_op jit(solution)/shard_map/ppermute | solution.py:35
  678.1 34.0 %collective-permute-done.103 = bf16[384,1536]{1,0:T(8,128)(2,1)S(1)} collective-permute-done((bf16[384,1536]{1,0:T(8,128)(2,1)S(1)}, bf16[384,1536]{1,0:T(8,128)(2,1)S(1)}, u32[]{:S(2)}, u32[]{:S(2)}) %collective-permute-start.103) | collective-permute-done | bytes 1179680 | tf_op jit(solution)/shard_map/ppermute | solution.py:35
  729.7 12.5 %fusion.31 = f32[1410,768]{1,0:T(8,128)S(1)} fusion(f32[704,768]{0,1:T(8,128)S(1)} %bitcast.791, f32[705,704]{0,1:T(8,128)S(1)} %copy-done.111, f32[705,704]{0,1:T(8,128)S(1)} %copy-done.109), kind=kOutput, calls=%fused_computation.95 | convolution fusion | flops 4575077888 | bytes 10464768 | tf_op jit(solution)/shard_map/transpose(jvp())/dot_general | solution.py:141
  770.6 7.2 reshape.1004
  777.9 9.4 multiply_reduce_fusion.4
  859.9 10.5 collective-permute-done.98
  878.6 6.9 collective-permute-done.99
  921.6 7.7 collective-permute-start.116
  940.3 14.6 %collective-permute-done.106 = bf16[384,1536]{1,0:T(8,128)(2,1)} collective-permute-done((bf16[384,1536]{1,0:T(8,128)(2,1)}, bf16[384,1536]{1,0:T(8,128)(2,1)}, u32[]{:S(2)}, u32[]{:S(2)}) %collective-permute-start.106) | collective-permute-done | bytes 1179680 | tf_op jit(solution)/shard_map/ppermute | solution.py:35
  960.5 37.0 %psum.7 = f32[2,2,768]{2,1,0:T(2,128)S(1)} all-reduce(f32[2,2,768]{2,1,0:T(2,128)S(1)} %pad_maximum_fusion.66), channel_id=1, replica_groups=mesh['section'=2,'dq'=2,'core'=2,'th'=2,'tl'=2] {'section','dq','core','..., use_global_device_ids=true, to_apply=%region_32.33 | all-reduce | flops 3072 | bytes 24576 | tf_op jit(solution)/shard_map/psum | solution.py:422
  1016.5 13.0 %collective-permute-done.108 = bf16[192,1536]{1,0:T(8,128)(2,1)S(1)} collective-permute-done((bf16[192,1536]{1,0:T(8,128)(2,1)}, bf16[192,1536]{1,0:T(8,128)(2,1)S(1)}, u32[]{:S(2)}, u32[]{:S(2)}) %collective-permute-start.108) | collective-permute-done | bytes 589856 | tf_op jit(solution)/shard_map/ppermute | solution.py:35
  1044.8 11.9 %maximum_convert_fusion = f32[1,768,2,768]{3,2,1,0:T(2,128)} fusion(bf16[1,192,2,768]{3,2,1,0:T(2,128)(2,1)S(1)} %concatenate.341, bf16[1,192,2,768]{3,2,1,0:T(2,128)(2,1)S(1)} %concatenate.340, bf16[1,192,2,768]{3,2,1,0:T(2,128)(2,1)S(1)} %concatenate.339, bf16[1,192,2,768]{3,2,1,0:T(2,128)(2,1)S(1)} %concatenate.338), kind=kLoop, calls=%fused_computation.40 | loop fusion | flops 4718592 | bytes 7077888 | tf_op jit(solution)/shard_map/convert_element_type | solution.py:281
  (1181 shorter events, 655.3 us)
Async XLA Ops:
  1.4 63.1 %collective-permute-start.11 = (f32[2,704]{1,0:T(2,128)S(1)}, f32[2,704]{1,0:T(2,128)S(1)}, u32[]{:S(2)}, u32[]{:S(2)}) collective-permute-start(f32[2,704]{1,0:T(2,128)S(1)} %convert_element_type.298), channel_id=1, source_target_pairs={{0,4},{4,0},{1,5},{5,1},{2,6},{6,2},{3,7},{7,3},{8,12},{12,8},{9,1... | collective-permute-start | bytes 16904 | tf_op jit(solution)/shard_map/ppermute | solution.py:35
  12.2 90.4 %collective-permute-start.12 = (f32[736,192]{0,1:T(8,128)}, f32[736,192]{0,1:T(8,128)}, u32[]{:S(2)}, u32[]{:S(2)}) collective-permute-start(f32[736,192]{0,1:T(8,128)} %bitcast.718), channel_id=1, source_target_pairs={{2,4},{4,2},{3,5},{5,3},{10,12},{12,10},{11,13},{13,11},{18,20},{2... | collective-permute-start | bytes 1695752 | tf_op jit(solution)/shard_map/ppermute | solution.py:35
  17.9 70.8 %collective-permute-start.7 = (bf16[384,576]{0,1:T(8,128)(2,1)}, bf16[384,576]{0,1:T(8,128)(2,1)}, u32[]{:S(2)}, u32[]{:S(2)}) collective-permute-start(bf16[384,576]{0,1:T(8,128)(2,1)} %bitcast.721), channel_id=1, source_target_pairs={{2,4},{4,2},{3,5},{5,3},{10,12},{12,10},{11,13},{13,11},{18,20},{2... | collective-permute-start | bytes 1327112 | tf_op jit(solution)/shard_map/ppermute | solution.py:35
  20.0 55.9 %collective-permute-start = (bf16[1,176,768]{2,1,0:T(8,128)(2,1)}, bf16[1,176,768]{2,1,0:T(8,128)(2,1)}, u32[]{:S(2)}, u32[]{:S(2)}) collective-permute-start(bf16[1,176,768]{2,1,0:T(8,128)(2,1)} %constant_dynamic-slice_fusion.22), channel_id=1, source_target_pairs={{0,0},{2,4},{4,2},{6,6},{1,1},{3,5},{5,3},{7,7},{8,8},{10,12},{12,... | collective-permute-start | bytes 811016 | tf_op jit(solution)/shard_map/ppermute | solution.py:35
  23.9 42.1 %collective-permute-start.3 = (f32[2,768]{1,0:T(2,128)S(1)}, f32[2,768]{1,0:T(2,128)S(1)}, u32[]{:S(2)}, u32[]{:S(2)}) collective-permute-start(f32[2,768]{1,0:T(2,128)S(1)} %pad_maximum_fusion.67), channel_id=1, source_target_pairs={{0,16},{16,0},{1,17},{17,1},{2,18},{18,2},{3,19},{19,3},{4,20},{20... | collective-permute-start | bytes 18440 | tf_op jit(solution)/shard_map/ppermute | solution.py:35
  71.0 141.8 %collective-permute-start.26 = (bf16[384,1536]{1,0:T(8,128)(2,1)}, bf16[384,1536]{1,0:T(8,128)(2,1)}, u32[]{:S(2)}, u32[]{:S(2)}) collective-permute-start(bf16[384,1536]{1,0:T(8,128)(2,1)} %dynamic-slice_bitcast_fusion), channel_id=1, source_target_pairs={{2,4},{4,2},{3,5},{5,3},{10,12},{12,10},{11,13},{13,11},{18,20},{2... | collective-permute-start | bytes 3538952 | tf_op jit(solution)/shard_map/ppermute | solution.py:35
  113.5 100.5 %collective-permute-start.32 = (bf16[384,768]{1,0:T(8,128)(2,1)}, bf16[384,768]{1,0:T(8,128)(2,1)}, u32[]{:S(2)}, u32[]{:S(2)}) collective-permute-start(bf16[384,768]{1,0:T(8,128)(2,1)} %broadcast_select_fusion.8), channel_id=1, source_target_pairs={{0,16},{16,0},{1,17},{17,1},{2,18},{18,2},{3,19},{19,3},{4,20},{20... | collective-permute-start | bytes 1769480 | tf_op jit(solution)/shard_map/ppermute | solution.py:35
  374.1 40.4 %collective-permute-start.42 = (f32[176,768]{1,0:T(8,128)}, f32[176,768]{1,0:T(8,128)S(1)}, u32[]{:S(2)}, u32[]{:S(2)}) collective-permute-start(f32[176,768]{1,0:T(8,128)} %get-tuple-element.182), channel_id=1, source_target_pairs={{0,4},{4,0},{1,5},{5,1},{2,6},{6,2},{3,7},{7,3},{8,12},{12,8},{9,1... | collective-permute-start | bytes 1622024 | tf_op jit(solution)/shard_map/ppermute | solution.py:35
  377.7 37.6 %collective-permute-start.41 = (f32[176,768]{1,0:T(8,128)}, f32[176,768]{1,0:T(8,128)}, u32[]{:S(2)}, u32[]{:S(2)}) collective-permute-start(f32[176,768]{1,0:T(8,128)} %fusion.148), channel_id=1, source_target_pairs={{0,1},{1,0},{2,3},{3,2},{4,5},{5,4},{6,7},{7,6},{8,9},{9,8},{10,11... | collective-permute-start | bytes 1622024 | tf_op jit(solution)/shard_map/ppermute | solution.py:35
  379.7 68.8 %collective-permute-start.53 = (bf16[176,768]{1,0:T(8,128)(2,1)}, bf16[176,768]{1,0:T(8,128)(2,1)}, u32[]{:S(2)}, u32[]{:S(2)}) collective-permute-start(bf16[176,768]{1,0:T(8,128)(2,1)} %bitcast.118), channel_id=1, source_target_pairs={{0,4},{4,0},{1,5},{5,1},{2,6},{6,2},{3,7},{7,3},{8,12},{12,8},{9,1... | collective-permute-start | bytes 811016 | tf_op jit(solution)/shard_map/ppermute | solution.py:35
  399.9 48.7 %collective-permute-start.54 = (bf16[176,768]{1,0:T(8,128)(2,1)}, bf16[176,768]{1,0:T(8,128)(2,1)}, u32[]{:S(2)}, u32[]{:S(2)}) collective-permute-start(bf16[176,768]{1,0:T(8,128)(2,1)} %collective-permute-done.52), channel_id=1, source_target_pairs={{0,4},{4,0},{1,5},{5,1},{2,6},{6,2},{3,7},{7,3},{8,12},{12,8},{9,1... | collective-permute-start | bytes 811016 | tf_op jit(solution)/shard_map/ppermute | solution.py:35
  493.3 87.4 %collective-permute-start.46 = (f32[176,768]{1,0:T(8,128)}, f32[176,768]{1,0:T(8,128)}, u32[]{:S(2)}, u32[]{:S(2)}) collective-permute-start(f32[176,768]{1,0:T(8,128)} %get-tuple-element.181), channel_id=1, source_target_pairs={{0,4},{4,0},{1,5},{5,1},{2,6},{6,2},{3,7},{7,3},{8,12},{12,8},{9,1... | collective-permute-start | bytes 1622024 | tf_op jit(solution)/shard_map/ppermute | solution.py:35
  493.3 118.6 %collective-permute-start.48 = (f32[176,768]{1,0:T(8,128)}, f32[176,768]{1,0:T(8,128)}, u32[]{:S(2)}, u32[]{:S(2)}) collective-permute-start(f32[176,768]{1,0:T(8,128)} %get-tuple-element.180), channel_id=1, source_target_pairs={{0,4},{4,0},{1,5},{5,1},{2,6},{6,2},{3,7},{7,3},{8,12},{12,8},{9,1... | collective-permute-start | bytes 1622024 | tf_op jit(solution)/shard_map/ppermute | solution.py:35
  503.9 172.7 %collective-permute-start.104 = (bf16[384,1536]{1,0:T(8,128)(2,1)}, bf16[384,1536]{1,0:T(8,128)(2,1)}, u32[]{:S(2)}, u32[]{:S(2)}) collective-permute-start(bf16[384,1536]{1,0:T(8,128)(2,1)} %fusion.41), channel_id=1, source_target_pairs={{0,8},{8,0},{1,9},{9,1},{2,10},{10,2},{3,11},{11,3},{4,12},{12,4},... | collective-permute-start | bytes 3538952 | tf_op jit(solution)/shard_map/ppermute | solution.py:35
  606.8 52.5 %collective-permute-start.111 = (bf16[384,768]{1,0:T(8,128)(2,1)}, bf16[384,768]{1,0:T(8,128)(2,1)}, u32[]{:S(2)}, u32[]{:S(2)}) collective-permute-start(bf16[384,768]{1,0:T(8,128)(2,1)} %fusion.90), channel_id=1, source_target_pairs={{0,8},{8,0},{1,9},{9,1},{2,10},{10,2},{3,11},{11,3},{4,12},{12,4},... | collective-permute-start | bytes 1769480 | tf_op jit(solution)/shard_map/ppermute | solution.py:35
  659.3 214.7 %collective-permute-start.79 = (bf16[384,576]{0,1:T(8,128)(2,1)}, bf16[384,576]{0,1:T(8,128)(2,1)}, u32[]{:S(2)}, u32[]{:S(2)}) collective-permute-start(bf16[384,576]{0,1:T(8,128)(2,1)} %bitcast.720), channel_id=1, source_target_pairs={{0,8},{8,0},{1,9},{9,1},{2,10},{10,2},{3,11},{11,3},{4,12},{12,4},... | collective-permute-start | bytes 1327112 | tf_op jit(solution)/shard_map/ppermute | solution.py:35
  671.0 179.4 %collective-permute-start.90 = (bf16[736,192]{0,1:T(8,128)(2,1)}, bf16[736,192]{0,1:T(8,128)(2,1)}, u32[]{:S(2)}, u32[]{:S(2)}) collective-permute-start(bf16[736,192]{0,1:T(8,128)(2,1)} %bitcast.722), channel_id=1, source_target_pairs={{0,8},{8,0},{1,9},{9,1},{2,10},{10,2},{3,11},{11,3},{4,12},{12,4},... | collective-permute-start | bytes 847880 | tf_op jit(solution)/shard_map/ppermute | solution.py:35
  673.9 38.2 %collective-permute-start.103 = (bf16[384,1536]{1,0:T(8,128)(2,1)S(1)}, bf16[384,1536]{1,0:T(8,128)(2,1)S(1)}, u32[]{:S(2)}, u32[]{:S(2)}) collective-permute-start(bf16[384,1536]{1,0:T(8,128)(2,1)S(1)} %fusion.40), channel_id=1, source_target_pairs={{0,8},{8,0},{1,9},{9,1},{2,10},{10,2},{3,11},{11,3},{4,12},{12,4},... | collective-permute-start | bytes 3538952 | tf_op jit(solution)/shard_map/ppermute | solution.py:35
  674.4 41.6 %collective-permute-start.112 = (bf16[384,768]{1,0:T(8,128)(2,1)S(1)}, bf16[384,768]{1,0:T(8,128)(2,1)S(1)}, u32[]{:S(2)}, u32[]{:S(2)}) collective-permute-start(bf16[384,768]{1,0:T(8,128)(2,1)S(1)} %select_convert_fusion.1), channel_id=1, source_target_pairs={{0,16},{16,0},{1,17},{17,1},{2,18},{18,2},{3,19},{19,3},{4,20},{20... | collective-permute-start | bytes 1769480 | tf_op jit(solution)/shard_map/ppermute | solution.py:35
  676.6 164.3 %collective-permute-start.97 = (bf16[96,768]{1,0:T(8,128)(2,1)}, bf16[96,768]{1,0:T(8,128)(2,1)}, u32[]{:S(2)}, u32[]{:S(2)}) collective-permute-start(bf16[96,768]{1,0:T(8,128)(2,1)} %fusion.211), channel_id=1, source_target_pairs={{0,8},{8,0},{1,9},{9,1},{2,10},{10,2},{3,11},{11,3},{4,12},{12,4},... | collective-permute-start | bytes 442376 | tf_op jit(solution)/shard_map/ppermute | solution.py:35
  723.4 123.8 %collective-permute-start.113 = (bf16[384,768]{1,0:T(8,128)(2,1)}, bf16[384,768]{1,0:T(8,128)(2,1)}, u32[]{:S(2)}, u32[]{:S(2)}) collective-permute-start(bf16[384,768]{1,0:T(8,128)(2,1)} %get-tuple-element.91), channel_id=1, source_target_pairs={{2,0},{4,6},{3,1},{5,7},{10,8},{12,14},{11,9},{13,15},{18,16},{20,... | collective-permute-start | bytes 1769480 | tf_op jit(solution)/shard_map/ppermute | solution.py:35
  841.0 60.5 %collective-permute-start.105 = (bf16[384,1536]{1,0:T(8,128)(2,1)}, bf16[384,1536]{1,0:T(8,128)(2,1)S(1)}, u32[]{:S(2)}, u32[]{:S(2)}) collective-permute-start(bf16[384,1536]{1,0:T(8,128)(2,1)} %select_convert_fusion), channel_id=1, source_target_pairs={{0,16},{16,0},{1,17},{17,1},{2,18},{18,2},{3,19},{19,3},{4,20},{20... | collective-permute-start | bytes 3538952 | tf_op jit(solution)/shard_map/ppermute | solution.py:35
  842.9 43.8 %collective-permute-start.73 = (f32[176,768]{1,0:T(8,128)}, f32[176,768]{1,0:T(8,128)S(1)}, u32[]{:S(2)}, u32[]{:S(2)}) collective-permute-start(f32[176,768]{1,0:T(8,128)} %get-tuple-element.173), channel_id=1, source_target_pairs={{0,4},{4,0},{1,5},{5,1},{2,6},{6,2},{3,7},{7,3},{8,12},{12,8},{9,1... | collective-permute-start | bytes 1622024 | tf_op jit(solution)/shard_map/ppermute | solution.py:35
  870.4 51.2 %collective-permute-start.75 = (f32[176,768]{1,0:T(8,128)S(1)}, f32[176,768]{1,0:T(8,128)S(1)}, u32[]{:S(2)}, u32[]{:S(2)}) collective-permute-start(f32[176,768]{1,0:T(8,128)S(1)} %copy-done.170), channel_id=1, source_target_pairs={{0,4},{4,0},{1,5},{5,1},{2,6},{6,2},{3,7},{7,3},{8,12},{12,8},{9,1... | collective-permute-start | bytes 1622024 | tf_op jit(solution)/shard_map/ppermute | solution.py:35
  874.0 32.9 %collective-permute-start.114 = (bf16[384,768]{1,0:T(8,128)(2,1)S(1)}, bf16[384,768]{1,0:T(8,128)(2,1)S(1)}, u32[]{:S(2)}, u32[]{:S(2)}) collective-permute-start(bf16[384,768]{1,0:T(8,128)(2,1)S(1)} %add_convert_fusion.5), channel_id=1, source_target_pairs={{0,4},{6,2},{1,5},{7,3},{8,12},{14,10},{9,13},{15,11},{16,20},{22,... | collective-permute-start | bytes 1769480 | tf_op jit(solution)/shard_map/ppermute | solution.py:35
  909.2 45.6 %collective-permute-start.106 = (bf16[384,1536]{1,0:T(8,128)(2,1)}, bf16[384,1536]{1,0:T(8,128)(2,1)}, u32[]{:S(2)}, u32[]{:S(2)}) collective-permute-start(bf16[384,1536]{1,0:T(8,128)(2,1)} %get-tuple-element.93), channel_id=1, source_target_pairs={{2,0},{4,6},{3,1},{5,7},{10,8},{12,14},{11,9},{13,15},{18,16},{20,... | collective-permute-start | bytes 3538952 | tf_op jit(solution)/shard_map/ppermute | solution.py:35
  919.2 79.1 %collective-permute-start.81 = (bf16[384,576]{0,1:T(8,128)(2,1)S(1)}, bf16[384,576]{0,1:T(8,128)(2,1)}, u32[]{:S(2)}, u32[]{:S(2)}) collective-permute-start(bf16[384,576]{0,1:T(8,128)(2,1)S(1)} %get-tuple-element.103), channel_id=1, source_target_pairs={{2,0},{4,6},{3,1},{5,7},{10,8},{12,14},{11,9},{13,15},{18,16},{20,... | collective-permute-start | bytes 1327112 | tf_op jit(solution)/shard_map/ppermute | solution.py:35
  921.6 112.1 %collective-permute-start.116 = (bf16[2,192,768]{2,1,0:T(8,128)(2,1)}, bf16[2,192,768]{2,1,0:T(8,128)(2,1)}, u32[]{:S(2)}, u32[]{:S(2)}) collective-permute-start(bf16[2,192,768]{2,1,0:T(8,128)(2,1)} %get-tuple-element.262), channel_id=1, source_target_pairs={{0,4},{4,0},{1,5},{5,1},{2,6},{6,2},{3,7},{7,3},{8,12},{12,8},{9,1... | collective-permute-start | bytes 1769480 | tf_op jit(solution)/shard_map/ppermute | solution.py:35
  933.3 97.3 %collective-permute-start.76 = (f32[1,176,768]{2,1,0:T(8,128)}, f32[1,176,768]{2,1,0:T(8,128)}, u32[]{:S(2)}, u32[]{:S(2)}) collective-permute-start(f32[1,176,768]{2,1,0:T(8,128)} %get-tuple-element.202), channel_id=1, source_target_pairs={{0,0},{2,4},{4,2},{6,6},{1,1},{3,5},{5,3},{7,7},{8,8},{10,12},{12,... | collective-permute-start | bytes 1622024 | tf_op jit(solution)/shard_map/ppermute | solution.py:35
  939.8 57.7 %collective-permute-start.94 = (bf16[368,192]{0,1:T(8,128)(2,1)S(1)}, bf16[368,192]{0,1:T(8,128)(2,1)S(1)}, u32[]{:S(2)}, u32[]{:S(2)}) collective-permute-start(bf16[368,192]{0,1:T(8,128)(2,1)S(1)} %bitcast.870), channel_id=1, source_target_pairs={{0,8},{8,0},{1,9},{9,1},{2,10},{10,2},{3,11},{11,3},{4,12},{12,4},... | collective-permute-start | bytes 423944 | tf_op jit(solution)/shard_map/ppermute | solution.py:35
  958.2 52.5 %collective-permute-start.107 = (bf16[384,1536]{1,0:T(8,128)(2,1)}, bf16[384,1536]{1,0:T(8,128)(2,1)}, u32[]{:S(2)}, u32[]{:S(2)}) collective-permute-start(bf16[384,1536]{1,0:T(8,128)(2,1)} %add_convert_fusion.2), channel_id=1, source_target_pairs={{0,4},{6,2},{1,5},{7,3},{8,12},{14,10},{9,13},{15,11},{16,20},{22,... | collective-permute-start | bytes 3538952 | tf_op jit(solution)/shard_map/ppermute | solution.py:35
  998.3 32.3 %collective-permute-start.77 = (f32[1,176,768]{2,1,0:T(8,128)}, f32[1,176,768]{2,1,0:T(8,128)}, u32[]{:S(2)}, u32[]{:S(2)}) collective-permute-start(f32[1,176,768]{2,1,0:T(8,128)} %get-tuple-element.203), channel_id=1, source_target_pairs={{0,16},{2,20},{4,18},{6,22},{16,0},{18,4},{20,2},{22,6},{1,17},{3,... | collective-permute-start | bytes 1622024 | tf_op jit(solution)/shard_map/ppermute | solution.py:35
  (385 other events, 4243.1 us)

commit v2 on v1

v2 whole, which is shorter than its diff:
```python
from functools import partial
import math

import jax
import jax.numpy as jnp
import numpy as np
from jax import lax
from jax.experimental import pallas as pl
from jax.experimental.pallas import tpu as pltpu
from jax.sharding import Mesh
from jax.sharding import PartitionSpec as P

SEGS = 4

FTILE = 256
HTILE = 384
PEAK = 1.0e9
VMEM_LIMIT = 56 * 1024 * 1024

ALL_AXES = ("section", "dq", "core", "th", "tl")


def permute(values, axes, mapping):
    sizes = [lax.axis_size(a) for a in axes]
    pairs = []
    total = math.prod(sizes)
    for source in range(total):
        place = []
        rest = source
        for size in reversed(sizes):
            place.append(rest % size)
            rest //= size
        place = tuple(reversed(place))
        target = mapping(*place)
        if target is None:
            continue
        flat = 0
        for size, at in zip(sizes, target):
            flat = flat * size + at
        pairs.append((source, flat))
    return lax.ppermute(values, axes if len(axes) > 1 else axes[0], pairs)


def swap_core(values):
    return permute(values, ("core",), lambda c: (1 - c,))


def swap_section(values):
    return permute(values, ("section",), lambda s: (1 - s,))


def shift(values, axis, by):
    size = lax.axis_size(axis)
    return permute(values, (axis,), lambda j: ((j + by) % size,))


def transposed(values):
    return permute(values, ("core", "th"), lambda c, h: (h, c))


def chip_blocks(rows):
    return [rows] + [shift(rows, "tl", k) for k in range(1, lax.axis_size("tl"))]


def both_cores(blocks):
    return blocks + [swap_core(block) for block in blocks]


def gather_rows(rows):
    return both_cores(chip_blocks(rows))


def core_sums(blocks):
    peers = lax.axis_size("tl")
    order = list(range(1, peers)) + [0]
    sums = {k: blocks[k] + swap_core(blocks[peers + k]) for k in order}
    return [sums[k] for k in range(peers)]


def sent_sums(sums):
    return [shift(sums[k], "tl", -k) for k in range(1, len(sums))]


def add_sums(sums, moved):
    total = sums[0]
    for term in moved:
        total = total + term.astype(jnp.float32)
    return total


def chip_sums(sums):
    return add_sums(sums, sent_sums(sums))


def after(values, *events):
    return lax.optimization_barrier((values, events))[0]


class Line:
    def __init__(self):
        self.events = ()

    def take(self, values):
        return after(values, self.events)

    def mark(self, *events):
        self.events = events


def layer_norm(values, gain):
    row_mean = jnp.mean(values, axis=-1, keepdims=True)
    centred = values - row_mean
    variance = jnp.mean(centred * centred, axis=-1, keepdims=True)
    return centred * lax.rsqrt(variance + 1e-05) * gain


def neighbours(segments):
    equal = (segments[1:] == segments[:-1]).astype(jnp.float32)
    blank = jnp.zeros((1,), jnp.float32)
    return (jnp.concatenate([blank, equal]), jnp.concatenate([equal, blank]))


def table_size(pack_len):
    return -(-(pack_len + 1) // FTILE) * FTILE


def split(values):
    upper = values.astype(jnp.bfloat16)
    lower = (values - upper.astype(jnp.float32)).astype(jnp.bfloat16)
    return upper, lower


def mm(a, b):
    return jnp.dot(a, b, preferred_element_type=jnp.float32)


def mm_t(a, b):
    return lax.dot_general(a, b, (((1,), (1,)), ((), ())), preferred_element_type=jnp.float32)


def mm3(upper, lower, b_upper, b_lower):
    return mm(upper, b_upper) + (mm(upper, b_lower) + mm(lower, b_upper))


STEP = 32


def tables_kernel(coarse_cos, coarse_sin, fine_cos, fine_sin, cos_hi, cos_lo, sin_hi, sin_lo):
    def body(p, carry):
        cc = coarse_cos[pl.ds(p, 1), :]
        cs = coarse_sin[pl.ds(p, 1), :]
        rows = pl.ds(pl.multiple_of(p * STEP, STEP), STEP)
        upper, lower = split(cc * fine_cos[...] - cs * fine_sin[...])
        cos_hi[rows, :] = upper
        cos_lo[rows, :] = lower
        upper, lower = split(cs * fine_cos[...] + cc * fine_sin[...])
        sin_hi[rows, :] = upper
        sin_lo[rows, :] = lower
        return carry

    lax.fori_loop(0, cos_hi.shape[0] // STEP, body, 0)


def spectral_tables(pack_len):
    size = table_size(pack_len)
    period = 2 * pack_len
    column = np.arange(size, dtype=np.int64)[None, :]
    coarse = (np.arange(size // STEP, dtype=np.int64)[:, None] * STEP * column) % period
    fine = (np.arange(STEP, dtype=np.int64)[:, None] * column) % period
    to_angle = 2.0 * np.pi / period
    small = [f(x * to_angle).astype(np.float32) for x in (coarse, fine) for f in (np.cos, np.sin)]
    return pl.pallas_call(
        tables_kernel,
        out_shape=[jax.ShapeDtypeStruct((size, size), jnp.bfloat16)] * 4,
        cost_estimate=pl.CostEstimate(flops=int(4 * PEAK), bytes_accessed=0, transcendentals=0),
        name="tables",
    )(*small)


def row_before(values):
    return pltpu.roll(values, 1, 0)


def row_after(values):
    return pltpu.roll(values, values.shape[0] - 1, 0)


def freq_weight(pack_len, step, shape):
    f = lax.broadcasted_iota(jnp.int32, shape, 0) + step * FTILE
    edge = (f == 0) | (f == pack_len)
    weight = jnp.where(edge, 1.0, 2.0) / (2.0 * pack_len)
    return f <= pack_len, jnp.where(f <= pack_len, weight, 0.0)


def join(whole_rows, parts, places):
    for k, part in enumerate(parts):
        count = part.shape[0]
        at = pl.ds(pl.multiple_of(places[k] * count, 8), count)
        whole_rows[at, :] = part[...]


def mixer_kernel(nb, np_, order, places, *refs):
    rows = refs[:nb]
    w_parts, s_parts = refs[nb : nb + np_], refs[nb + np_ : nb + 2 * np_]
    refs = refs[nb + 2 * np_ :]
    (taps, cols, ch_r, cl_r, sh_r, sl_r, ch_c, cl_c, sh_c, sl_c) = refs[:10]
    parts = refs[10 : nb + 10]
    (gathered, mix, proj, long, cond_hat, piece_hat) = refs[nb + 10 : nb + 16]
    x_hi, x_lo, acc, query, w_in_out, spectrum = refs[nb + 16 :]
    step = pl.program_id(0)
    count = rows[0].shape[0]
    pack_len = proj.shape[0]
    width = mix.shape[2]
    scale = 1.0 / math.sqrt(pack_len)

    @pl.when(step == 0)
    def _():
        join(w_in_out, w_parts, places)
        for j in range(nb):
            gathered[j] = rows[j][...]
            at = pl.ds(pl.multiple_of(order[j] * count, 8), count)
            proj[at, :] = mm_t(rows[j][...], w_in_out[: 3 * width, :])
        prev = cols[:, 0:1]
        nxt = cols[:, 1:2]

        def short(values, w0, w1, w2):
            return w0 * (row_before(values) * prev) + w1 * values + w2 * (row_after(values) * nxt)

        def one(k):
            return short(
                proj[:, k * width : (k + 1) * width],
                taps[0, k : k + 1, :],
                taps[0, 3 + k : 4 + k, :],
                taps[0, 6 + k : 7 + k, :],
            )

        query[...] = one(0)
        condition = short(one(1), taps[0, 9:10, :], taps[0, 10:11, :], taps[0, 11:12, :])
        value = one(2)
        x_hi[pack_len:, :] = jnp.zeros((x_hi.shape[0] - pack_len, x_hi.shape[1]), jnp.bfloat16)
        x_lo[pack_len:, :] = jnp.zeros((x_hi.shape[0] - pack_len, x_hi.shape[1]), jnp.bfloat16)
        pieces = [value * cols[:, 2 + g : 3 + g] for g in range(SEGS)] + [condition]
        for g, piece in enumerate(pieces):
            upper, lower = split(piece)
            x_hi[:pack_len, g * width : (g + 1) * width] = upper
            x_lo[:pack_len, g * width : (g + 1) * width] = lower
        acc[...] = jnp.zeros_like(acc)

    wide = SEGS * width
    hat_re = mm3(ch_r[...], cl_r[...], x_hi[...], x_lo[...])
    hat_im = -mm3(sh_r[...], sl_r[...], x_hi[...], x_lo[...])
    v_re, v_im = hat_re[:, :wide], hat_im[:, :wide]
    c_re, c_im = hat_re[:, wide:], hat_im[:, wide:]
    cond_hat[0] = c_re
    cond_hat[1] = c_im
    piece_hat[0] = v_re
    piece_hat[1] = v_im
    gain_in = taps[0, 12:13, :] * scale
    gain_out = taps[0, 13:14, :]
    inside, weight = freq_weight(pack_len, step, c_re.shape)
    join(spectrum, s_parts, places)
    s_re = jnp.transpose(spectrum[:width, :])
    s_im = jnp.transpose(spectrum[width:, :])
    f_re = jnp.where(inside, s_re + gain_out * jnp.tanh(gain_in * c_re), 0.0) * weight
    f_im = jnp.where(inside, s_im + gain_out * jnp.tanh(gain_in * c_im), 0.0) * weight
    f_re = jnp.concatenate([f_re] * SEGS, axis=1)
    f_im = jnp.concatenate([f_im] * SEGS, axis=1)
    p_hi, p_lo = split(v_re * f_re - v_im * f_im)
    m_hi, m_lo = split(-(v_re * f_im + v_im * f_re))
    acc[...] += mm3(ch_c[...], cl_c[...], p_hi, p_lo) + mm3(sh_c[...], sl_c[...], m_hi, m_lo)

    @pl.when(step == pl.num_programs(0) - 1)
    def _():
        total = acc[:, :width] * cols[:, 2:3]
        for g in range(1, SEGS):
            total = total + acc[:, g * width : (g + 1) * width] * cols[:, 2 + g : 3 + g]
        long[...] = total
        query[...] = query[...] * total
        for j in range(nb):
            at = pl.ds(pl.multiple_of(order[j] * count, 8), count)
            mixed = query[at, :].astype(jnp.bfloat16)
            mix[j] = mixed
            parts[j][...] = mm(mixed, w_in_out[3 * width :, :])


def table_specs(size, pack_len):
    row = pl.BlockSpec((FTILE, size), lambda i: (i, 0))
    col = pl.BlockSpec((pack_len, FTILE), lambda i: (0, i))
    return [row] * 4 + [col] * 4


def whole(shape):
    zeros = (0,) * len(shape)
    return pl.BlockSpec(shape, lambda i: zeros)


def of_layer(layer, shape):
    rest = (0,) * len(shape)
    return pl.BlockSpec((1,) + shape, lambda i: (layer,) + rest)


SMEM = pl.BlockSpec(memory_space=pltpu.SMEM)


def part_specs(w_in_out, spectra):
    return [whole(p.shape) for p in w_in_out] + [
        pl.BlockSpec((p.shape[0], FTILE), lambda i: (0, i)) for p in spectra
    ]


def part_scratch(w_in_out, spectra):
    peers = len(w_in_out)
    return [
        pltpu.VMEM((peers * w_in_out[0].shape[0], w_in_out[0].shape[1]), jnp.bfloat16),
        pltpu.VMEM((peers * spectra[0].shape[0], FTILE), jnp.float32),
    ]


def mixer_forward(blocks, w_in_out, taps, cols, spectra, tables, order, places):
    layer = 0
    pack_len = cols.shape[0]
    nb = len(blocks)
    count, model = blocks[0].shape
    width = taps.shape[2]
    size = tables[0].shape[0]
    f32, low = jnp.float32, jnp.bfloat16
    out = pl.pallas_call(
        partial(mixer_kernel, nb, len(w_in_out)),
        grid=(size // FTILE,),
        in_specs=[SMEM, SMEM]
        + [whole((count, model))] * nb
        + part_specs(w_in_out, spectra)
        + [of_layer(layer, taps.shape[1:]), whole(cols.shape)]
        + table_specs(size, pack_len),
        out_specs=[whole((count, model))] * nb
        + [
            whole((nb, count, model)),
            whole((nb, count, width)),
            whole((pack_len, 3 * width)),
            whole((pack_len, width)),
            pl.BlockSpec((2, FTILE, width), lambda i: (0, i, 0)),
            pl.BlockSpec((2, FTILE, SEGS * width), lambda i: (0, i, 0)),
        ],
        out_shape=[jax.ShapeDtypeStruct((count, model), f32)] * nb
        + [
            jax.ShapeDtypeStruct((nb, count, model), low),
            jax.ShapeDtypeStruct((nb, count, width), low),
            jax.ShapeDtypeStruct((pack_len, 3 * width), f32),
            jax.ShapeDtypeStruct((pack_len, width), f32),
            jax.ShapeDtypeStruct((2, size, width), f32),
            jax.ShapeDtypeStruct((2, size, SEGS * width), f32),
        ],
        scratch_shapes=[
            pltpu.VMEM((size, (SEGS + 1) * width), low),
            pltpu.VMEM((size, (SEGS + 1) * width), low),
            pltpu.VMEM((pack_len, SEGS * width), f32),
            pltpu.VMEM((pack_len, width), f32),
        ]
        + part_scratch(w_in_out, spectra),
        compiler_params=pltpu.CompilerParams(vmem_limit_bytes=VMEM_LIMIT),
        cost_estimate=pl.CostEstimate(flops=int(26 * PEAK), bytes_accessed=0, transcendentals=0),
        name="mixer_forward",
    )(order, places, *blocks, *w_in_out, *spectra, taps, cols, *tables, *tables)
    return out[:nb], out[nb].reshape(pack_len, model), out[nb + 1].reshape(pack_len, width), out[nb + 2 :]


def mixer_grad_kernel(nb, np_, order, places, *refs):
    grads = refs[:nb]
    w_parts, s_parts = refs[nb : nb + np_], refs[nb + np_ : nb + 2 * np_]
    refs = refs[nb + 2 * np_ :]
    (taps, cols, proj, long, cond_hat, piece_hat) = refs[:6]
    (ch_r, cl_r, sh_r, sl_r, ch_c, cl_c, sh_c, sl_c) = refs[6:14]
    partials = refs[14 : nb + 14]
    gathered, proj_grad, grad_spectrum, grad_taps = refs[nb + 14 : nb + 18]
    x_hi, x_lo, acc, query_grad, full, w_in_out, spectrum = refs[nb + 18 :]
    step = pl.program_id(0)
    count = grads[0].shape[0]
    pack_len = proj.shape[0]
    width = long.shape[1]
    wide = SEGS * width
    scale = 1.0 / math.sqrt(pack_len)

    def short(values, w0, w1, w2):
        return (
            w0 * (row_before(values) * cols[:, 0:1])
            + w1 * values
            + w2 * (row_after(values) * cols[:, 1:2])
        )

    @pl.when(step == 0)
    def _():
        join(w_in_out, w_parts, places)
        for j in range(nb):
            gathered[j] = grads[j][...]
            at = pl.ds(pl.multiple_of(order[j] * count, 8), count)
            query_grad[at, :] = mm_t(grads[j][...], w_in_out[3 * width :, :])
        query = short(proj[:, :width], taps[0, 0:1, :], taps[0, 3:4, :], taps[0, 6:7, :])
        mix_grad = query_grad[...]
        long_grad = mix_grad * query
        query_grad[...] = mix_grad * long[...]
        x_hi[pack_len:, :] = jnp.zeros((x_hi.shape[0] - pack_len, wide), jnp.bfloat16)
        x_lo[pack_len:, :] = jnp.zeros((x_hi.shape[0] - pack_len, wide), jnp.bfloat16)
        for g in range(SEGS):
            upper, lower = split(long_grad * cols[:, 2 + g : 3 + g])
            x_hi[:pack_len, g * width : (g + 1) * width] = upper
            x_lo[:pack_len, g * width : (g + 1) * width] = lower
        acc[...] = jnp.zeros_like(acc)
        grad_taps[...] = jnp.zeros_like(grad_taps)

    c_re, c_im = cond_hat[0], cond_hat[1]
    inside, weight = freq_weight(pack_len, step, c_re.shape)
    w4 = jnp.concatenate([weight] * SEGS, axis=1)
    b_re = mm3(ch_r[...], cl_r[...], x_hi[...], x_lo[...]) * w4
    b_im = mm3(sh_r[...], sl_r[...], x_hi[...], x_lo[...]) * (-w4)
    v_re, v_im = piece_hat[0], piece_hat[1]

    def over_segments(values):
        total = values[:, :width]
        for g in range(1, SEGS):
            total = total + values[:, g * width : (g + 1) * width]
        return total

    h_re = over_segments(v_re * b_re + v_im * b_im)
    h_im = over_segments(v_re * b_im - v_im * b_re)
    grad_spectrum[0] = jnp.transpose(h_re).astype(jnp.bfloat16)
    grad_spectrum[1] = jnp.transpose(h_im).astype(jnp.bfloat16)
    gain_in = taps[0, 12:13, :] * scale
    gain_out = taps[0, 13:14, :]
    t_re = jnp.tanh(gain_in * c_re)
    t_im = jnp.tanh(gain_in * c_im)
    join(spectrum, s_parts, places)
    f_re = jnp.where(inside, jnp.transpose(spectrum[:width, :]) + gain_out * t_re, 0.0)
    f_im = jnp.where(inside, jnp.transpose(spectrum[width:, :]) + gain_out * t_im, 0.0)
    a_re = h_re * gain_out * (1.0 - t_re * t_re)
    a_im = h_im * gain_out * (1.0 - t_im * t_im)
    grad_taps[12:13, :] += jnp.sum(a_re * c_re + a_im * c_im, axis=0, keepdims=True) * scale
    grad_taps[13:14, :] += jnp.sum(h_re * t_re + h_im * t_im, axis=0, keepdims=True)
    f_re = jnp.concatenate([f_re] * SEGS, axis=1)
    f_im = jnp.concatenate([f_im] * SEGS, axis=1)
    p = jnp.concatenate([f_re * b_re + f_im * b_im, a_re * gain_in], axis=1)
    m = jnp.concatenate([f_im * b_re - f_re * b_im, -(a_im * gain_in)], axis=1)
    p_hi, p_lo = split(p)
    m_hi, m_lo = split(m)
    acc[...] += mm3(ch_c[...], cl_c[...], p_hi, p_lo) + mm3(sh_c[...], sl_c[...], m_hi, m_lo)

    @pl.when(step == pl.num_programs(0) - 1)
    def _():
        prev = cols[:, 0:1]
        nxt = cols[:, 1:2]
        value_grad = acc[:, :width] * cols[:, 2:3]
        for g in range(1, SEGS):
            value_grad = value_grad + acc[:, g * width : (g + 1) * width] * cols[:, 2 + g : 3 + g]

        def column_sum(values):
            return jnp.sum(values, axis=0, keepdims=True)

        def adjoint(values, grad, row, stride):
            w0 = taps[0, row : row + 1, :]
            w1 = taps[0, row + stride : row + stride + 1, :]
            w2 = taps[0, row + 2 * stride : row + 2 * stride + 1, :]
            from_prev = prev * grad
            from_next = nxt * grad
            grad_taps[row : row + 1, :] = column_sum(row_before(values) * from_prev)
            grad_taps[row + stride : row + stride + 1, :] = column_sum(values * grad)
            grad_taps[row + 2 * stride : row + 2 * stride + 1, :] = column_sum(
                row_after(values) * from_next
            )
            return w1 * grad + w0 * row_after(from_prev) + w2 * row_before(from_next)

        key_proj = proj[:, width : 2 * width]
        key_part = short(key_proj, taps[0, 1:2, :], taps[0, 4:5, :], taps[0, 7:8, :])
        key_grad = adjoint(key_part, acc[:, wide:], 9, 1)
        parts = [query_grad[...], key_grad, value_grad]
        for j in range(3):
            full[:, j * width : (j + 1) * width] = adjoint(
                proj[:, j * width : (j + 1) * width], parts[j], j, 3
            )
        for j in range(nb):
            at = pl.ds(pl.multiple_of(order[j] * count, 8), count)
            low = full[at, :].astype(jnp.bfloat16)
            proj_grad[j] = low
            partials[j][...] = mm(low, w_in_out[: 3 * width, :])


def mixer_backward(blocks, w_in_out, taps, cols, kept, spectra, tables, order, places):
    layer = 0
    proj, long, cond_hat, piece_hat = kept
    pack_len = cols.shape[0]
    nb = len(blocks)
    count, model = blocks[0].shape
    width = taps.shape[2]
    size = tables[0].shape[0]
    f32, low = jnp.float32, jnp.bfloat16
    freq = pl.BlockSpec((2, FTILE, width), lambda i: (0, i, 0))
    out = pl.pallas_call(
        partial(mixer_grad_kernel, nb, len(w_in_out)),
        grid=(size // FTILE,),
        in_specs=[SMEM, SMEM]
        + [whole((count, model))] * nb
        + part_specs(w_in_out, spectra)
        + [
            of_layer(layer, taps.shape[1:]),
            whole(cols.shape),
            whole(proj.shape),
            whole(long.shape),
            freq,
            pl.BlockSpec((2, FTILE, SEGS * width), lambda i: (0, i, 0)),
        ]
        + table_specs(size, pack_len),
        out_specs=[whole((count, model))] * nb
        + [
            whole((nb, count, model)),
            whole((nb, count, 3 * width)),
            pl.BlockSpec((2, width, FTILE), lambda i: (0, 0, i)),
            whole(taps.shape[1:]),
        ],
        out_shape=[jax.ShapeDtypeStruct((count, model), f32)] * nb
        + [
            jax.ShapeDtypeStruct((nb, count, model), low),
            jax.ShapeDtypeStruct((nb, count, 3 * width), low),
            jax.ShapeDtypeStruct((2, width, size), low),
            jax.ShapeDtypeStruct(taps.shape[1:], f32),
        ],
        scratch_shapes=[
            pltpu.VMEM((size, SEGS * width), low),
            pltpu.VMEM((size, SEGS * width), low),
            pltpu.VMEM((pack_len, (SEGS + 1) * width), f32),
            pltpu.VMEM((pack_len, width), f32),
            pltpu.VMEM((pack_len, 3 * width), f32),
        ]
        + part_scratch(w_in_out, spectra),
        compiler_params=pltpu.CompilerParams(vmem_limit_bytes=VMEM_LIMIT),
        cost_estimate=pl.CostEstimate(flops=int(30 * PEAK), bytes_accessed=0, transcendentals=0),
        name="mixer_backward",
    )(
        order, places, *blocks, *w_in_out, *spectra, taps, cols, proj, long, cond_hat, piece_hat,
        *tables, *tables,
    )
    rows, proj_grad, grad_spectrum, grad_taps = out[nb:]
    return (
        out[:nb],
        rows.reshape(pack_len, model),
        proj_grad.reshape(pack_len, 3 * width),
        grad_spectrum.reshape(2 * width, size),
        grad_taps,
    )


def glu_kernel(nb, np_, places, *refs):
    rows = refs[:nb]
    gu_parts, down_parts = refs[nb : nb + np_], refs[nb + np_ : nb + 2 * np_]
    refs = refs[nb + 2 * np_ :]
    parts = refs[:nb]
    gathered, gate, up, act, total, gate_up, down_w = refs[nb:]
    step = pl.program_id(0)
    count, model = rows[0].shape
    tile = gate.shape[1]
    join(gate_up, gu_parts, places)

    @pl.when(step == 0)
    def _():
        join(down_w, down_parts, places)
        for j in range(nb):
            gathered[j * count : (j + 1) * count, :] = rows[j][...]

    gates = mm(gathered[...], gate_up[:model, :])
    ups = mm(gathered[...], gate_up[model:, :])
    gate[...] = gates
    up[...] = ups
    low = (gates * jax.nn.sigmoid(gates) * ups).astype(jnp.bfloat16)
    act[...] = low
    grown = mm(low, down_w[pl.ds(pl.multiple_of(step * tile, tile), tile), :])

    @pl.when(step == 0)
    def _():
        total[...] = grown

    @pl.when(step > 0)
    def _():
        total[...] += grown

    @pl.when(step == pl.num_programs(0) - 1)
    def _():
        for j in range(nb):
            parts[j][...] = total[j * count : (j + 1) * count, :]


def glu_specs(gate_up, down, tile):
    return [pl.BlockSpec((p.shape[0], tile), lambda i: (0, i)) for p in gate_up] + [
        whole(p.shape) for p in down
    ]


def glu_scratch(gate_up, down, tile):
    peers = len(down)
    return [
        pltpu.VMEM((peers * gate_up[0].shape[0], tile), jnp.bfloat16),
        pltpu.VMEM((peers * down[0].shape[0], down[0].shape[1]), jnp.bfloat16),
    ]


def glu_forward(blocks, gate_up, down, places):
    nb = len(blocks)
    count, model = blocks[0].shape
    hidden = len(down) * down[0].shape[0]
    tile = min(HTILE, hidden)
    length = nb * count
    f32, low = jnp.float32, jnp.bfloat16
    column = pl.BlockSpec((length, tile), lambda i: (0, i))
    out = pl.pallas_call(
        partial(glu_kernel, nb, len(down)),
        grid=(hidden // tile,),
        in_specs=[SMEM] + [whole((count, model))] * nb + glu_specs(gate_up, down, tile),
        out_specs=[whole((count, model))] * nb + [whole((length, model))] + [column] * 3,
        out_shape=[jax.ShapeDtypeStruct((count, model), f32)] * nb
        + [
            jax.ShapeDtypeStruct((length, model), low),
            jax.ShapeDtypeStruct((length, hidden), f32),
            jax.ShapeDtypeStruct((length, hidden), f32),
            jax.ShapeDtypeStruct((length, hidden), low),
        ],
        scratch_shapes=[pltpu.VMEM((length, model), f32)] + glu_scratch(gate_up, down, tile),
        compiler_params=pltpu.CompilerParams(vmem_limit_bytes=VMEM_LIMIT),
        cost_estimate=pl.CostEstimate(flops=int(9 * PEAK), bytes_accessed=0, transcendentals=0),
        name="glu_forward",
    )(places, *blocks, *gate_up, *down)
    return out[:nb], out[nb:]


def glu_grad_kernel(nb, np_, places, *refs):
    rows = refs[:nb]
    gate, up = refs[nb : nb + 2]
    gu_parts, down_parts = refs[nb + 2 : nb + 2 + np_], refs[nb + 2 + np_ : nb + 2 + 2 * np_]
    refs = refs[nb + 2 + 2 * np_ :]
    parts = refs[:nb]
    gathered, gate_grad, up_grad, total, gate_up, down_w = refs[nb:]
    step = pl.program_id(0)
    count, model = rows[0].shape
    tile = gate.shape[1]
    join(gate_up, gu_parts, places)

    @pl.when(step == 0)
    def _():
        join(down_w, down_parts, places)
        for j in range(nb):
            gathered[j * count : (j + 1) * count, :] = rows[j][...]

    act_grad = mm_t(gathered[...], down_w[pl.ds(pl.multiple_of(step * tile, tile), tile), :])
    gates = gate[...]
    s = jax.nn.sigmoid(gates)
    low_gate = (act_grad * up[...] * (s * (1.0 + gates * (1.0 - s)))).astype(jnp.bfloat16)
    low_up = (act_grad * (gates * s)).astype(jnp.bfloat16)
    gate_grad[...] = low_gate
    up_grad[...] = low_up
    grown = mm_t(low_gate, gate_up[:model, :]) + mm_t(low_up, gate_up[model:, :])

    @pl.when(step == 0)
    def _():
        total[...] = grown

    @pl.when(step > 0)
    def _():
        total[...] += grown

    @pl.when(step == pl.num_programs(0) - 1)
    def _():
        for j in range(nb):
            parts[j][...] = total[j * count : (j + 1) * count, :]


def glu_backward(blocks, gate, up, gate_up, down, places):
    nb = len(blocks)
    count, model = blocks[0].shape
    hidden = len(down) * down[0].shape[0]
    tile = min(HTILE, hidden)
    length = nb * count
    f32, low = jnp.float32, jnp.bfloat16
    column = pl.BlockSpec((length, tile), lambda i: (0, i))
    out = pl.pallas_call(
        partial(glu_grad_kernel, nb, len(down)),
        grid=(hidden // tile,),
        in_specs=[SMEM] + [whole((count, model))] * nb + [column] * 2 + glu_specs(gate_up, down, tile),
        out_specs=[whole((count, model))] * nb + [whole((length, model))] + [column] * 2,
        out_shape=[jax.ShapeDtypeStruct((count, model), f32)] * nb
        + [
            jax.ShapeDtypeStruct((length, model), low),
            jax.ShapeDtypeStruct((length, hidden), low),
            jax.ShapeDtypeStruct((length, hidden), low),
        ],
        scratch_shapes=[pltpu.VMEM((length, model), f32)] + glu_scratch(gate_up, down, tile),
        compiler_params=pltpu.CompilerParams(vmem_limit_bytes=VMEM_LIMIT),
        cost_estimate=pl.CostEstimate(flops=int(9.5 * PEAK), bytes_accessed=0, transcendentals=0),
        name="glu_backward",
    )(places, *blocks, gate, up, *gate_up, *down)
    return out[:nb], out[nb:]


def dot32(spec, a, b):
    return jnp.einsum(spec, a, b, preferred_element_type=jnp.float32)


def low(values):
    return values.astype(jnp.bfloat16)


def add(old, new):
    return new if old is None else old + new


def exchange_dq(grad):
    peers = lax.axis_size("dq")
    dq = lax.axis_index("dq")
    parts = low(grad).reshape(peers, grad.shape[0] // peers, grad.shape[1])
    moved = [shift(parts[(dq + k) % peers], "dq", k) for k in range(1, peers)]
    return parts[dq], moved


def total_dq(own, moved):
    total = own.astype(jnp.float32)
    for term in moved:
        total = total + term.astype(jnp.float32)
    return total


def to_section(total, target):
    source = 1 - target
    return permute(low(total), ("section",), lambda s: (target,) if s == source else None)


def own_part(own):
    count = own.shape[0] // lax.axis_size("dq")
    return lax.dynamic_slice_in_dim(own, lax.axis_index("dq") * count, count, 0)


def join_parts(part):
    return [part] + [shift(part, "dq", k) for k in range(1, lax.axis_size("dq"))]


def to_holder(total):
    return permute(low(total), ("core", "th"), lambda c, h: (c, 1 - h) if c != h else None)


def quarters(total, other):
    core, high_part = lax.axis_index("core"), lax.axis_index("th")
    total = low(total + other.astype(jnp.float32))
    halves = total.reshape(2, total.shape[0] // 2, total.shape[1])
    got = permute(halves[1 - core], ("core", "th"), lambda c, h: (1 - c, h) if c == h else None)
    quarter = jnp.where(core == high_part, halves[core], got)
    peers = lax.axis_size("dq")
    joined = [quarter] + [shift(quarter, "dq", k) for k in range(1, peers)]
    return joined + [swap_core(block) for block in joined]


def quarter_places():
    core, dq, peers = lax.axis_index("core"), lax.axis_index("dq"), lax.axis_size("dq")
    return jnp.stack(
        [
            (dq - k) % peers * 2 + jnp.bitwise_xor(core, c)
            for c in range(2)
            for k in range(peers)
        ]
    ).astype(jnp.int32)


def assemble_kernel(counts, finish, places, *refs):
    taken = 0
    n_out = len(refs) - sum(counts) - len(counts)
    outs = refs[sum(counts) : sum(counts) + n_out]
    joined = refs[sum(counts) + n_out :]
    for buffer, nb in zip(joined, counts):
        for j in range(nb):
            block = refs[taken + j]
            rows = block.shape[0]
            at = pl.ds(pl.multiple_of(places[j] * rows, 8), rows)
            buffer[at, :] = block[...].astype(jnp.float32)
        taken += nb
    finish(joined, outs)


def assemble(messages, finish, out_shapes):
    counts = [len(blocks) for blocks in messages]
    vmem = pl.BlockSpec(memory_space=pltpu.VMEM)
    return pl.pallas_call(
        partial(assemble_kernel, counts, finish),
        in_specs=[pl.BlockSpec(memory_space=pltpu.SMEM)] + [vmem] * sum(counts),
        out_specs=[vmem] * len(out_shapes),
        out_shape=[jax.ShapeDtypeStruct(s, jnp.float32) for s in out_shapes],
        scratch_shapes=[
            pltpu.VMEM((len(blocks) * blocks[0].shape[0], blocks[0].shape[1]), jnp.float32)
            for blocks in messages
        ],
        compiler_params=pltpu.CompilerParams(vmem_limit_bytes=VMEM_LIMIT),
        cost_estimate=pl.CostEstimate(flops=int(4 * PEAK), bytes_accessed=0, transcendentals=0),
        name="assemble",
    )(quarter_places(), *[block for blocks in messages for block in blocks])


def pack(arrays):
    if len({a.shape[1] for a in arrays}) == 1:
        return [jnp.concatenate(arrays, axis=0)]
    return list(arrays)


def row_reader(buffers):
    state = [0, 0]

    def take(rows):
        at, offset = state
        if offset + rows > buffers[at].shape[0]:
            at, offset = at + 1, 0
        state[0], state[1] = at, offset + rows
        return buffers[at][offset : offset + rows, :]

    return take


def per_device(
    tokens,
    segment_ids,
    cotangent,
    norm_gain1,
    w_in,
    short_taps,
    cond_taps,
    spectrum,
    spectral_gain,
    w_out,
    norm_gain2,
    w_gate_up,
    w_down,
):
    slots, row_count, width = tokens.shape
    pack_len = segment_ids.shape[1]
    channels = w_in.shape[3]
    hidden_cols = w_gate_up.shape[3]
    place5 = tuple(lax.axis_index(a) for a in ALL_AXES)
    section, dq, core, high_part, along = place5
    packs = slots // 2
    peers = lax.axis_size("tl")
    order = jnp.stack(
        [jnp.bitwise_xor(core, c) * peers + (along - t) % peers for c in range(2) for t in range(peers)]
    ).astype(jnp.int32)

    tables = spectral_tables(pack_len)

    def own_slots(array):
        return lax.dynamic_slice_in_dim(array, section * packs, packs, 0)

    freqs = spectrum.shape[2]
    dqs = lax.axis_size("dq")
    places = jnp.stack([(dq - k) % dqs for k in range(dqs)]).astype(jnp.int32)
    w_in_t = jnp.transpose(w_in[0], (1, 2, 0)).reshape(3 * channels, width)
    spectrum_t = jnp.transpose(spectrum[0], (0, 2, 1)).reshape(2 * channels, freqs)
    io_own = own_part(jnp.concatenate([w_in_t, w_out[0]], axis=0))
    sp_own = own_part(spectrum_t)
    per = 2 * width // dqs
    gu_own = lax.dynamic_slice(
        w_gate_up[0], (dq * per % width, dq * 2 // dqs, 0), (per, 1, hidden_cols)
    ).reshape(per, hidden_cols)
    dn_own = own_part(w_down[0])
    rows_in = after(transposed(own_slots(tokens)), gu_own, dn_own)
    first_wave = (transposed(io_own), transposed(sp_own))
    swapped = permute(segment_ids.astype(jnp.float32), ("core",), lambda c: (1 - c,))
    ids_both = jnp.stack([segment_ids, swapped.astype(jnp.int32)])
    segments = own_slots(ids_both[jnp.bitwise_xor(core, high_part)])
    first = section == 0
    own_taps = jnp.concatenate(
        [
            short_taps[0].reshape(9, channels),
            cond_taps[0],
            spectral_gain[0],
            jnp.zeros((2, channels), jnp.float32),
        ],
        axis=0,
    )
    own_taps = transposed(own_taps)
    own_gains = jnp.concatenate([norm_gain1, norm_gain2], axis=0)

    def both_layers(own):
        other = swap_section(own)
        return jnp.stack([jnp.where(first, own, other), jnp.where(first, other, own)])

    taps = both_layers(own_taps)
    gains = both_layers(own_gains)

    def columns(ids):
        prev, nxt = neighbours(ids)
        masks = [(ids == g).astype(jnp.float32) for g in range(SEGS)]
        return jnp.stack([prev, nxt] + masks + [jnp.zeros_like(prev)] * 2, axis=1)

    cols = [columns(segments[index]) for index in range(packs)]
    line = Line()

    def by_layer(part, other):
        return jnp.where(first, part, other), jnp.where(first, other, part)

    w_io, spectra, gate_up, down = [None, None], [None, None], [None, None], [None, None]
    results = [[], []]
    saved = [[], []]
    late = []
    for index in range(packs):
        state = rows_in[index].astype(jnp.float32)
        for layer in range(2):
            opening = index == 0 and layer == 0
            normed, norm_pull = jax.vjp(layer_norm, state, gains[layer, 0])
            blocks = gather_rows(low(normed))
            if opening:
                line.mark(blocks)
                io_part, sp_part = line.take(first_wave)
                io_other, sp_other = swap_section(io_part), swap_section(sp_part)
                held = after((gu_own, dn_own), io_part, sp_part)
                gu_moved, dn_moved = transposed(held[0]), transposed(held[1])
                sp_both = by_layer(sp_part, sp_other)
                spectra[0] = join_parts(sp_both[0])
                io_both = by_layer(io_part, io_other)
                w_io[0] = join_parts(io_both[0])
                line.mark(io_both[0], sp_both[0])
                gu_part, dn_part = line.take((gu_moved, dn_moved))
                gu_other, dn_other = swap_section(gu_part), swap_section(dn_part)
                blocks = after(blocks, gu_part, dn_part)
            parts, gathered, mix, kept = mixer_forward(
                blocks, w_io[layer], taps[layer : layer + 1], cols[index], spectra[layer], tables,
                order, places,
            )
            if opening:
                gu_both = by_layer(gu_part, after(gu_other, parts))
                parts = after(parts, gu_both[0])
            sums_of = core_sums(parts)
            if opening:
                gate_up[0] = join_parts(gu_both[0])
                dn_both = by_layer(dn_part, after(dn_other, sums_of))
                down[0] = join_parts(dn_both[0])
            if layer == 1:
                cot_blocks = both_cores(after(cot_chip, sums_of))
            hidden = state + chip_sums(sums_of)
            normed_two, norm_pull_two = jax.vjp(layer_norm, hidden, gains[layer, 1])
            blocks = gather_rows(low(normed_two))
            if opening:
                io_part, sp_part = after((io_both[1], sp_both[1]), blocks)
                w_io[1] = join_parts(io_part)
                spectra[1] = join_parts(sp_part)
            parts, (gathered_two, gate, up, act) = glu_forward(
                blocks, gate_up[layer], down[layer], places
            )
            saved[layer].append(
                (norm_pull, gathered, mix, kept, norm_pull_two, gathered_two, gate, up, act)
            )
            if layer == 0:
                sums_of = core_sums(parts)
                if opening:
                    gu_part, dn_part = after((gu_both[1], dn_both[1]), sums_of)
                    gate_up[1] = join_parts(gu_part)
                    down[1] = join_parts(dn_part)
                    cot_in = transposed(own_slots(after(cotangent, sums_of)))
                state = hidden + chip_sums(sums_of)
                results[0].append(state)
                cot_chip = chip_blocks(after(cot_in[index], state))
            else:
                late.append((hidden, parts, cot_blocks))

    def deliver(zero, one):
        keep = transposed(jnp.where(first, zero, one))
        given = permute(
            jnp.where(first, one, zero),
            ("section", "core", "th"),
            lambda s, c, h: (1 - s, h, c),
        )
        return keep, given

    def ordered(keep, given):
        lead = jnp.where(first, keep, given)
        trail = jnp.where(first, given, keep)
        return jnp.concatenate([lead, trail], axis=0).astype(jnp.float32)

    sums = [{}, {}]

    def collect(layer, terms, last):
        for name, term in terms.items():
            total = term if name not in sums[layer] else sums[layer][name] + term
            sums[layer][name] = low(total) if last else total.astype(jnp.float32)

    def glu_terms(layer, kept, sums_of, grad_rows, gate_grad, up_grad, last):
        act, rows_two, grad_rows, gate_grad, up_grad = after(
            (kept[8], kept[5], grad_rows, gate_grad, up_grad), sums_of
        )
        half = width // 2
        terms = {
            "down": dot32("lf,ld->fd", act, grad_rows),
            "gate_a": dot32("ld,lf->df", rows_two[:, :half], gate_grad),
            "gate_b": dot32("ld,lf->df", rows_two[:, half:], gate_grad),
            "up": dot32("ld,lf->df", rows_two, up_grad),
        }
        collect(layer, terms, last)

    def mix_terms(layer, kept, sums_of, mix_rows, proj_grad, spectrum_grad, last):
        mix, mix_rows, proj_grad, rows_one = after((kept[2], mix_rows, proj_grad, kept[1]), sums_of)
        terms = {
            "w_in": dot32("lc,ld->cd", proj_grad, rows_one),
            "w_out": dot32("lc,ld->cd", mix, mix_rows),
            "spectrum": spectrum_grad,
        }
        collect(layer, terms, last)

    contents = (("down", "gate_a"), ("gate_b", "up"), ("w_in", "w_out", "spectrum"))
    own = [{}, {}]
    moved = [{}, {}]
    crossed = [{}, {}]

    def send_dq(layer, *messages):
        for m in messages:
            arrays = pack([sums[layer][name] for name in contents[m]])
            sent = [exchange_dq(a) for a in arrays]
            own[layer][m] = [s[0] for s in sent]
            moved[layer][m] = [s[1] for s in sent]

    def send_section(layer, m, *events):
        terms = after(moved[layer][m], *events)
        own[layer][m] = [total_dq(o, t) for o, t in zip(own[layer][m], terms)]
        crossed[layer][m] = [to_section(o, layer) for o in own[layer][m]]

    small_sum = [None, None]
    gain_sum = [None, None]
    grads_in = [[], []]
    for index in range(packs):
        last = index == packs - 1
        state = cot_in[index].astype(jnp.float32)
        kept = saved[1][index]
        late_hidden, late_parts, cot_blocks = late[index]
        parts, (grad_rows, gate_grad, up_grad) = glu_backward(
            cot_blocks, kept[6], kept[7], gate_up[1], down[1], places
        )
        sums_of = core_sums(parts)
        glu_terms(1, kept, sums_of, grad_rows, gate_grad, up_grad, last)
        if last:
            send_dq(1, 0, 1)
        grad_part, gain_two = kept[4](chip_sums(sums_of))
        hidden_grad = state + grad_part
        blocks = gather_rows(low(hidden_grad))
        late_sums = core_sums(after(late_parts, blocks))
        parts, mix_rows, proj_grad, spectrum_grad, tap_grad = mixer_backward(
            blocks, w_io[1], taps[1:2], cols[index], kept[3], spectra[1], tables, order, places
        )
        sums_of = core_sums(parts)
        mix_terms(1, kept, sums_of, mix_rows, proj_grad, spectrum_grad, last)
        moved_sums = sent_sums(sums_of)
        late_moved = sent_sums(after(late_sums, sums_of))
        if last:
            send_section(1, 0, sums_of)
            send_section(1, 1, sums_of)
            send_dq(1, 2)
            moved_sums = after(moved_sums, own[1][1], own[1][2])
        grad_part, gain_one = kept[0](add_sums(sums_of, moved_sums))
        state = hidden_grad + grad_part
        small_sum[1] = add(small_sum[1], tap_grad)
        gain_sum[1] = add(gain_sum[1], jnp.stack([gain_one, gain_two]))
        grads_in[1].append(state)
        kept = saved[0][index]
        blocks = gather_rows(low(state))
        results[1].append(late_hidden + add_sums(late_sums, after(late_moved, blocks)))
        parts, (grad_rows, gate_grad, up_grad) = glu_backward(
            blocks, kept[6], kept[7], gate_up[0], down[0], places
        )
        sums_of = core_sums(parts)
        glu_terms(0, kept, sums_of, grad_rows, gate_grad, up_grad, last)
        moved_sums = sent_sums(sums_of)
        if last:
            send_dq(0, 0, 1)
            out_sent = deliver(
                low(after(jnp.stack(results[0]), sums_of)), low(after(jnp.stack(results[1]), sums_of))
            )
            moved_sums = after(moved_sums, own[0][1])
            send_section(1, 2, moved_sums)
            moved_sums = after(moved_sums, own[1][2])
        grad_part, gain_two = kept[4](add_sums(sums_of, moved_sums))
        hidden_grad = state + grad_part
        chip = chip_blocks(low(hidden_grad))
        if last:
            send_section(0, 0, hidden_grad)
            chip = after(chip, own[0][0])
        blocks = both_cores(chip)
        if last:
            send_section(0, 1, blocks)
            blocks = after(blocks, own[0][1])
        parts, mix_rows, proj_grad, spectrum_grad, tap_grad = mixer_backward(
            blocks, w_io[0], taps[0:1], cols[index], kept[3], spectra[0], tables, order, places
        )
        sums_of = core_sums(parts)
        mix_terms(0, kept, sums_of, mix_rows, proj_grad, spectrum_grad, last)
        moved_sums = sent_sums(sums_of)
        small_sum[0] = add(small_sum[0], tap_grad)
        if last:
            break
        grad_part, gain_one = kept[0](add_sums(sums_of, moved_sums))
        grads_in[0].append(hidden_grad + grad_part)
        gain_sum[0] = add(gain_sum[0], jnp.stack([gain_one, gain_two]))

    send_dq(0, 2)
    line.mark(own[0][2])
    total = {}
    held = {}

    def send_holder(m):
        terms = line.take((crossed[0][m], crossed[1][m]))
        total[m] = [
            jnp.where(first, o, p) + jnp.where(first, t, u).astype(jnp.float32)
            for o, p, t, u in zip(own[0][m], own[1][m], *terms)
        ]
        line.mark(total[m])
        held[m] = [to_holder(t) for t in total[m]]

    joined = {}

    def send_quarters(m):
        terms = line.take(held[m])
        joined[m] = [quarters(t, o) for t, o in zip(total[m], terms)]
        line.mark([j[0] for j in joined[m]])

    send_holder(0)
    grad_part, gain_one = kept[0](add_sums(sums_of, line.take(moved_sums)))
    state = hidden_grad + grad_part
    grads_in[0].append(state)
    gain_sum[0] = add(gain_sum[0], jnp.stack([gain_one, gain_two]))
    line.mark(state)
    grad_sent = deliver(low(jnp.stack(grads_in[0])), low(jnp.stack(grads_in[1])))
    small = [
        jnp.concatenate(
            [jnp.pad(small_sum[k], ((0, 0), (0, width - channels))), gain_sum[k]], axis=0
        )
        for k in range(2)
    ]
    small_other = swap_section(jnp.where(first, small[1], small[0]))
    send_holder(1)
    send_section(0, 2, line.events)
    line.mark(own[0][2])
    mine = jnp.where(first, small[0], small[1]) + line.take(small_other)
    moved_small = [shift(mine, "dq", k) for k in range(1, lax.axis_size("dq"))]
    line.mark(mine)
    send_quarters(0)
    sum_dq = mine
    for term in line.take(moved_small):
        sum_dq = sum_dq + term
    moved_small = permute(sum_dq, ("th",), lambda h: (1 - h,))
    line.mark(sum_dq)
    layer_out = ordered(*line.take(out_sent))
    line.mark(layer_out)
    send_holder(2)
    mine = sum_dq + line.take(moved_small)
    rows_of = own_taps.shape[0]
    tap_grads = transposed(mine[:rows_of, :channels])
    gain_grads = mine[rows_of:]
    gain_other = swap_core(gain_grads)
    line.mark(mine)
    send_quarters(1)
    gain_grads = gain_grads + line.take(gain_other)
    gain_moved = [shift(gain_grads, "tl", k) for k in range(1, peers)]
    line.mark(gain_grads)
    grad_in = ordered(*line.take(grad_sent))
    line.mark(grad_in)
    send_quarters(2)
    gain_total = gain_grads
    for term in line.take(gain_moved):
        gain_total = gain_total + term

    def finish_wide(buffers, outs):
        take = row_reader(buffers)
        outs[0][...] = take(hidden_cols)
        outs[1][: width // 2, 0, :] = take(width // 2)
        outs[1][width // 2 :, 0, :] = take(width // 2)
        outs[1][:, 1, :] = take(width)

    def finish_rest(buffers, outs):
        take = row_reader(buffers)
        outs[0][...] = take(3 * channels)
        outs[1][...] = take(channels)
        outs[2][...] = take(2 * channels)[:, :freqs]

    grad_down, grad_gate_up = assemble(
        line.take(joined[0] + joined[1]), finish_wide, [(hidden_cols, width), (width, 2, hidden_cols)]
    )
    grad_w_in, grad_w_out, grad_spectrum = assemble(
        after(joined[2], grad_down),
        finish_rest,
        [(3 * channels, width), (channels, width), (2 * channels, freqs)],
    )
    grad_spectrum = grad_spectrum.reshape(2, channels, freqs)
    return (
        layer_out[None],
        grad_in[None],
        gain_total[0:1],
        jnp.transpose(grad_w_in.reshape(3, channels, width), (2, 0, 1))[None],
        tap_grads[:9].reshape(1, 3, 3, channels),
        tap_grads[9:12][None],
        jnp.transpose(grad_spectrum, (0, 2, 1))[None],
        tap_grads[12:14][None],
        grad_w_out[None],
        gain_total[1:2],
        grad_gate_up[None],
        grad_down[None],
    )


def solution(mesh):
    sections, dps, tensors = (mesh.shape[a] for a in ("section", "dp", "tensor"))
    devices = mesh.devices.reshape(sections, dps // 2, 2, 2, tensors // 2)
    fine = Mesh(devices, ALL_AXES)
    dp = ("dq", "core")
    tensor = ("th", "tl")
    return jax.shard_map(
        per_device,
        mesh=fine,
        in_specs=(
            P(dp, tensor, None),
            P(dp, None),
            P(dp, tensor, None),
            P("section", None),
            P("section", None, None, tensor),
            P("section", None, None, tensor),
            P("section", None, tensor),
            P("section", None, None, tensor),
            P("section", None, tensor),
            P("section", tensor, None),
            P("section", None),
            P("section", None, None, tensor),
            P("section", tensor, None),
        ),
        out_specs=(
            P("section", dp, tensor, None),
            P("section", dp, tensor, None),
            P("section", None),
            P("section", None, None, tensor),
            P("section", None, None, tensor),
            P("section", None, tensor),
            P("section", None, None, tensor),
            P("section", None, tensor),
            P("section", tensor, None),
            P("section", None),
            P("section", None, None, tensor),
            P("section", tensor, None),
        ),
        check_vma=False,
    )
```

time: 1070 us -> 687 us (0.64)
  local copies, waits for them, and re-layouts: 253 us -> 30.5 us
  Pallas kernels: 0 us -> 169 us
  other arithmetic: 201 us -> 41.2 us
  matrix products: 149 us -> 9.79 us
  waiting for transfers between devices: 206 us -> 273 us
  starting transfers between devices: 205 us -> 154 us
  blocking collectives: 37 us -> 0 us
    pallas_call x0 -> x11, Pallas kernels: none -> 169 us  [the longest x2 61.9 us: mixer_backward(): pl.pallas_call(partial(mixer_grad_kernel, nb, len(w_in_out)), grid=(size...]
    dot_general x12 -> x0, matrix products: 98.6 us -> none  [the longest x4 45.1 us: orchid_mix(): jnp.dot(forward_table, pieces, precision=high)]
    ppermute x117 -> x107, waiting for transfers between devices: 206 us -> 273 us  [permute(): return lax.ppermute(values, axes if len(axes) > 1 else axes[0], pairs)]
    ppermute x117 -> x107, starting transfers between devices: 205 us -> 154 us  [permute(): return lax.ppermute(values, axes if len(axes) > 1 else axes[0], pairs)]
    dot_general x24 -> x12, matrix products: 50.6 us -> 9.79 us  [dot32(): return jnp.einsum(spec, a, b, preferred_element_type=jnp.float32)]
    reshape x20 -> x1, local copies, waits for them, and re-layouts: 39.7 us -> 0.61 us  [per_device(): tap_grads[:9].reshape(1, 3, 3, channels)]
    convert_element_type x32 -> x22, other arithmetic: 50.7 us -> 13.5 us  [the longest x19 12 us: low(): return values.astype(jnp.bfloat16)]
    psum x1 -> x0, blocking collectives: 37 us -> none  [per_device(): gain_both = lax.psum(gain_both, ALL_AXES)]
  transfers between devices with their start and end apart: 117 -> 107, of which waited for: 30 -> 38; matrix products, arithmetic and copies ran while one was open for 45% -> 9% of each run, Pallas kernels for 0% -> 13%
where the time goes in v2:
time: 687 us; the launch traced here: 681 us
  waiting for transfers between devices  273 us (40%)
  Pallas kernels  169 us (25%)
  starting transfers between devices  154 us (22%)
  other arithmetic  41.2 us (6%)
  local copies, waits for them, and re-layouts  30.5 us (4%)
  matrix products  9.79 us (1%)
    ppermute x107, waiting for transfers between devices, permute(): return lax.ppermute(values, axes if len(axes) > 1 else axes[0], pairs)  273 us
    ppermute x107, starting transfers between devices, permute(): return lax.ppermute(values, axes if len(axes) > 1 else axes[0], pairs)  154 us
    pallas_call x2, Pallas kernels, mixer_backward(): pl.pallas_call(partial(mixer_grad_kernel, nb, len(w_in_out)), grid=(size...  61.9 us
    pallas_call x2, Pallas kernels, mixer_forward(): pl.pallas_call(partial(mixer_kernel, nb, len(w_in_out)), grid=(size // FT...  53.3 us
    pallas_call x2, Pallas kernels, glu_backward(): pl.pallas_call(partial(glu_grad_kernel, nb, len(down)), grid=(hidden // t...  20.4 us
    pallas_call x2, Pallas kernels, glu_forward(): pl.pallas_call(partial(glu_kernel, nb, len(down)), grid=(hidden // tile,)...  19.3 us
    unnamed x281, local copies, waits for them, and re-layouts  17 us
  transfers between devices with their start and end apart: 107, of which 38 were waited for; matrix products, arithmetic and copies ran while one was open for 9% of the time, Pallas kernels for 13%

profile of v2, /device:TPU:0, one launch (start us, length us, event | category | flops | bytes accessed | tf_op | source)
XLA Modules:
  0.0 680.6 jit_solution(1205647019474432086)
XLA Ops:
  38.7 6.0 collective-permute-start.8
  64.1 26.6 %mixer_forward.2 = (f32[176,768]{1,0:T(8,128)}, f32[176,768]{1,0:T(8,128)}, f32[176,768]{1,0:T(8,128)}, f32[176,768]{1,0:T(8,128)}, bf16[4,176,768]{2,1,0:T(8,12...) custom-call(s32[4]{0:T(128)} %pad_add_fusion.order, ...), custom_call_target="tpu_custom_call" | custom-call | flops 25999998976 | tf_op jit(solution)/shard_map/mixer_forward/pallas_call | solution.py:327
  91.8 34.6 %collective-permute-start.18 = (f32[176,768]{1,0:T(8,128)S(1)}, f32[176,768]{1,0:T(8,128)S(1)}, u32[]{:S(2)}, u32[]{:S(2)}) collective-permute-start(f32[176,768]{1,0:T(8,128)S(1)} %copy-done.93), channel_id=1, source_target_pairs={{0,4},{4,0},{1,5},{5,1},{2,6},{6,2},{3,7},{7,3},{8,12},{12,8},{9,1... | collective-permute-start | bytes 1622024 | tf_op jit(solution)/shard_map/ppermute | solution.py:41
  131.1 11.5 %collective-permute-done.19 = f32[176,768]{1,0:T(8,128)S(1)} collective-permute-done((f32[176,768]{1,0:T(8,128)S(1)}, f32[176,768]{1,0:T(8,128)S(1)}, u32[]{:S(2)}, u32[]{:S(2)}) %collective-permute-start.19) | collective-permute-done | bytes 540704 | tf_op jit(solution)/shard_map/ppermute | solution.py:41
  148.8 6.0 collective-permute-done.20.refs_1_
  159.5 10.6 %collective-permute-done.25.refs_7_.refs_9_ = bf16[384,768]{1,0:T(8,128)(2,1)S(1)} collective-permute-done((bf16[384,768]{1,0:T(8,128)(2,1)S(1)}, bf16[384,768]{1,0:T(8,128)(2,1)S(1)}, u32[]{:S(2)}, u32[]{:S(2)}) %collective-permute-start.25) | collective-permute-done | bytes 589856 | tf_op jit(solution)/shard_map/ppermute | solution.py:41
  171.1 9.6 %glu_forward.2 = (f32[176,768]{1,0:T(8,128)}, f32[176,768]{1,0:T(8,128)}, f32[176,768]{1,0:T(8,128)}, f32[176,768]{1,0:T(8,128)}, bf16[704,768]{1,0:T(8,128)(2,1...) custom-call(s32[2]{0:T(128)} %pad_add_fusion.1.places, bf16[176,768]{1,0:T(8,128)(2,1)} %copy-done.59, ...), custom_call_target="tpu_custom_call" | custom-call | flops 8999999488 | tf_op jit(solution)/shard_map/glu_forward/pallas_call | solution.py:610
  187.9 10.5 %collective-permute-done.28 = f32[176,768]{1,0:T(8,128)S(1)} collective-permute-done((f32[176,768]{1,0:T(8,128)S(1)}, f32[176,768]{1,0:T(8,128)S(1)}, u32[]{:S(2)}, u32[]{:S(2)}) %collective-permute-start.28) | collective-permute-done | bytes 540704 | tf_op jit(solution)/shard_map/ppermute | solution.py:41
  200.7 6.0 collective-permute-done.31.refs_1_
  206.7 6.8 %collective-permute-done.35.refs_7_ = f32[192,705]{1,0:T(8,128)S(1)} collective-permute-done((f32[192,705]{1,0:T(8,128)S(1)}, f32[192,705]{1,0:T(8,128)S(1)}, u32[]{:S(2)}, u32[]{:S(2)}) %collective-permute-start.35) | collective-permute-done | bytes 541472 | tf_op jit(solution)/shard_map/ppermute | solution.py:41
  214.9 26.6 %mixer_forward.3 = (f32[176,768]{1,0:T(8,128)}, f32[176,768]{1,0:T(8,128)}, f32[176,768]{1,0:T(8,128)}, f32[176,768]{1,0:T(8,128)}, bf16[4,176,768]{2,1,0:T(8,12...) custom-call(s32[4]{0:T(128)} %pad_add_fusion.order, ...), custom_call_target="tpu_custom_call" | custom-call | flops 25999998976 | tf_op jit(solution)/shard_map/mixer_forward/pallas_call | solution.py:327
  248.1 14.0 %collective-permute-done.40 = f32[176,768]{1,0:T(8,128)S(1)} collective-permute-done((f32[176,768]{1,0:T(8,128)S(1)}, f32[176,768]{1,0:T(8,128)S(1)}, u32[]{:S(2)}, u32[]{:S(2)}) %collective-permute-start.40) | collective-permute-done | bytes 540704 | tf_op jit(solution)/shard_map/ppermute | solution.py:41
  264.8 7.4 %collective-permute-done.41.refs_1_ = bf16[176,768]{1,0:T(8,128)(2,1)S(1)} collective-permute-done((bf16[176,768]{1,0:T(8,128)(2,1)S(1)}, bf16[176,768]{1,0:T(8,128)(2,1)S(1)}, u32[]{:S(2)}, u32[]{:S(2)}) %collective-permute-start.41) | collective-permute-done | bytes 270368 | tf_op jit(solution)/shard_map/ppermute | solution.py:41
  276.8 8.6 %collective-permute-done.44.refs_5_.refs_7_ = bf16[768,768]{1,0:T(8,128)(2,1)S(1)} collective-permute-done((bf16[768,768]{1,0:T(8,128)(2,1)S(1)}, bf16[768,768]{1,0:T(8,128)(2,1)S(1)}, u32[]{:S(2)}, u32[]{:S(2)}) %collective-permute-start.44) | collective-permute-done | bytes 1179680 | tf_op jit(solution)/shard_map/ppermute | solution.py:41
  287.2 9.8 %glu_forward.3 = (f32[176,768]{1,0:T(8,128)}, f32[176,768]{1,0:T(8,128)}, f32[176,768]{1,0:T(8,128)}, f32[176,768]{1,0:T(8,128)}, bf16[704,768]{1,0:T(8,128)(2,1...) custom-call(s32[2]{0:T(128)} %pad_add_fusion.1.places, bf16[176,768]{1,0:T(8,128)(2,1)} %copy-done.57, ...), custom_call_target="tpu_custom_call" | custom-call | flops 8999999488 | tf_op jit(solution)/shard_map/glu_forward/pallas_call | solution.py:610
  297.8 10.3 %glu_backward.2 = (f32[176,768]{1,0:T(8,128)}, f32[176,768]{1,0:T(8,128)}, f32[176,768]{1,0:T(8,128)}, f32[176,768]{1,0:T(8,128)}, bf16[704,768]{1,0:T(8,128)(2,...) custom-call(s32[2]{0:T(128)} %pad_add_fusion.1.places, bf16[176,768]{1,0:T(8,128)(2,1)} %bitcast.221, ...), custom_call_target="tpu_custom_call" | custom-call | flops 9500000256 | tf_op jit(solution)/shard_map/glu_backward/pallas_call | solution.py:679
  314.7 12.9 %collective-permute-done.48 = f32[176,768]{1,0:T(8,128)S(1)} collective-permute-done((f32[176,768]{1,0:T(8,128)S(1)}, f32[176,768]{1,0:T(8,128)S(1)}, u32[]{:S(2)}, u32[]{:S(2)}) %collective-permute-start.48) | collective-permute-done | bytes 540704 | tf_op jit(solution)/shard_map/ppermute | solution.py:41
  333.3 6.0 collective-permute-done.49.refs_1_
  341.6 31.0 %mixer_backward.2 = (f32[176,768]{1,0:T(8,128)}, f32[176,768]{1,0:T(8,128)}, f32[176,768]{1,0:T(8,128)}, f32[176,768]{1,0:T(8,128)}, bf16[4,176,768]{2,1,0:T(8,1...) custom-call(s32[4]{0:T(128)} %pad_add_fusion.order, ...), custom_call_target="tpu_custom_call" | custom-call | flops 30000001024 | tf_op jit(solution)/shard_map/mixer_backward/pallas_call | solution.py:495
  380.2 14.9 %collective-permute-done.55 = bf16[576,768]{1,0:T(8,128)(2,1)S(1)} collective-permute-done((bf16[576,768]{1,0:T(8,128)(2,1)S(1)}, bf16[576,768]{1,0:T(8,128)(2,1)S(1)}, u32[]{:S(2)}, u32[]{:S(2)}) %collective-permute-start.55) | collective-permute-done | bytes 884768 | tf_op jit(solution)/shard_map/ppermute | solution.py:41
  414.5 10.1 %glu_backward.3 = (f32[176,768]{1,0:T(8,128)}, f32[176,768]{1,0:T(8,128)}, f32[176,768]{1,0:T(8,128)}, f32[176,768]{1,0:T(8,128)}, bf16[704,768]{1,0:T(8,128)(2,...) custom-call(s32[2]{0:T(128)} %pad_add_fusion.1.places, bf16[176,768]{1,0:T(8,128)(2,1)} %copy-done.19, ...), custom_call_target="tpu_custom_call" | custom-call | flops 9500000256 | tf_op jit(solution)/shard_map/glu_backward/pallas_call | solution.py:679
  455.8 14.6 %collective-permute-done.69 = bf16[576,768]{1,0:T(8,128)(2,1)S(1)} collective-permute-done((bf16[576,768]{1,0:T(8,128)(2,1)S(1)}, bf16[576,768]{1,0:T(8,128)(2,1)S(1)}, u32[]{:S(2)}, u32[]{:S(2)}) %collective-permute-start.69) | collective-permute-done | bytes 884768 | tf_op jit(solution)/shard_map/ppermute | solution.py:41
  477.0 30.9 %mixer_backward.3 = (f32[176,768]{1,0:T(8,128)}, f32[176,768]{1,0:T(8,128)}, f32[176,768]{1,0:T(8,128)}, f32[176,768]{1,0:T(8,128)}, bf16[4,176,768]{2,1,0:T(8,1...) custom-call(s32[4]{0:T(128)} %pad_add_fusion.order, ...), custom_call_target="tpu_custom_call" | custom-call | flops 30000001024 | tf_op jit(solution)/shard_map/mixer_backward/pallas_call | solution.py:495
  518.2 18.2 %collective-permute-done.77 = bf16[576,768]{1,0:T(8,128)(2,1)S(1)} collective-permute-done((bf16[576,768]{1,0:T(8,128)(2,1)}, bf16[576,768]{1,0:T(8,128)(2,1)S(1)}, u32[]{:S(2)}, u32[]{:S(2)}) %collective-permute-start.77) | collective-permute-done | bytes 884768 | tf_op jit(solution)/shard_map/ppermute | solution.py:41
  541.2 13.0 %collective-permute-done.81 = bf16[576,768]{1,0:T(8,128)(2,1)S(1)} collective-permute-done((bf16[576,768]{1,0:T(8,128)(2,1)S(1)}, bf16[576,768]{1,0:T(8,128)(2,1)S(1)}, u32[]{:S(2)}, u32[]{:S(2)}) %collective-permute-start.81) | collective-permute-done | bytes 884768 | tf_op jit(solution)/shard_map/ppermute | solution.py:41
  568.7 18.0 %collective-permute-done.65 = bf16[1,176,768]{2,1,0:T(8,128)(2,1)S(1)} collective-permute-done((bf16[1,176,768]{2,1,0:T(8,128)(2,1)S(1)}, bf16[1,176,768]{2,1,0:T(8,128)(2,1)S(1)}, u32[]{:S(2)}, u32[]{:S(2)}) %collective-permute-start.65) | collective-permute-done | bytes 270368 | tf_op jit(solution)/shard_map/ppermute | solution.py:41
  592.6 29.3 %collective-permute-done.88 = f32[18,768]{1,0:T(8,128)S(1)} collective-permute-done((f32[18,768]{1,0:T(8,128)S(1)}, f32[18,768]{1,0:T(8,128)S(1)}, u32[]{:S(2)}, u32[]{:S(2)}) %collective-permute-start.88) | collective-permute-done | bytes 55328 | tf_op jit(solution)/shard_map/ppermute | solution.py:41
  622.8 10.7 %collective-permute-start.93 = (bf16[288,768]{1,0:T(8,128)(2,1)S(1)}, bf16[288,768]{1,0:T(8,128)(2,1)S(1)}, u32[]{:S(2)}, u32[]{:S(2)}) collective-permute-start(bf16[288,768]{1,0:T(8,128)(2,1)S(1)} %dynamic-slice_bitcast_fusion.11), channel_id=1, source_target_pairs={{0,4},{6,2},{1,5},{7,3},{8,12},{14,10},{9,13},{15,11},{16,20},{22,... | collective-permute-start | bytes 1327112 | tf_op jit(solution)/shard_map/ppermute | solution.py:41
  643.0 7.6 %collective-permute-done.100.refs_1_ = bf16[288,768]{1,0:T(8,128)(2,1)} collective-permute-done((bf16[288,768]{1,0:T(8,128)(2,1)S(1)}, bf16[288,768]{1,0:T(8,128)(2,1)}, u32[]{:S(2)}, u32[]{:S(2)}) %collective-permute-start.100) | collective-permute-done | bytes 442400 | tf_op jit(solution)/shard_map/ppermute | solution.py:41
  651.1 9.0 %collective-permute-done.103.refs_5_ = bf16[288,768]{1,0:T(8,128)(2,1)} collective-permute-done((bf16[288,768]{1,0:T(8,128)(2,1)S(1)}, bf16[288,768]{1,0:T(8,128)(2,1)}, u32[]{:S(2)}, u32[]{:S(2)}) %collective-permute-start.103) | collective-permute-done | bytes 442400 | tf_op jit(solution)/shard_map/ppermute | solution.py:41
  662.3 5.7 collective-permute-done.97.refs_1_
  670.2 5.6 assemble.2
  (624 shorter events, 234.8 us)
Async XLA Ops:
  15.9 22.8 %collective-permute-start.15 = (f32[2,704]{1,0:T(2,128)}, f32[2,704]{1,0:T(2,128)S(1)}, u32[]{:S(2)}, u32[]{:S(2)}) collective-permute-start(f32[2,704]{1,0:T(2,128)} %convert_element_type.267), channel_id=1, source_target_pairs={{0,4},{4,0},{1,5},{5,1},{2,6},{6,2},{3,7},{7,3},{8,12},{12,8},{9,1... | collective-permute-start | bytes 16904 | tf_op jit(solution)/shard_map/ppermute | solution.py:41
  60.2 30.5 %collective-permute-start.16 = (bf16[768,768]{1,0:T(8,128)(2,1)S(1)}, bf16[768,768]{1,0:T(8,128)(2,1)S(1)}, u32[]{:S(2)}, u32[]{:S(2)}) collective-permute-start(bf16[768,768]{1,0:T(8,128)(2,1)S(1)} %collective-permute-done.7), channel_id=1, source_target_pairs={{0,16},{16,0},{1,17},{17,1},{2,18},{18,2},{3,19},{19,3},{4,20},{20... | collective-permute-start | bytes 3538952 | tf_op jit(solution)/shard_map/ppermute | solution.py:41
  91.8 36.1 %collective-permute-start.18 = (f32[176,768]{1,0:T(8,128)S(1)}, f32[176,768]{1,0:T(8,128)S(1)}, u32[]{:S(2)}, u32[]{:S(2)}) collective-permute-start(f32[176,768]{1,0:T(8,128)S(1)} %copy-done.93), channel_id=1, source_target_pairs={{0,4},{4,0},{1,5},{5,1},{2,6},{6,2},{3,7},{7,3},{8,12},{12,8},{9,1... | collective-permute-start | bytes 1622024 | tf_op jit(solution)/shard_map/ppermute | solution.py:41
  129.6 28.8 %collective-permute-start.23 = (bf16[768,768]{1,0:T(8,128)(2,1)S(1)}, bf16[768,768]{1,0:T(8,128)(2,1)S(1)}, u32[]{:S(2)}, u32[]{:S(2)}) collective-permute-start(bf16[768,768]{1,0:T(8,128)(2,1)S(1)} %get-tuple-element.437.refs_4_.refs_6_), channel_id=1, source_target_pairs={{0,8},{8,0},{1,9},{9,1},{2,10},{10,2},{3,11},{11,3},{4,12},{12,4},... | collective-permute-start | bytes 3538952 | tf_op jit(solution)/shard_map/ppermute | solution.py:41
  145.1 25.0 %collective-permute-start.25 = (bf16[384,768]{1,0:T(8,128)(2,1)S(1)}, bf16[384,768]{1,0:T(8,128)(2,1)S(1)}, u32[]{:S(2)}, u32[]{:S(2)}) collective-permute-start(bf16[384,768]{1,0:T(8,128)(2,1)S(1)} %get-tuple-element.445.refs_6_.refs_8_), channel_id=1, source_target_pairs={{0,8},{8,0},{1,9},{9,1},{2,10},{10,2},{3,11},{11,3},{4,12},{12,4},... | collective-permute-start | bytes 1769480 | tf_op jit(solution)/shard_map/ppermute | solution.py:41
  185.8 27.8 %collective-permute-start.34 = (bf16[384,768]{1,0:T(8,128)(2,1)S(1)}, bf16[384,768]{1,0:T(8,128)(2,1)S(1)}, u32[]{:S(2)}, u32[]{:S(2)}) collective-permute-start(bf16[384,768]{1,0:T(8,128)(2,1)S(1)} %copy-done.32), channel_id=1, source_target_pairs={{0,8},{8,0},{1,9},{9,1},{2,10},{10,2},{3,11},{11,3},{4,12},{12,4},... | collective-permute-start | bytes 1769480 | tf_op jit(solution)/shard_map/ppermute | solution.py:41
  187.3 26.2 %collective-permute-start.35 = (f32[192,705]{1,0:T(8,128)S(1)}, f32[192,705]{1,0:T(8,128)S(1)}, u32[]{:S(2)}, u32[]{:S(2)}) collective-permute-start(f32[192,705]{1,0:T(8,128)S(1)} %copy-done.31), channel_id=1, source_target_pairs={{0,8},{8,0},{1,9},{9,1},{2,10},{10,2},{3,11},{11,3},{4,12},{12,4},... | collective-permute-start | bytes 1624328 | tf_op jit(solution)/shard_map/ppermute | solution.py:41
  246.0 30.3 %collective-permute-start.45 = (bf16[384,768]{1,0:T(8,128)(2,1)S(1)}, bf16[384,768]{1,0:T(8,128)(2,1)S(1)}, u32[]{:S(2)}, u32[]{:S(2)}) collective-permute-start(bf16[384,768]{1,0:T(8,128)(2,1)S(1)} %get-tuple-element.223.refs_6_.refs_8_), channel_id=1, source_target_pairs={{0,8},{8,0},{1,9},{9,1},{2,10},{10,2},{3,11},{11,3},{4,12},{12,4},... | collective-permute-start | bytes 1769480 | tf_op jit(solution)/shard_map/ppermute | solution.py:41
  247.6 37.8 %collective-permute-start.44 = (bf16[768,768]{1,0:T(8,128)(2,1)S(1)}, bf16[768,768]{1,0:T(8,128)(2,1)S(1)}, u32[]{:S(2)}, u32[]{:S(2)}) collective-permute-start(bf16[768,768]{1,0:T(8,128)(2,1)S(1)} %get-tuple-element.222.refs_4_.refs_6_), channel_id=1, source_target_pairs={{0,8},{8,0},{1,9},{9,1},{2,10},{10,2},{3,11},{11,3},{4,12},{12,4},... | collective-permute-start | bytes 3538952 | tf_op jit(solution)/shard_map/ppermute | solution.py:41
  376.1 34.1 %collective-permute-start.61 = (f32[176,768]{1,0:T(8,128)S(1)}, f32[176,768]{1,0:T(8,128)S(1)}, u32[]{:S(2)}, u32[]{:S(2)}) collective-permute-start(f32[176,768]{1,0:T(8,128)S(1)} %copy-done.91), channel_id=1, source_target_pairs={{0,4},{4,0},{1,5},{5,1},{2,6},{6,2},{3,7},{7,3},{8,12},{12,8},{9,1... | collective-permute-start | bytes 1622024 | tf_op jit(solution)/shard_map/ppermute | solution.py:41
  376.2 34.9 %collective-permute-start.62 = (f32[176,768]{1,0:T(8,128)S(1)}, f32[176,768]{1,0:T(8,128)S(1)}, u32[]{:S(2)}, u32[]{:S(2)}) collective-permute-start(f32[176,768]{1,0:T(8,128)S(1)} %copy-done.90), channel_id=1, source_target_pairs={{0,4},{4,0},{1,5},{5,1},{2,6},{6,2},{3,7},{7,3},{8,12},{12,8},{9,1... | collective-permute-start | bytes 1622024 | tf_op jit(solution)/shard_map/ppermute | solution.py:41
  408.7 21.8 %collective-permute-start.76 = (bf16[576,768]{1,0:T(8,128)(2,1)}, bf16[576,768]{1,0:T(8,128)(2,1)}, u32[]{:S(2)}, u32[]{:S(2)}) collective-permute-start(bf16[576,768]{1,0:T(8,128)(2,1)} %dynamic-slice_bitcast_fusion.2), channel_id=1, source_target_pairs={{0,8},{8,0},{1,9},{9,1},{2,10},{10,2},{3,11},{11,3},{4,12},{12,4},... | collective-permute-start | bytes 2654216 | tf_op jit(solution)/shard_map/ppermute | solution.py:41
  412.0 22.4 %collective-permute-start.63 = (f32[176,768]{1,0:T(8,128)}, f32[176,768]{1,0:T(8,128)}, u32[]{:S(2)}, u32[]{:S(2)}) collective-permute-start(f32[176,768]{1,0:T(8,128)} %add.356), channel_id=1, source_target_pairs={{0,1},{1,0},{2,3},{3,2},{4,5},{5,4},{6,7},{7,6},{8,9},{9,8},{10,11... | collective-permute-start | bytes 1622024 | tf_op jit(solution)/shard_map/ppermute | solution.py:41
  425.8 115.4 %collective-permute-start.82 = (bf16[576,768]{1,0:T(8,128)(2,1)}, bf16[576,768]{1,0:T(8,128)(2,1)}, u32[]{:S(2)}, u32[]{:S(2)}) collective-permute-start(bf16[576,768]{1,0:T(8,128)(2,1)} %get-tuple-element.406), channel_id=1, source_target_pairs={{0,16},{1,17},{2,18},{3,19},{4,20},{5,21},{6,22},{7,23},{8,24},{9,... | collective-permute-start | bytes 2654216 | tf_op jit(solution)/shard_map/ppermute | solution.py:41
  430.6 44.0 %collective-permute-start.67 = (bf16[576,768]{1,0:T(8,128)(2,1)}, bf16[576,768]{1,0:T(8,128)(2,1)S(1)}, u32[]{:S(2)}, u32[]{:S(2)}) collective-permute-start(bf16[576,768]{1,0:T(8,128)(2,1)} %get-tuple-element.438), channel_id=1, source_target_pairs={{0,8},{8,0},{1,9},{9,1},{2,10},{10,2},{3,11},{11,3},{4,12},{12,4},... | collective-permute-start | bytes 2654216 | tf_op jit(solution)/shard_map/ppermute | solution.py:41
  434.4 82.4 %collective-permute-start.78 = (bf16[576,768]{1,0:T(8,128)(2,1)}, bf16[576,768]{1,0:T(8,128)(2,1)}, u32[]{:S(2)}, u32[]{:S(2)}) collective-permute-start(bf16[576,768]{1,0:T(8,128)(2,1)} %fusion), channel_id=1, source_target_pairs={{0,16},{1,17},{2,18},{3,19},{4,20},{5,21},{6,22},{7,23},{8,24},{9,... | collective-permute-start | bytes 2654216 | tf_op jit(solution)/shard_map/ppermute | solution.py:41
  446.7 23.7 %collective-permute-start.69 = (bf16[576,768]{1,0:T(8,128)(2,1)S(1)}, bf16[576,768]{1,0:T(8,128)(2,1)S(1)}, u32[]{:S(2)}, u32[]{:S(2)}) collective-permute-start(bf16[576,768]{1,0:T(8,128)(2,1)S(1)} %dynamic-slice_bitcast_fusion.4), channel_id=1, source_target_pairs={{0,8},{8,0},{1,9},{9,1},{2,10},{10,2},{3,11},{11,3},{4,12},{12,4},... | collective-permute-start | bytes 2654216 | tf_op jit(solution)/shard_map/ppermute | solution.py:41
  474.6 34.1 %collective-permute-start.72 = (bf16[576,768]{1,0:T(8,128)(2,1)}, bf16[576,768]{1,0:T(8,128)(2,1)S(1)}, u32[]{:S(2)}, u32[]{:S(2)}) collective-permute-start(bf16[576,768]{1,0:T(8,128)(2,1)} %get-tuple-element.440), channel_id=1, source_target_pairs={{0,8},{8,0},{1,9},{9,1},{2,10},{10,2},{3,11},{11,3},{4,12},{12,4},... | collective-permute-start | bytes 2654216 | tf_op jit(solution)/shard_map/ppermute | solution.py:41
  508.8 78.7 %collective-permute-start.90 = (bf16[576,768]{1,0:T(8,128)(2,1)S(1)}, bf16[576,768]{1,0:T(8,128)(2,1)S(1)}, u32[]{:S(2)}, u32[]{:S(2)}) collective-permute-start(bf16[576,768]{1,0:T(8,128)(2,1)S(1)} %fusion.32), channel_id=1, source_target_pairs={{0,16},{1,17},{2,18},{3,19},{4,20},{5,21},{6,22},{7,23},{8,24},{9,... | collective-permute-start | bytes 2654216 | tf_op jit(solution)/shard_map/ppermute | solution.py:41
  511.7 24.8 %collective-permute-start.77 = (bf16[576,768]{1,0:T(8,128)(2,1)}, bf16[576,768]{1,0:T(8,128)(2,1)S(1)}, u32[]{:S(2)}, u32[]{:S(2)}) collective-permute-start(bf16[576,768]{1,0:T(8,128)(2,1)} %get-tuple-element.414), channel_id=1, source_target_pairs={{16,0},{17,1},{18,2},{19,3},{20,4},{21,5},{22,6},{23,7},{24,8},{25... | collective-permute-start | bytes 2654216 | tf_op jit(solution)/shard_map/ppermute | solution.py:41
  513.2 25.5 %collective-permute-start.75 = (f32[176,768]{1,0:T(8,128)S(1)}, f32[176,768]{1,0:T(8,128)S(1)}, u32[]{:S(2)}, u32[]{:S(2)}) collective-permute-start(f32[176,768]{1,0:T(8,128)S(1)} %add.365), channel_id=1, source_target_pairs={{0,1},{1,0},{2,3},{3,2},{4,5},{5,4},{6,7},{7,6},{8,9},{9,8},{10,11... | collective-permute-start | bytes 1622024 | tf_op jit(solution)/shard_map/ppermute | solution.py:41
  516.8 37.4 %collective-permute-start.81 = (bf16[576,768]{1,0:T(8,128)(2,1)S(1)}, bf16[576,768]{1,0:T(8,128)(2,1)S(1)}, u32[]{:S(2)}, u32[]{:S(2)}) collective-permute-start(bf16[576,768]{1,0:T(8,128)(2,1)S(1)} %fusion.33), channel_id=1, source_target_pairs={{16,0},{17,1},{18,2},{19,3},{20,4},{21,5},{22,6},{23,7},{24,8},{25... | collective-permute-start | bytes 2654216 | tf_op jit(solution)/shard_map/ppermute | solution.py:41
  536.4 22.9 %collective-permute-start.80 = (bf16[576,768]{1,0:T(8,128)(2,1)S(1)}, bf16[576,768]{1,0:T(8,128)(2,1)S(1)}, u32[]{:S(2)}, u32[]{:S(2)}) collective-permute-start(bf16[576,768]{1,0:T(8,128)(2,1)S(1)} %get-tuple-element.442), channel_id=1, source_target_pairs={{0,8},{8,0},{1,9},{9,1},{2,10},{10,2},{3,11},{11,3},{4,12},{12,4},... | collective-permute-start | bytes 2654216 | tf_op jit(solution)/shard_map/ppermute | solution.py:41
  538.8 25.4 %collective-permute-start.84 = (bf16[576,768]{1,0:T(8,128)(2,1)S(1)}, bf16[576,768]{1,0:T(8,128)(2,1)S(1)}, u32[]{:S(2)}, u32[]{:S(2)}) collective-permute-start(bf16[576,768]{1,0:T(8,128)(2,1)S(1)} %get-tuple-element.412), channel_id=1, source_target_pairs={{2,0},{4,6},{3,1},{5,7},{10,8},{12,14},{11,9},{13,15},{18,16},{20,... | collective-permute-start | bytes 2654216 | tf_op jit(solution)/shard_map/ppermute | solution.py:41
  559.5 31.0 %collective-permute-start.89 = (bf16[576,768]{1,0:T(8,128)(2,1)S(1)}, bf16[576,768]{1,0:T(8,128)(2,1)S(1)}, u32[]{:S(2)}, u32[]{:S(2)}) collective-permute-start(bf16[576,768]{1,0:T(8,128)(2,1)S(1)} %fusion.34), channel_id=1, source_target_pairs={{16,0},{17,1},{18,2},{19,3},{20,4},{21,5},{22,6},{23,7},{24,8},{25... | collective-permute-start | bytes 2654216 | tf_op jit(solution)/shard_map/ppermute | solution.py:41
  567.3 54.6 %collective-permute-start.92 = (bf16[576,768]{1,0:T(8,128)(2,1)S(1)}, bf16[576,768]{1,0:T(8,128)(2,1)S(1)}, u32[]{:S(2)}, u32[]{:S(2)}) collective-permute-start(bf16[576,768]{1,0:T(8,128)(2,1)S(1)} %get-tuple-element.404), channel_id=1, source_target_pairs={{2,0},{4,6},{3,1},{5,7},{10,8},{12,14},{11,9},{13,15},{18,16},{20,... | collective-permute-start | bytes 2654216 | tf_op jit(solution)/shard_map/ppermute | solution.py:41
  586.7 53.5 %collective-permute-start.86 = (bf16[1,176,768]{2,1,0:T(8,128)(2,1)S(1)}, bf16[1,176,768]{2,1,0:T(8,128)(2,1)S(1)}, u32[]{:S(2)}, u32[]{:S(2)}) collective-permute-start(bf16[1,176,768]{2,1,0:T(8,128)(2,1)S(1)} %select_bitcast_fusion.3), channel_id=1, source_target_pairs={{0,0},{2,4},{4,2},{6,6},{1,1},{3,5},{5,3},{7,7},{8,8},{10,12},{12,... | collective-permute-start | bytes 811016 | tf_op jit(solution)/shard_map/ppermute | solution.py:41
  587.4 52.9 %collective-permute-start.87 = (bf16[1,176,768]{2,1,0:T(8,128)(2,1)S(1)}, bf16[1,176,768]{2,1,0:T(8,128)(2,1)S(1)}, u32[]{:S(2)}, u32[]{:S(2)}) collective-permute-start(bf16[1,176,768]{2,1,0:T(8,128)(2,1)S(1)} %get-tuple-element.408), channel_id=1, source_target_pairs={{0,16},{2,20},{4,18},{6,22},{16,0},{18,4},{20,2},{22,6},{1,17},{3,... | collective-permute-start | bytes 811016 | tf_op jit(solution)/shard_map/ppermute | solution.py:41
  587.5 34.4 %collective-permute-start.88 = (f32[18,768]{1,0:T(8,128)S(1)}, f32[18,768]{1,0:T(8,128)S(1)}, u32[]{:S(2)}, u32[]{:S(2)}) collective-permute-start(f32[18,768]{1,0:T(8,128)S(1)} %add.376), channel_id=1, source_target_pairs={{0,2},{2,0},{1,3},{3,1},{4,6},{6,4},{5,7},{7,5},{8,10},{10,8},{9,1... | collective-permute-start | bytes 165896 | tf_op jit(solution)/shard_map/ppermute | solution.py:41
  591.2 42.3 %collective-permute-start.95 = (bf16[576,768]{1,0:T(8,128)(2,1)S(1)}, bf16[576,768]{1,0:T(8,128)(2,1)S(1)}, u32[]{:S(2)}, u32[]{:S(2)}) collective-permute-start(bf16[576,768]{1,0:T(8,128)(2,1)S(1)} %get-tuple-element.402), channel_id=1, source_target_pairs={{2,0},{4,6},{3,1},{5,7},{10,8},{12,14},{11,9},{13,15},{18,16},{20,... | collective-permute-start | bytes 2654216 | tf_op jit(solution)/shard_map/ppermute | solution.py:41
  621.9 39.8 %collective-permute-start.101 = (bf16[288,768]{1,0:T(8,128)(2,1)S(1)}, bf16[288,768]{1,0:T(8,128)(2,1)S(1)}, u32[]{:S(2)}, u32[]{:S(2)}) collective-permute-start(bf16[288,768]{1,0:T(8,128)(2,1)S(1)} %bitcast_select_fusion.2.refs_0_), channel_id=1, source_target_pairs={{0,4},{4,0},{1,5},{5,1},{2,6},{6,2},{3,7},{7,3},{8,12},{12,8},{9,1... | collective-permute-start | bytes 1327112 | tf_op jit(solution)/shard_map/ppermute | solution.py:41
  640.3 27.6 %collective-permute-start.97 = (bf16[288,768]{1,0:T(8,128)(2,1)S(1)}, bf16[288,768]{1,0:T(8,128)(2,1)}, u32[]{:S(2)}, u32[]{:S(2)}) collective-permute-start(bf16[288,768]{1,0:T(8,128)(2,1)S(1)} %bitcast_select_fusion.refs_0_), channel_id=1, source_target_pairs={{0,8},{8,0},{1,9},{9,1},{2,10},{10,2},{3,11},{11,3},{4,12},{12,4},... | collective-permute-start | bytes 1327112 | tf_op jit(solution)/shard_map/ppermute | solution.py:41
  (214 other events, 2592.0 us)

commit v3 on v2

--- a/solution.py
+++ b/solution.py
@@ -15,7 +15,7 @@
 FTILE = 256
 HTILE = 384
 PEAK = 1.0e9
-VMEM_LIMIT = 56 * 1024 * 1024
+MIB = 1024 * 1024
 
 ALL_AXES = ("section", "dq", "core", "th", "tl")
 
@@ -94,6 +94,10 @@
 
 def after(values, *events):
     return lax.optimization_barrier((values, events))[0]
+
+
+def tie(*values):
+    return lax.optimization_barrier(values)
 
 
 class Line:
@@ -357,7 +361,7 @@
             pltpu.VMEM((pack_len, width), f32),
         ]
         + part_scratch(w_in_out, spectra),
-        compiler_params=pltpu.CompilerParams(vmem_limit_bytes=VMEM_LIMIT),
+        compiler_params=pltpu.CompilerParams(vmem_limit_bytes=36 * MIB),
         cost_estimate=pl.CostEstimate(flops=int(26 * PEAK), bytes_accessed=0, transcendentals=0),
         name="mixer_forward",
     )(order, places, *blocks, *w_in_out, *spectra, taps, cols, *tables, *tables)
@@ -529,7 +533,7 @@
             pltpu.VMEM((pack_len, 3 * width), f32),
         ]
         + part_scratch(w_in_out, spectra),
-        compiler_params=pltpu.CompilerParams(vmem_limit_bytes=VMEM_LIMIT),
+        compiler_params=pltpu.CompilerParams(vmem_limit_bytes=37 * MIB),
         cost_estimate=pl.CostEstimate(flops=int(30 * PEAK), bytes_accessed=0, transcendentals=0),
         name="mixer_backward",
     )(
@@ -620,7 +624,7 @@
             jax.ShapeDtypeStruct((length, hidden), low),
         ],
         scratch_shapes=[pltpu.VMEM((length, model), f32)] + glu_scratch(gate_up, down, tile),
-        compiler_params=pltpu.CompilerParams(vmem_limit_bytes=VMEM_LIMIT),
+        compiler_params=pltpu.CompilerParams(vmem_limit_bytes=28 * MIB),
         cost_estimate=pl.CostEstimate(flops=int(9 * PEAK), bytes_accessed=0, transcendentals=0),
         name="glu_forward",
     )(places, *blocks, *gate_up, *down)
@@ -688,7 +692,7 @@
             jax.ShapeDtypeStruct((length, hidden), low),
         ],
         scratch_shapes=[pltpu.VMEM((length, model), f32)] + glu_scratch(gate_up, down, tile),
-        compiler_params=pltpu.CompilerParams(vmem_limit_bytes=VMEM_LIMIT),
+        compiler_params=pltpu.CompilerParams(vmem_limit_bytes=28 * MIB),
         cost_estimate=pl.CostEstimate(flops=int(9.5 * PEAK), bytes_accessed=0, transcendentals=0),
         name="glu_backward",
     )(places, *blocks, gate, up, *gate_up, *down)
@@ -740,59 +744,64 @@
     return permute(low(total), ("core", "th"), lambda c, h: (c, 1 - h) if c != h else None)
 
 
-def quarters(total, other):
-    core, high_part = lax.axis_index("core"), lax.axis_index("th")
-    total = low(total + other.astype(jnp.float32))
-    halves = total.reshape(2, total.shape[0] // 2, total.shape[1])
-    got = permute(halves[1 - core], ("core", "th"), lambda c, h: (1 - c, h) if c == h else None)
-    quarter = jnp.where(core == high_part, halves[core], got)
+def holder_total(total, other):
+    return low(total + other.astype(jnp.float32))
+
+
+def from_holder(values):
+    return permute(values, ("core", "th"), lambda c, h: (1 - c, h) if c == h else None)
+
+
+def join_holders(total):
     peers = lax.axis_size("dq")
-    joined = [quarter] + [shift(quarter, "dq", k) for k in range(1, peers)]
-    return joined + [swap_core(block) for block in joined]
-
-
-def quarter_places():
-    core, dq, peers = lax.axis_index("core"), lax.axis_index("dq"), lax.axis_size("dq")
-    return jnp.stack(
-        [
-            (dq - k) % peers * 2 + jnp.bitwise_xor(core, c)
-            for c in range(2)
-            for k in range(peers)
-        ]
-    ).astype(jnp.int32)
+    held = [total]
+    for k in range(1, peers):
+        held.append(
+            permute(
+                total,
+                ("dq", "core", "th"),
+                lambda d, c, h: ((d + k) % peers, c, h) if c == h else None,
+            )
+        )
+    return held, [from_holder(part) for part in held]
 
 
 def assemble_kernel(counts, finish, places, *refs):
     taken = 0
-    n_out = len(refs) - sum(counts) - len(counts)
-    outs = refs[sum(counts) : sum(counts) + n_out]
-    joined = refs[sum(counts) + n_out :]
+    n_in = 2 * sum(counts)
+    n_out = len(refs) - n_in - len(counts)
+    outs = refs[n_in : n_in + n_out]
+    joined = refs[n_in + n_out :]
+    holds = places[len(places) - 1] == 1
     for buffer, nb in zip(joined, counts):
         for j in range(nb):
-            block = refs[taken + j]
-            rows = block.shape[0]
+            held, given = refs[taken + j], refs[taken + nb + j]
+            rows = held.shape[0]
             at = pl.ds(pl.multiple_of(places[j] * rows, 8), rows)
-            buffer[at, :] = block[...].astype(jnp.float32)
-        taken += nb
+            buffer[at, :] = jnp.where(
+                holds, held[...].astype(jnp.float32), given[...].astype(jnp.float32)
+            )
+        taken += 2 * nb
     finish(joined, outs)
 
 
-def assemble(messages, finish, out_shapes):
-    counts = [len(blocks) for blocks in messages]
+def assemble(messages, places, finish, out_shapes):
+    counts = [len(held) for held, given in messages]
     vmem = pl.BlockSpec(memory_space=pltpu.VMEM)
+    holds = (lax.axis_index("core") == lax.axis_index("th")).astype(jnp.int32)
     return pl.pallas_call(
         partial(assemble_kernel, counts, finish),
-        in_specs=[pl.BlockSpec(memory_space=pltpu.SMEM)] + [vmem] * sum(counts),
+        in_specs=[SMEM] + [vmem] * (2 * sum(counts)),
         out_specs=[vmem] * len(out_shapes),
         out_shape=[jax.ShapeDtypeStruct(s, jnp.float32) for s in out_shapes],
         scratch_shapes=[
-            pltpu.VMEM((len(blocks) * blocks[0].shape[0], blocks[0].shape[1]), jnp.float32)
-            for blocks in messages
+            pltpu.VMEM((len(held) * held[0].shape[0], held[0].shape[1]), jnp.float32)
+            for held, given in messages
         ],
-        compiler_params=pltpu.CompilerParams(vmem_limit_bytes=VMEM_LIMIT),
+        compiler_params=pltpu.CompilerParams(vmem_limit_bytes=40 * MIB),
         cost_estimate=pl.CostEstimate(flops=int(4 * PEAK), bytes_accessed=0, transcendentals=0),
         name="assemble",
-    )(quarter_places(), *[block for blocks in messages for block in blocks])
+    )(jnp.append(places, holds), *[p for held, given in messages for p in held + given])
 
 
 def pack(arrays):
@@ -858,8 +867,9 @@
         w_gate_up[0], (dq * per % width, dq * 2 // dqs, 0), (per, 1, hidden_cols)
     ).reshape(per, hidden_cols)
     dn_own = own_part(w_down[0])
-    rows_in = after(transposed(own_slots(tokens)), gu_own, dn_own)
-    first_wave = (transposed(io_own), transposed(sp_own))
+    rows_in, io_part, sp_part, gu_own, dn_own = tie(
+        transposed(own_slots(tokens)), transposed(io_own), transposed(sp_own), gu_own, dn_own
+    )
     swapped = permute(segment_ids.astype(jnp.float32), ("core",), lambda c: (1 - c,))
     ids_both = jnp.stack([segment_ids, swapped.astype(jnp.int32)])
     segments = own_slots(ids_both[jnp.bitwise_xor(core, high_part)])
@@ -905,33 +915,40 @@
             normed, norm_pull = jax.vjp(layer_norm, state, gains[layer, 0])
             blocks = gather_rows(low(normed))
             if opening:
-                line.mark(blocks)
-                io_part, sp_part = line.take(first_wave)
                 io_other, sp_other = swap_section(io_part), swap_section(sp_part)
-                held = after((gu_own, dn_own), io_part, sp_part)
-                gu_moved, dn_moved = transposed(held[0]), transposed(held[1])
+                dn_moved = transposed(dn_own)
+                gu_moved = transposed(gu_own)
+                blocks, io_other, sp_other = tie(blocks, io_other, sp_other)
                 sp_both = by_layer(sp_part, sp_other)
                 spectra[0] = join_parts(sp_both[0])
                 io_both = by_layer(io_part, io_other)
                 w_io[0] = join_parts(io_both[0])
                 line.mark(io_both[0], sp_both[0])
-                gu_part, dn_part = line.take((gu_moved, dn_moved))
-                gu_other, dn_other = swap_section(gu_part), swap_section(dn_part)
-                blocks = after(blocks, gu_part, dn_part)
+                dn_part = line.take(dn_moved)
+                dn_other = swap_section(dn_part)
+                line.mark(dn_part)
+                gu_part = line.take(gu_moved)
+                dn_both = by_layer(dn_part, after(dn_other, gu_part))
+                blocks, gu_part, dn_first, cot_own = tie(blocks, gu_part, dn_both[0], own_slots(cotangent))
+                cot_in = transposed(cot_own)
+                gu_other = swap_section(gu_part)
+                down[0] = join_parts(dn_first)
             parts, gathered, mix, kept = mixer_forward(
                 blocks, w_io[layer], taps[layer : layer + 1], cols[index], spectra[layer], tables,
                 order, places,
             )
             if opening:
                 gu_both = by_layer(gu_part, after(gu_other, parts))
-                parts = after(parts, gu_both[0])
+                parts, gu_first, cot_in = tie(parts, gu_both[0], cot_in)
+            if layer == 1:
+                parts, cot_chip = tie(parts, cot_chip)
+            if index == 0 and layer == 1:
+                parts, gate_up[1], down[1] = tie(parts, gate_up[1], down[1])
             sums_of = core_sums(parts)
             if opening:
-                gate_up[0] = join_parts(gu_both[0])
-                dn_both = by_layer(dn_part, after(dn_other, sums_of))
-                down[0] = join_parts(dn_both[0])
+                gate_up[0] = join_parts(gu_first)
             if layer == 1:
-                cot_blocks = both_cores(after(cot_chip, sums_of))
+                cot_blocks = both_cores(cot_chip)
             hidden = state + chip_sums(sums_of)
             normed_two, norm_pull_two = jax.vjp(layer_norm, hidden, gains[layer, 1])
             blocks = gather_rows(low(normed_two))
@@ -951,8 +968,8 @@
                     gu_part, dn_part = after((gu_both[1], dn_both[1]), sums_of)
                     gate_up[1] = join_parts(gu_part)
                     down[1] = join_parts(dn_part)
-                    cot_in = transposed(own_slots(after(cotangent, sums_of)))
-                state = hidden + chip_sums(sums_of)
+                moved_sums = sent_sums(sums_of)
+                state = hidden + add_sums(sums_of, moved_sums)
                 results[0].append(state)
                 cot_chip = chip_blocks(after(cot_in[index], state))
             else:
@@ -1006,17 +1023,31 @@
     moved = [{}, {}]
     crossed = [{}, {}]
 
-    def send_dq(layer, *messages):
-        for m in messages:
-            arrays = pack([sums[layer][name] for name in contents[m]])
+    def send_dq(layer, m, *events):
+            arrays = pack(after([sums[layer][name] for name in contents[m]], *events))
             sent = [exchange_dq(a) for a in arrays]
             own[layer][m] = [s[0] for s in sent]
             moved[layer][m] = [s[1] for s in sent]
 
-    def send_section(layer, m, *events):
+    def add_own(layer, m, *events):
         terms = after(moved[layer][m], *events)
         own[layer][m] = [total_dq(o, t) for o, t in zip(own[layer][m], terms)]
+
+    def cross(layer, m):
         crossed[layer][m] = [to_section(o, layer) for o in own[layer][m]]
+
+    total = {}
+    held = {}
+
+    def add_total(m, *events):
+        terms = after((crossed[0][m], crossed[1][m]), *events)
+        total[m] = [
+            jnp.where(first, o, p) + jnp.where(first, t, u).astype(jnp.float32)
+            for o, p, t, u in zip(own[0][m], own[1][m], *terms)
+        ]
+
+    def hold(m):
+        held[m] = [to_holder(t) for t in total[m]]
 
     small_sum = [None, None]
     gain_sum = [None, None]
@@ -1031,61 +1062,83 @@
         )
         sums_of = core_sums(parts)
         glu_terms(1, kept, sums_of, grad_rows, gate_grad, up_grad, last)
-        if last:
-            send_dq(1, 0, 1)
         grad_part, gain_two = kept[4](chip_sums(sums_of))
         hidden_grad = state + grad_part
+        if last:
+            send_dq(1, 0)
+            send_dq(1, 1, hidden_grad)
         blocks = gather_rows(low(hidden_grad))
-        late_sums = core_sums(after(late_parts, blocks))
+        late_sums = core_sums(after(late_parts, hidden_grad))
+        blocks, late_sums = tie(blocks, late_sums)
+        late_moved = sent_sums(late_sums)
         parts, mix_rows, proj_grad, spectrum_grad, tap_grad = mixer_backward(
             blocks, w_io[1], taps[1:2], cols[index], kept[3], spectra[1], tables, order, places
         )
+        parts, late_moved = tie(parts, late_moved)
+        if last:
+            parts, moved[1][0], moved[1][1] = tie(parts, moved[1][0], moved[1][1])
         sums_of = core_sums(parts)
-        mix_terms(1, kept, sums_of, mix_rows, proj_grad, spectrum_grad, last)
+        results[1].append(late_hidden + add_sums(late_sums, after(late_moved, sums_of)))
         moved_sums = sent_sums(sums_of)
-        late_moved = sent_sums(after(late_sums, sums_of))
         if last:
-            send_section(1, 0, sums_of)
-            send_section(1, 1, sums_of)
-            send_dq(1, 2)
-            moved_sums = after(moved_sums, own[1][1], own[1][2])
+            add_own(1, 0, sums_of)
+            add_own(1, 1, sums_of)
+            moved_sums, own[1][0], own[1][1], results[1][-1] = tie(
+                moved_sums, own[1][0], own[1][1], results[1][-1]
+            )
+            cross(1, 0)
+            cross(1, 1)
+            out_sent = deliver(low(jnp.stack(results[0])), low(jnp.stack(results[1])))
         grad_part, gain_one = kept[0](add_sums(sums_of, moved_sums))
         state = hidden_grad + grad_part
         small_sum[1] = add(small_sum[1], tap_grad)
         gain_sum[1] = add(gain_sum[1], jnp.stack([gain_one, gain_two]))
         grads_in[1].append(state)
+        mix_terms(1, kept, state, mix_rows, proj_grad, spectrum_grad, last)
+        if last:
+            send_dq(1, 2)
         kept = saved[0][index]
         blocks = gather_rows(low(state))
-        results[1].append(late_hidden + add_sums(late_sums, after(late_moved, blocks)))
+        if last:
+            blocks, own[1][2] = tie(blocks, own[1][2])
         parts, (grad_rows, gate_grad, up_grad) = glu_backward(
             blocks, kept[6], kept[7], gate_up[0], down[0], places
         )
+        if last:
+            parts, out_sent = tie(parts, out_sent)
         sums_of = core_sums(parts)
         glu_terms(0, kept, sums_of, grad_rows, gate_grad, up_grad, last)
         moved_sums = sent_sums(sums_of)
         if last:
-            send_dq(0, 0, 1)
-            out_sent = deliver(
-                low(after(jnp.stack(results[0]), sums_of)), low(after(jnp.stack(results[1]), sums_of))
-            )
-            moved_sums = after(moved_sums, own[0][1])
-            send_section(1, 2, moved_sums)
-            moved_sums = after(moved_sums, own[1][2])
+            send_dq(0, 0)
+            layer_out = ordered(*after(out_sent, sums_of))
+            moved_sums, own[0][0], layer_out = tie(moved_sums, own[0][0], layer_out)
         grad_part, gain_two = kept[4](add_sums(sums_of, moved_sums))
         hidden_grad = state + grad_part
-        chip = chip_blocks(low(hidden_grad))
+        blocks = gather_rows(low(hidden_grad))
         if last:
-            send_section(0, 0, hidden_grad)
-            chip = after(chip, own[0][0])
-        blocks = both_cores(chip)
-        if last:
-            send_section(0, 1, blocks)
-            blocks = after(blocks, own[0][1])
+            send_dq(0, 1, hidden_grad)
+            add_own(1, 2, blocks)
+            blocks, own[0][1], own[1][2] = tie(blocks, own[0][1], own[1][2])
+            cross(1, 2)
         parts, mix_rows, proj_grad, spectrum_grad, tap_grad = mixer_backward(
             blocks, w_io[0], taps[0:1], cols[index], kept[3], spectra[0], tables, order, places
         )
+        if last:
+            parts, moved[0][0], moved[0][1], crossed[1][2] = tie(
+                parts, moved[0][0], moved[0][1], crossed[1][2]
+            )
+            add_own(0, 0, parts)
+            parts, own[0][0] = tie(parts, own[0][0])
+            cross(0, 0)
+            mix_terms(0, kept, parts, mix_rows, proj_grad, spectrum_grad, last)
+            send_dq(0, 2)
+            parts, own[0][2] = tie(parts, own[0][2])
         sums_of = core_sums(parts)
-        mix_terms(0, kept, sums_of, mix_rows, proj_grad, spectrum_grad, last)
+        if last:
+            add_own(0, 1, sums_of)
+        else:
+            mix_terms(0, kept, sums_of, mix_rows, proj_grad, spectrum_grad, last)
         moved_sums = sent_sums(sums_of)
         small_sum[0] = add(small_sum[0], tap_grad)
         if last:
@@ -1094,34 +1147,24 @@
         grads_in[0].append(hidden_grad + grad_part)
         gain_sum[0] = add(gain_sum[0], jnp.stack([gain_one, gain_two]))
 
-    send_dq(0, 2)
-    line.mark(own[0][2])
-    total = {}
-    held = {}
-
-    def send_holder(m):
-        terms = line.take((crossed[0][m], crossed[1][m]))
-        total[m] = [
-            jnp.where(first, o, p) + jnp.where(first, t, u).astype(jnp.float32)
-            for o, p, t, u in zip(own[0][m], own[1][m], *terms)
-        ]
-        line.mark(total[m])
-        held[m] = [to_holder(t) for t in total[m]]
-
+    line.mark(own[0][1])
+    add_total(0, line.events)
+    (total[0], own[0][1]) = tie(total[0], own[0][1])
+    hold(0)
+    cross(0, 1)
+    line.mark(total[0])
     joined = {}
 
-    def send_quarters(m):
-        terms = line.take(held[m])
-        joined[m] = [quarters(t, o) for t, o in zip(total[m], terms)]
-        line.mark([j[0] for j in joined[m]])
-
-    send_holder(0)
+    def send_joined(m):
+        terms = [holder_total(t, o) for t, o in zip(total[m], line.take(held[m]))]
+        line.mark(terms)
+        joined[m] = [join_holders(t) for t in terms]
+
     grad_part, gain_one = kept[0](add_sums(sums_of, line.take(moved_sums)))
     state = hidden_grad + grad_part
     grads_in[0].append(state)
     gain_sum[0] = add(gain_sum[0], jnp.stack([gain_one, gain_two]))
     line.mark(state)
-    grad_sent = deliver(low(jnp.stack(grads_in[0])), low(jnp.stack(grads_in[1])))
     small = [
         jnp.concatenate(
             [jnp.pad(small_sum[k], ((0, 0), (0, width - channels))), gain_sum[k]], axis=0
@@ -1129,37 +1172,43 @@
         for k in range(2)
     ]
     small_other = swap_section(jnp.where(first, small[1], small[0]))
-    send_holder(1)
-    send_section(0, 2, line.events)
+    add_own(0, 2, line.events)
+    cross(0, 2)
     line.mark(own[0][2])
+    add_total(1, line.events)
+    hold(1)
+    line.mark(total[1])
+    send_joined(0)
     mine = jnp.where(first, small[0], small[1]) + line.take(small_other)
     moved_small = [shift(mine, "dq", k) for k in range(1, lax.axis_size("dq"))]
     line.mark(mine)
-    send_quarters(0)
+    add_total(2, line.events)
+    hold(2)
+    line.mark(total[2])
+    grad_sent = deliver(
+        *line.take((low(jnp.stack(grads_in[0])), low(jnp.stack(grads_in[1]))))
+    )
     sum_dq = mine
     for term in line.take(moved_small):
         sum_dq = sum_dq + term
     moved_small = permute(sum_dq, ("th",), lambda h: (1 - h,))
     line.mark(sum_dq)
-    layer_out = ordered(*line.take(out_sent))
-    line.mark(layer_out)
-    send_holder(2)
     mine = sum_dq + line.take(moved_small)
     rows_of = own_taps.shape[0]
     tap_grads = transposed(mine[:rows_of, :channels])
     gain_grads = mine[rows_of:]
     gain_other = swap_core(gain_grads)
     line.mark(mine)
-    send_quarters(1)
+    send_joined(1)
     gain_grads = gain_grads + line.take(gain_other)
     gain_moved = [shift(gain_grads, "tl", k) for k in range(1, peers)]
     line.mark(gain_grads)
     grad_in = ordered(*line.take(grad_sent))
     line.mark(grad_in)
-    send_quarters(2)
     gain_total = gain_grads
     for term in line.take(gain_moved):
         gain_total = gain_total + term
+    line.mark(gain_total)
 
     def finish_wide(buffers, outs):
         take = row_reader(buffers)
@@ -1175,10 +1224,16 @@
         outs[2][...] = take(2 * channels)[:, :freqs]
 
     grad_down, grad_gate_up = assemble(
-        line.take(joined[0] + joined[1]), finish_wide, [(hidden_cols, width), (width, 2, hidden_cols)]
+        line.take(joined[0] + joined[1]),
+        places,
+        finish_wide,
+        [(hidden_cols, width), (width, 2, hidden_cols)],
     )
+    line.mark(grad_down)
+    send_joined(2)
     grad_w_in, grad_w_out, grad_spectrum = assemble(
-        after(joined[2], grad_down),
+        joined[2],
+        places,
         finish_rest,
         [(3 * channels, width), (channels, width), (2 * channels, freqs)],
     )

time: 687 us -> 651 us (0.948)
  Pallas kernels: 169 us -> 139 us
  waiting for transfers between devices: 273 us -> 248 us
  local copies, waits for them, and re-layouts: 30.5 us -> 52.8 us
    ppermute x107 -> x104, waiting for transfers between devices: 273 us -> 248 us  [permute(): return lax.ppermute(values, axes if len(axes) > 1 else axes[0], pairs)]
    unnamed x281 -> x345, local copies, waits for them, and re-layouts: 17 us -> 37.4 us
    pallas_call x2, Pallas kernels: 61.9 us -> 53.6 us  [mixer_backward(): pl.pallas_call(partial(mixer_grad_kernel, nb, len(w_in_out)), grid=(size...]
    pallas_call x2, Pallas kernels: 53.3 us -> 45.1 us  [mixer_forward(): pl.pallas_call(partial(mixer_kernel, nb, len(w_in_out)), grid=(size // FT...]
    pallas_call x2, Pallas kernels: 20.4 us -> 12.9 us  [glu_backward(): pl.pallas_call(partial(glu_grad_kernel, nb, len(down)), grid=(hidden // t...]
    pallas_call x2, Pallas kernels: 19.3 us -> 12.4 us  [glu_forward(): pl.pallas_call(partial(glu_kernel, nb, len(down)), grid=(hidden // tile,)...]
    ppermute x107 -> x104, starting transfers between devices: 154 us -> 150 us  [permute(): return lax.ppermute(values, axes if len(axes) > 1 else axes[0], pairs)]
  transfers between devices with their start and end apart: 107 -> 104, of which waited for: 38 -> 35; matrix products, arithmetic and copies ran while one was open for 9% -> 9% of each run, Pallas kernels for 13% -> 19%
where the time goes in v3:
time: 651 us; the launch traced here: 643 us
  waiting for transfers between devices  248 us (38%)
  starting transfers between devices  150 us (23%)
  Pallas kernels  139 us (21%)
  local copies, waits for them, and re-layouts  52.8 us (8%)
  other arithmetic  39.6 us (6%)
  matrix products  9.75 us (1%)
    ppermute x104, waiting for transfers between devices, permute(): return lax.ppermute(values, axes if len(axes) > 1 else axes[0], pairs)  248 us
    ppermute x104, starting transfers between devices, permute(): return lax.ppermute(values, axes if len(axes) > 1 else axes[0], pairs)  150 us
    pallas_call x2, Pallas kernels, mixer_backward(): pl.pallas_call(partial(mixer_grad_kernel, nb, len(w_in_out)), grid=(size...  53.6 us
    pallas_call x2, Pallas kernels, mixer_forward(): pl.pallas_call(partial(mixer_kernel, nb, len(w_in_out)), grid=(size // FT...  45.1 us
    unnamed x345, local copies, waits for them, and re-layouts  37.4 us
  transfers between devices with their start and end apart: 104, of which 35 were waited for; matrix products, arithmetic and copies ran while one was open for 9% of the time, Pallas kernels for 19%

profile of v3, /device:TPU:0, one launch (start us, length us, event | category | flops | bytes accessed | tf_op | source)
XLA Modules:
  0.0 642.8 jit_solution(1624712715255820207)
XLA Ops:
  38.6 10.6 %collective-permute-start.5 = (bf16[176,768]{1,0:T(8,128)(2,1)S(1)}, bf16[176,768]{1,0:T(8,128)(2,1)S(1)}, u32[]{:S(2)}, u32[]{:S(2)}) collective-permute-start(bf16[176,768]{1,0:T(8,128)(2,1)S(1)} %fusion.9.refs_0_), channel_id=1, source_target_pairs={{0,4},{4,0},{1,5},{5,1},{2,6},{6,2},{3,7},{7,3},{8,12},{12,8},{9,1... | collective-permute-start | bytes 811016 | tf_op jit(solution)/shard_map/ppermute | solution.py:41
  52.1 6.0 collective-permute-start.10
  60.1 10.3 %collective-permute-start.9 = (bf16[768,768]{1,0:T(8,128)(2,1)}, bf16[768,768]{1,0:T(8,128)(2,1)}, u32[]{:S(2)}, u32[]{:S(2)}) collective-permute-start(bf16[768,768]{1,0:T(8,128)(2,1)} %bitcast.169), channel_id=1, source_target_pairs={{0,0},{2,4},{4,2},{6,6},{1,1},{3,5},{5,3},{7,7},{8,8},{10,12},{12,... | collective-permute-start | bytes 3538952 | tf_op jit(solution)/shard_map/ppermute | solution.py:41
  86.9 6.2 collective-permute-done.12.refs_5_
  103.1 22.8 %mixer_forward.2 = (f32[176,768]{1,0:T(8,128)S(1)}, f32[176,768]{1,0:T(8,128)S(1)}, f32[176,768]{1,0:T(8,128)S(1)}, f32[176,768]{1,0:T(8,128)S(1)}, bf16[4,176,7...) custom-call(s32[4]{0:T(128)S(1)} %copy-done.29, ...), custom_call_target="tpu_custom_call" | custom-call | flops 25999998976 | tf_op jit(solution)/shard_map/mixer_forward/pallas_call | solution.py:331
  129.4 10.2 %collective-permute-start.20 = (f32[176,768]{1,0:T(8,128)S(1)}, f32[176,768]{1,0:T(8,128)S(1)}, u32[]{:S(2)}, u32[]{:S(2)}) collective-permute-start(f32[176,768]{1,0:T(8,128)S(1)} %get-tuple-element.298), channel_id=1, source_target_pairs={{0,4},{4,0},{1,5},{5,1},{2,6},{6,2},{3,7},{7,3},{8,12},{12,8},{9,1... | collective-permute-start | bytes 1622024 | tf_op jit(solution)/shard_map/ppermute | solution.py:41
  147.2 10.8 %collective-permute-done.21 = f32[176,768]{1,0:T(8,128)S(1)} collective-permute-done((f32[176,768]{1,0:T(8,128)S(1)}, f32[176,768]{1,0:T(8,128)S(1)}, u32[]{:S(2)}, u32[]{:S(2)}) %collective-permute-start.21) | collective-permute-done | bytes 540704 | tf_op jit(solution)/shard_map/ppermute | solution.py:41
  160.4 6.4 %collective-permute-done.22.refs_1_ = bf16[176,768]{1,0:T(8,128)(2,1)S(1)} collective-permute-done((bf16[176,768]{1,0:T(8,128)(2,1)S(1)}, bf16[176,768]{1,0:T(8,128)(2,1)S(1)}, u32[]{:S(2)}, u32[]{:S(2)}) %collective-permute-start.22) | collective-permute-done | bytes 270368 | tf_op jit(solution)/shard_map/ppermute | solution.py:41
  166.9 18.9 %collective-permute-done.25.refs_5_.refs_7_ = bf16[768,768]{1,0:T(8,128)(2,1)S(1)} collective-permute-done((bf16[768,768]{1,0:T(8,128)(2,1)S(1)}, bf16[768,768]{1,0:T(8,128)(2,1)S(1)}, u32[]{:S(2)}, u32[]{:S(2)}) %collective-permute-start.25) | collective-permute-done | bytes 1179680 | tf_op jit(solution)/shard_map/ppermute | solution.py:41
  185.8 6.3 glu_forward.2
  198.0 11.9 %collective-permute-done.29 = f32[176,768]{1,0:T(8,128)S(1)} collective-permute-done((f32[176,768]{1,0:T(8,128)S(1)}, f32[176,768]{1,0:T(8,128)S(1)}, u32[]{:S(2)}, u32[]{:S(2)}) %collective-permute-start.29) | collective-permute-done | bytes 540704 | tf_op jit(solution)/shard_map/ppermute | solution.py:41
  211.1 7.3 %collective-permute-done.30.refs_1_ = bf16[176,768]{1,0:T(8,128)(2,1)S(1)} collective-permute-done((bf16[176,768]{1,0:T(8,128)(2,1)S(1)}, bf16[176,768]{1,0:T(8,128)(2,1)S(1)}, u32[]{:S(2)}, u32[]{:S(2)}) %collective-permute-start.30) | collective-permute-done | bytes 270368 | tf_op jit(solution)/shard_map/ppermute | solution.py:41
  225.8 22.3 %mixer_forward.3 = (f32[176,768]{1,0:T(8,128)S(1)}, f32[176,768]{1,0:T(8,128)S(1)}, f32[176,768]{1,0:T(8,128)S(1)}, f32[176,768]{1,0:T(8,128)S(1)}, bf16[4,176,7...) custom-call(s32[4]{0:T(128)S(1)} %copy-done.29, ...), custom_call_target="tpu_custom_call" | custom-call | flops 25999998976 | tf_op jit(solution)/shard_map/mixer_forward/pallas_call | solution.py:331
  249.4 13.8 %collective-permute-done.38.refs_5_.refs_7_ = bf16[768,768]{1,0:T(8,128)(2,1)S(1)} collective-permute-done((bf16[768,768]{1,0:T(8,128)(2,1)S(1)}, bf16[768,768]{1,0:T(8,128)(2,1)S(1)}, u32[]{:S(2)}, u32[]{:S(2)}) %collective-permute-start.38) | collective-permute-done | bytes 1179680 | tf_op jit(solution)/shard_map/ppermute | solution.py:41
  267.0 12.6 %collective-permute-done.42 = f32[176,768]{1,0:T(8,128)S(1)} collective-permute-done((f32[176,768]{1,0:T(8,128)S(1)}, f32[176,768]{1,0:T(8,128)S(1)}, u32[]{:S(2)}, u32[]{:S(2)}) %collective-permute-start.42) | collective-permute-done | bytes 540704 | tf_op jit(solution)/shard_map/ppermute | solution.py:41
  282.0 6.0 collective-permute-done.43.refs_1_
  289.6 6.1 glu_forward.3
  297.6 6.8 %glu_backward.2 = (f32[176,768]{1,0:T(8,128)S(1)}, f32[176,768]{1,0:T(8,128)S(1)}, f32[176,768]{1,0:T(8,128)}, f32[176,768]{1,0:T(8,128)S(1)}, bf16[704,768]{1,0...) custom-call(s32[2]{0:T(128)S(1)} %copy-done.62, bf16[176,768]{1,0:T(8,128)(2,1)S(1)} %bitcast.181, ...), custom_call_target="tpu_custom_call" | custom-call | flops 9500000256 | tf_op jit(solution)/shard_map/glu_backward/pallas_call | solution.py:683
  311.0 13.0 %collective-permute-done.48 = f32[176,768]{1,0:T(8,128)} collective-permute-done((f32[176,768]{1,0:T(8,128)}, f32[176,768]{1,0:T(8,128)}, u32[]{:S(2)}, u32[]{:S(2)}) %collective-permute-start.48) | collective-permute-done | bytes 540704 | tf_op jit(solution)/shard_map/ppermute | solution.py:41
  342.9 27.4 %mixer_backward.2 = (f32[176,768]{1,0:T(8,128)S(1)}, f32[176,768]{1,0:T(8,128)S(1)}, f32[176,768]{1,0:T(8,128)}, f32[176,768]{1,0:T(8,128)}, bf16[4,176,768]{2,1...) custom-call(s32[4]{0:T(128)S(1)} %copy-done.30, ...), custom_call_target="tpu_custom_call" | custom-call | flops 30000001024 | tf_op jit(solution)/shard_map/mixer_backward/pallas_call | solution.py:499
  384.0 9.7 %collective-permute-done.59 = f32[176,768]{1,0:T(8,128)S(1)} collective-permute-done((f32[176,768]{1,0:T(8,128)S(1)}, f32[176,768]{1,0:T(8,128)S(1)}, u32[]{:S(2)}, u32[]{:S(2)}) %collective-permute-start.59) | collective-permute-done | bytes 540704 | tf_op jit(solution)/shard_map/ppermute | solution.py:41
  398.9 7.7 %collective-permute-done.60.refs_1_ = bf16[176,768]{1,0:T(8,128)(2,1)S(1)} collective-permute-done((bf16[176,768]{1,0:T(8,128)(2,1)S(1)}, bf16[176,768]{1,0:T(8,128)(2,1)S(1)}, u32[]{:S(2)}, u32[]{:S(2)}) %collective-permute-start.60) | collective-permute-done | bytes 270368 | tf_op jit(solution)/shard_map/ppermute | solution.py:41
  409.6 6.1 glu_backward.3
  430.4 8.1 %collective-permute-done.66 = f32[176,768]{1,0:T(8,128)S(1)} collective-permute-done((f32[176,768]{1,0:T(8,128)S(1)}, f32[176,768]{1,0:T(8,128)S(1)}, u32[]{:S(2)}, u32[]{:S(2)}) %collective-permute-start.66) | collective-permute-done | bytes 540704 | tf_op jit(solution)/shard_map/ppermute | solution.py:41
  441.2 6.4 collective-permute-done.68.refs_1_
  452.0 26.1 %mixer_backward.3 = (f32[176,768]{1,0:T(8,128)S(1)}, f32[176,768]{1,0:T(8,128)S(1)}, f32[176,768]{1,0:T(8,128)S(1)}, f32[176,768]{1,0:T(8,128)S(1)}, bf16[4,176,...) custom-call(s32[4]{0:T(128)S(1)} %copy-done.30, ...), custom_call_target="tpu_custom_call" | custom-call | flops 30000001024 | tf_op jit(solution)/shard_map/mixer_backward/pallas_call | solution.py:499
  495.2 13.7 %collective-permute-done.78 = bf16[576,768]{1,0:T(8,128)(2,1)S(1)} collective-permute-done((bf16[576,768]{1,0:T(8,128)(2,1)S(1)}, bf16[576,768]{1,0:T(8,128)(2,1)S(1)}, u32[]{:S(2)}, u32[]{:S(2)}) %collective-permute-start.78) | collective-permute-done | bytes 884768 | tf_op jit(solution)/shard_map/ppermute | solution.py:41
  517.4 18.0 %collective-permute-done.84 = bf16[576,768]{1,0:T(8,128)(2,1)S(1)} collective-permute-done((bf16[576,768]{1,0:T(8,128)(2,1)S(1)}, bf16[576,768]{1,0:T(8,128)(2,1)S(1)}, u32[]{:S(2)}, u32[]{:S(2)}) %collective-permute-start.84) | collective-permute-done | bytes 884768 | tf_op jit(solution)/shard_map/ppermute | solution.py:41
  539.0 14.4 %collective-permute-done.81 = bf16[576,768]{1,0:T(8,128)(2,1)S(1)} collective-permute-done((bf16[576,768]{1,0:T(8,128)(2,1)S(1)}, bf16[576,768]{1,0:T(8,128)(2,1)S(1)}, u32[]{:S(2)}, u32[]{:S(2)}) %collective-permute-start.81) | collective-permute-done | bytes 884768 | tf_op jit(solution)/shard_map/ppermute | solution.py:41
  573.7 6.2 collective-permute-done.97.refs_5_
  588.5 6.6 %assemble.2 = (f32[768,768]{1,0:T(8,128)}, f32[768,2,768]{2,1,0:T(2,128)}) custom-call(s32[3]{0:T(128)S(1)} %pad_add_fusion.2.places, bf16[576,768]{1,0:T(8,128)(2,1)S(1)} %add_convert_fusion.2.refs_0_, bf16[576,768]{1,0:T(8,128)(2,1)S(1)} %collective-permute-done.94.refs_1_, bf16[576,768]{1,0:T(8,128)(2,1)} %collective-permute-done.95.refs_2_, ...), custom_call_target="tpu_custom_call" | custom-call | flops 4000000000 | tf_op jit(solution)/shard_map/assemble/pallas_call | solution.py:792
  595.1 17.6 %collective-permute-done.93 = bf16[576,768]{1,0:T(8,128)(2,1)} collective-permute-done((bf16[576,768]{1,0:T(8,128)(2,1)}, bf16[576,768]{1,0:T(8,128)(2,1)}, u32[]{:S(2)}, u32[]{:S(2)}) %collective-permute-start.93) | collective-permute-done | bytes 884768 | tf_op jit(solution)/shard_map/ppermute | solution.py:41
  (682 shorter events, 262.9 us)
Async XLA Ops:
  2.1 28.9 %collective-permute-start.3 = (f32[2,768]{1,0:T(2,128)}, f32[2,768]{1,0:T(2,128)}, u32[]{:S(2)}, u32[]{:S(2)}) collective-permute-start(f32[2,768]{1,0:T(2,128)} %pad_maximum_fusion.6), channel_id=1, source_target_pairs={{0,16},{16,0},{1,17},{17,1},{2,18},{18,2},{3,19},{19,3},{4,20},{20... | collective-permute-start | bytes 18440 | tf_op jit(solution)/shard_map/ppermute | solution.py:41
  5.7 46.3 %collective-permute-start.16 = (f32[2,704]{1,0:T(2,128)S(1)}, f32[2,704]{1,0:T(2,128)S(1)}, u32[]{:S(2)}, u32[]{:S(2)}) collective-permute-start(f32[2,704]{1,0:T(2,128)S(1)} %convert_element_type.265), channel_id=1, source_target_pairs={{0,4},{4,0},{1,5},{5,1},{2,6},{6,2},{3,7},{7,3},{8,12},{12,8},{9,1... | collective-permute-start | bytes 16904 | tf_op jit(solution)/shard_map/ppermute | solution.py:41
  6.8 25.6 %collective-permute-start = (bf16[1,176,768]{2,1,0:T(8,128)(2,1)S(1)}, bf16[1,176,768]{2,1,0:T(8,128)(2,1)S(1)}, u32[]{:S(2)}, u32[]{:S(2)}) collective-permute-start(bf16[1,176,768]{2,1,0:T(8,128)(2,1)S(1)} %constant_dynamic-slice_fusion.3), channel_id=1, source_target_pairs={{0,0},{2,4},{4,2},{6,6},{1,1},{3,5},{5,3},{7,7},{8,8},{10,12},{12,... | collective-permute-start | bytes 811016 | tf_op jit(solution)/shard_map/ppermute | solution.py:41
  9.7 22.7 %collective-permute-start.1 = (bf16[384,768]{1,0:T(8,128)(2,1)}, bf16[384,768]{1,0:T(8,128)(2,1)S(1)}, u32[]{:S(2)}, u32[]{:S(2)}) collective-permute-start(bf16[384,768]{1,0:T(8,128)(2,1)} %fusion.8), channel_id=1, source_target_pairs={{0,0},{2,4},{4,2},{6,6},{1,1},{3,5},{5,3},{7,7},{8,8},{10,12},{12,... | collective-permute-start | bytes 1769480 | tf_op jit(solution)/shard_map/ppermute | solution.py:41
  34.6 35.8 %collective-permute-start.7 = (bf16[384,768]{1,0:T(8,128)(2,1)S(1)}, bf16[384,768]{1,0:T(8,128)(2,1)S(1)}, u32[]{:S(2)}, u32[]{:S(2)}) collective-permute-start(bf16[384,768]{1,0:T(8,128)(2,1)S(1)} %collective-permute-done.1), channel_id=1, source_target_pairs={{0,16},{16,0},{1,17},{17,1},{2,18},{18,2},{3,19},{19,3},{4,20},{20... | collective-permute-start | bytes 1769480 | tf_op jit(solution)/shard_map/ppermute | solution.py:41
  35.9 34.5 %collective-permute-start.8 = (f32[192,705]{1,0:T(8,128)}, f32[192,705]{1,0:T(8,128)S(1)}, u32[]{:S(2)}, u32[]{:S(2)}) collective-permute-start(f32[192,705]{1,0:T(8,128)} %collective-permute-done.2), channel_id=1, source_target_pairs={{0,16},{16,0},{1,17},{17,1},{2,18},{18,2},{3,19},{19,3},{4,20},{20... | collective-permute-start | bytes 1624328 | tf_op jit(solution)/shard_map/ppermute | solution.py:41
  83.7 45.7 %collective-permute-start.18 = (bf16[1,176,768]{2,1,0:T(8,128)(2,1)}, bf16[1,176,768]{2,1,0:T(8,128)(2,1)S(1)}, u32[]{:S(2)}, u32[]{:S(2)}) collective-permute-start(bf16[1,176,768]{2,1,0:T(8,128)(2,1)} %constant_dynamic-slice_fusion), channel_id=1, source_target_pairs={{0,0},{2,4},{4,2},{6,6},{1,1},{3,5},{5,3},{7,7},{8,8},{10,12},{12,... | collective-permute-start | bytes 811016 | tf_op jit(solution)/shard_map/ppermute | solution.py:41
  85.5 41.5 %collective-permute-start.17 = (bf16[768,768]{1,0:T(8,128)(2,1)}, bf16[768,768]{1,0:T(8,128)(2,1)S(1)}, u32[]{:S(2)}, u32[]{:S(2)}) collective-permute-start(bf16[768,768]{1,0:T(8,128)(2,1)} %collective-permute-done.9), channel_id=1, source_target_pairs={{0,16},{16,0},{1,17},{17,1},{2,18},{18,2},{3,19},{19,3},{4,20},{20... | collective-permute-start | bytes 3538952 | tf_op jit(solution)/shard_map/ppermute | solution.py:41
  146.7 39.1 %collective-permute-start.25 = (bf16[768,768]{1,0:T(8,128)(2,1)S(1)}, bf16[768,768]{1,0:T(8,128)(2,1)S(1)}, u32[]{:S(2)}, u32[]{:S(2)}) collective-permute-start(bf16[768,768]{1,0:T(8,128)(2,1)S(1)} %get-tuple-element.299.refs_4_.refs_6_), channel_id=1, source_target_pairs={{0,8},{8,0},{1,9},{9,1},{2,10},{10,2},{3,11},{11,3},{4,12},{12,4},... | collective-permute-start | bytes 3538952 | tf_op jit(solution)/shard_map/ppermute | solution.py:41
  160.4 25.3 %collective-permute-start.23 = (bf16[176,768]{1,0:T(8,128)(2,1)S(1)}, bf16[176,768]{1,0:T(8,128)(2,1)S(1)}, u32[]{:S(2)}, u32[]{:S(2)}) collective-permute-start(bf16[176,768]{1,0:T(8,128)(2,1)S(1)} %multiply_convert_fusion.2.refs_0_), channel_id=1, source_target_pairs={{0,4},{4,0},{1,5},{5,1},{2,6},{6,2},{3,7},{7,3},{8,12},{12,8},{9,1... | collective-permute-start | bytes 811016 | tf_op jit(solution)/shard_map/ppermute | solution.py:41
  196.0 29.3 %collective-permute-start.33 = (bf16[384,768]{1,0:T(8,128)(2,1)S(1)}, bf16[384,768]{1,0:T(8,128)(2,1)S(1)}, u32[]{:S(2)}, u32[]{:S(2)}) collective-permute-start(bf16[384,768]{1,0:T(8,128)(2,1)S(1)} %get-tuple-element.305.refs_4_), channel_id=1, source_target_pairs={{0,8},{8,0},{1,9},{9,1},{2,10},{10,2},{3,11},{11,3},{4,12},{12,4},... | collective-permute-start | bytes 1769480 | tf_op jit(solution)/shard_map/ppermute | solution.py:41
  197.5 26.2 %collective-permute-start.34 = (f32[192,705]{1,0:T(8,128)S(1)}, f32[192,705]{1,0:T(8,128)S(1)}, u32[]{:S(2)}, u32[]{:S(2)}) collective-permute-start(f32[192,705]{1,0:T(8,128)S(1)} %get-tuple-element.306.refs_6_), channel_id=1, source_target_pairs={{0,8},{8,0},{1,9},{9,1},{2,10},{10,2},{3,11},{11,3},{4,12},{12,4},... | collective-permute-start | bytes 1624328 | tf_op jit(solution)/shard_map/ppermute | solution.py:41
  218.4 31.0 %collective-permute-start.35 = (bf16[176,768]{1,0:T(8,128)(2,1)S(1)}, bf16[176,768]{1,0:T(8,128)(2,1)S(1)}, u32[]{:S(2)}, u32[]{:S(2)}) collective-permute-start(bf16[176,768]{1,0:T(8,128)(2,1)S(1)} %bitcast.179), channel_id=1, source_target_pairs={{0,1},{1,0},{2,3},{3,2},{4,5},{5,4},{6,7},{7,6},{8,9},{9,8},{10,11... | collective-permute-start | bytes 811016 | tf_op jit(solution)/shard_map/ppermute | solution.py:41
  223.7 25.7 %collective-permute-start.39 = (bf16[384,768]{1,0:T(8,128)(2,1)S(1)}, bf16[384,768]{1,0:T(8,128)(2,1)S(1)}, u32[]{:S(2)}, u32[]{:S(2)}) collective-permute-start(bf16[384,768]{1,0:T(8,128)(2,1)S(1)} %get-tuple-element.326.refs_6_.refs_8_), channel_id=1, source_target_pairs={{0,8},{8,0},{1,9},{9,1},{2,10},{10,2},{3,11},{11,3},{4,12},{12,4},... | collective-permute-start | bytes 1769480 | tf_op jit(solution)/shard_map/ppermute | solution.py:41
  225.3 38.0 %collective-permute-start.38 = (bf16[768,768]{1,0:T(8,128)(2,1)S(1)}, bf16[768,768]{1,0:T(8,128)(2,1)S(1)}, u32[]{:S(2)}, u32[]{:S(2)}) collective-permute-start(bf16[768,768]{1,0:T(8,128)(2,1)S(1)} %get-tuple-element.324.refs_4_.refs_6_), channel_id=1, source_target_pairs={{0,8},{8,0},{1,9},{9,1},{2,10},{10,2},{3,11},{11,3},{4,12},{12,4},... | collective-permute-start | bytes 3538952 | tf_op jit(solution)/shard_map/ppermute | solution.py:41
  335.0 38.7 %collective-permute-start.56 = (bf16[576,768]{1,0:T(8,128)(2,1)S(1)}, bf16[576,768]{1,0:T(8,128)(2,1)S(1)}, u32[]{:S(2)}, u32[]{:S(2)}) collective-permute-start(bf16[576,768]{1,0:T(8,128)(2,1)S(1)} %dynamic-slice_bitcast_fusion.8), channel_id=1, source_target_pairs={{0,8},{8,0},{1,9},{9,1},{2,10},{10,2},{3,11},{11,3},{4,12},{12,4},... | collective-permute-start | bytes 2654216 | tf_op jit(solution)/shard_map/ppermute | solution.py:41
  338.5 37.3 %collective-permute-start.55 = (bf16[576,768]{1,0:T(8,128)(2,1)S(1)}, bf16[576,768]{1,0:T(8,128)(2,1)S(1)}, u32[]{:S(2)}, u32[]{:S(2)}) collective-permute-start(bf16[576,768]{1,0:T(8,128)(2,1)S(1)} %dynamic-slice_bitcast_fusion.9), channel_id=1, source_target_pairs={{0,8},{8,0},{1,9},{9,1},{2,10},{10,2},{3,11},{11,3},{4,12},{12,4},... | collective-permute-start | bytes 2654216 | tf_op jit(solution)/shard_map/ppermute | solution.py:41
  341.0 32.7 %collective-permute-start.54 = (f32[176,768]{1,0:T(8,128)S(1)}, f32[176,768]{1,0:T(8,128)S(1)}, u32[]{:S(2)}, u32[]{:S(2)}) collective-permute-start(f32[176,768]{1,0:T(8,128)S(1)} %add.310), channel_id=1, source_target_pairs={{0,1},{1,0},{2,3},{3,2},{4,5},{5,4},{6,7},{7,6},{8,9},{9,8},{10,11... | collective-permute-start | bytes 1622024 | tf_op jit(solution)/shard_map/ppermute | solution.py:41
  417.4 77.7 %collective-permute-start.79 = (bf16[576,768]{1,0:T(8,128)(2,1)}, bf16[576,768]{1,0:T(8,128)(2,1)}, u32[]{:S(2)}, u32[]{:S(2)}) collective-permute-start(bf16[576,768]{1,0:T(8,128)(2,1)} %convert_element_type.311), channel_id=1, source_target_pairs={{0,16},{1,17},{2,18},{3,19},{4,20},{5,21},{6,22},{7,23},{8,24},{9,... | collective-permute-start | bytes 2654216 | tf_op jit(solution)/shard_map/ppermute | solution.py:41
  422.8 26.0 %collective-permute-start.71 = (bf16[576,768]{1,0:T(8,128)(2,1)S(1)}, bf16[576,768]{1,0:T(8,128)(2,1)S(1)}, u32[]{:S(2)}, u32[]{:S(2)}) collective-permute-start(bf16[576,768]{1,0:T(8,128)(2,1)S(1)} %get-tuple-element.602), channel_id=1, source_target_pairs={{0,8},{8,0},{1,9},{9,1},{2,10},{10,2},{3,11},{11,3},{4,12},{12,4},... | collective-permute-start | bytes 2654216 | tf_op jit(solution)/shard_map/ppermute | solution.py:41
  427.6 50.5 %collective-permute-start.72 = (bf16[576,768]{1,0:T(8,128)(2,1)}, bf16[576,768]{1,0:T(8,128)(2,1)}, u32[]{:S(2)}, u32[]{:S(2)}) collective-permute-start(bf16[576,768]{1,0:T(8,128)(2,1)} %get-tuple-element.600), channel_id=1, source_target_pairs={{0,8},{8,0},{1,9},{9,1},{2,10},{10,2},{3,11},{11,3},{4,12},{12,4},... | collective-permute-start | bytes 2654216 | tf_op jit(solution)/shard_map/ppermute | solution.py:41
  448.8 33.6 %collective-permute-start.73 = (bf16[576,768]{1,0:T(8,128)(2,1)}, bf16[576,768]{1,0:T(8,128)(2,1)S(1)}, u32[]{:S(2)}, u32[]{:S(2)}) collective-permute-start(bf16[576,768]{1,0:T(8,128)(2,1)} %get-tuple-element.598), channel_id=1, source_target_pairs={{0,8},{8,0},{1,9},{9,1},{2,10},{10,2},{3,11},{11,3},{4,12},{12,4},... | collective-permute-start | bytes 2654216 | tf_op jit(solution)/shard_map/ppermute | solution.py:41
  449.6 32.8 %collective-permute-start.74 = (bf16[576,768]{1,0:T(8,128)(2,1)S(1)}, bf16[576,768]{1,0:T(8,128)(2,1)S(1)}, u32[]{:S(2)}, u32[]{:S(2)}) collective-permute-start(bf16[576,768]{1,0:T(8,128)(2,1)S(1)} %convert_element_type.305), channel_id=1, source_target_pairs={{0,16},{1,17},{2,18},{3,19},{4,20},{5,21},{6,22},{7,23},{8,24},{9,... | collective-permute-start | bytes 2654216 | tf_op jit(solution)/shard_map/ppermute | solution.py:41
  486.1 22.8 %collective-permute-start.78 = (bf16[576,768]{1,0:T(8,128)(2,1)S(1)}, bf16[576,768]{1,0:T(8,128)(2,1)S(1)}, u32[]{:S(2)}, u32[]{:S(2)}) collective-permute-start(bf16[576,768]{1,0:T(8,128)(2,1)S(1)} %convert_element_type.310), channel_id=1, source_target_pairs={{16,0},{17,1},{18,2},{19,3},{20,4},{21,5},{22,6},{23,7},{24,8},{25... | collective-permute-start | bytes 2654216 | tf_op jit(solution)/shard_map/ppermute | solution.py:41
  488.3 29.0 %collective-permute-start.85 = (bf16[576,768]{1,0:T(8,128)(2,1)S(1)}, bf16[576,768]{1,0:T(8,128)(2,1)S(1)}, u32[]{:S(2)}, u32[]{:S(2)}) collective-permute-start(bf16[576,768]{1,0:T(8,128)(2,1)S(1)} %convert_element_type.323), channel_id=1, source_target_pairs={{0,16},{1,17},{2,18},{3,19},{4,20},{5,21},{6,22},{7,23},{8,24},{9,... | collective-permute-start | bytes 2654216 | tf_op jit(solution)/shard_map/ppermute | solution.py:41
  493.2 22.7 %collective-permute-start.80 = (bf16[576,768]{1,0:T(8,128)(2,1)S(1)}, bf16[576,768]{1,0:T(8,128)(2,1)S(1)}, u32[]{:S(2)}, u32[]{:S(2)}) collective-permute-start(bf16[576,768]{1,0:T(8,128)(2,1)S(1)} %get-tuple-element.596), channel_id=1, source_target_pairs={{0,8},{8,0},{1,9},{9,1},{2,10},{10,2},{3,11},{11,3},{4,12},{12,4},... | collective-permute-start | bytes 2654216 | tf_op jit(solution)/shard_map/ppermute | solution.py:41
  509.5 26.3 %collective-permute-start.83 = (bf16[576,768]{1,0:T(8,128)(2,1)S(1)}, bf16[576,768]{1,0:T(8,128)(2,1)S(1)}, u32[]{:S(2)}, u32[]{:S(2)}) collective-permute-start(bf16[576,768]{1,0:T(8,128)(2,1)S(1)} %convert_element_type.321), channel_id=1, source_target_pairs={{2,0},{4,6},{3,1},{5,7},{10,8},{12,14},{11,9},{13,15},{18,16},{20,... | collective-permute-start | bytes 2654216 | tf_op jit(solution)/shard_map/ppermute | solution.py:41
  510.9 24.5 %collective-permute-start.84 = (bf16[576,768]{1,0:T(8,128)(2,1)S(1)}, bf16[576,768]{1,0:T(8,128)(2,1)S(1)}, u32[]{:S(2)}, u32[]{:S(2)}) collective-permute-start(bf16[576,768]{1,0:T(8,128)(2,1)S(1)} %convert_element_type.322), channel_id=1, source_target_pairs={{16,0},{17,1},{18,2},{19,3},{20,4},{21,5},{22,6},{23,7},{24,8},{25... | collective-permute-start | bytes 2654216 | tf_op jit(solution)/shard_map/ppermute | solution.py:41
  513.0 24.4 %collective-permute-start.82 = (f32[18,768]{1,0:T(8,128)S(1)}, f32[18,768]{1,0:T(8,128)S(1)}, u32[]{:S(2)}, u32[]{:S(2)}) collective-permute-start(f32[18,768]{1,0:T(8,128)S(1)} %fusion.19), channel_id=1, source_target_pairs={{0,16},{16,0},{1,17},{17,1},{2,18},{18,2},{3,19},{19,3},{4,20},{20... | collective-permute-start | bytes 165896 | tf_op jit(solution)/shard_map/ppermute | solution.py:41
  516.1 37.3 %collective-permute-start.81 = (bf16[576,768]{1,0:T(8,128)(2,1)S(1)}, bf16[576,768]{1,0:T(8,128)(2,1)S(1)}, u32[]{:S(2)}, u32[]{:S(2)}) collective-permute-start(bf16[576,768]{1,0:T(8,128)(2,1)S(1)} %fusion.30), channel_id=1, source_target_pairs={{16,0},{17,1},{18,2},{19,3},{20,4},{21,5},{22,6},{23,7},{24,8},{25... | collective-permute-start | bytes 2654216 | tf_op jit(solution)/shard_map/ppermute | solution.py:41
  535.8 27.7 %collective-permute-start.91 = (bf16[576,768]{1,0:T(8,128)(2,1)S(1)}, bf16[576,768]{1,0:T(8,128)(2,1)S(1)}, u32[]{:S(2)}, u32[]{:S(2)}) collective-permute-start(bf16[576,768]{1,0:T(8,128)(2,1)S(1)} %get-tuple-element.568), channel_id=1, source_target_pairs={{2,0},{4,6},{3,1},{5,7},{10,8},{12,14},{11,9},{13,15},{18,16},{20,... | collective-permute-start | bytes 2654216 | tf_op jit(solution)/shard_map/ppermute | solution.py:41
  587.0 25.6 %collective-permute-start.93 = (bf16[576,768]{1,0:T(8,128)(2,1)}, bf16[576,768]{1,0:T(8,128)(2,1)}, u32[]{:S(2)}, u32[]{:S(2)}) collective-permute-start(bf16[576,768]{1,0:T(8,128)(2,1)} %get-tuple-element.566), channel_id=1, source_target_pairs={{2,0},{4,6},{3,1},{5,7},{10,8},{12,14},{11,9},{13,15},{18,16},{20,... | collective-permute-start | bytes 2654216 | tf_op jit(solution)/shard_map/ppermute | solution.py:41
  (243 other events, 3087.1 us)

commit v4 on v3

--- a/solution.py
+++ b/solution.py
@@ -177,6 +177,7 @@
         tables_kernel,
         out_shape=[jax.ShapeDtypeStruct((size, size), jnp.bfloat16)] * 4,
         cost_estimate=pl.CostEstimate(flops=int(4 * PEAK), bytes_accessed=0, transcendentals=0),
+        compiler_params=pltpu.CompilerParams(vmem_limit_bytes=12 * MIB),
         name="tables",
     )(*small)
 
@@ -372,11 +373,11 @@
     grads = refs[:nb]
     w_parts, s_parts = refs[nb : nb + np_], refs[nb + np_ : nb + 2 * np_]
     refs = refs[nb + 2 * np_ :]
-    (taps, cols, proj, long, cond_hat, piece_hat) = refs[:6]
-    (ch_r, cl_r, sh_r, sl_r, ch_c, cl_c, sh_c, sl_c) = refs[6:14]
-    partials = refs[14 : nb + 14]
-    gathered, proj_grad, grad_spectrum, grad_taps = refs[nb + 14 : nb + 18]
-    x_hi, x_lo, acc, query_grad, full, w_in_out, spectrum = refs[nb + 18 :]
+    (taps, cols, normed, gain, proj, long, cond_hat, piece_hat) = refs[:8]
+    (ch_r, cl_r, sh_r, sl_r, ch_c, cl_c, sh_c, sl_c) = refs[8:16]
+    partials = refs[16 : nb + 16]
+    gathered, proj_grad, grad_spectrum, grad_taps, grad_gain = refs[nb + 16 : nb + 21]
+    x_hi, x_lo, acc, query_grad, full, w_in_out, spectrum = refs[nb + 21 :]
     step = pl.program_id(0)
     count = grads[0].shape[0]
     pack_len = proj.shape[0]
@@ -483,10 +484,15 @@
             at = pl.ds(pl.multiple_of(order[j] * count, 8), count)
             low = full[at, :].astype(jnp.bfloat16)
             proj_grad[j] = low
-            partials[j][...] = mm(low, w_in_out[: 3 * width, :])
-
-
-def mixer_backward(blocks, w_in_out, taps, cols, kept, spectra, tables, order, places):
+            rows_grad = mm(low, w_in_out[: 3 * width, :])
+            partials[j][...] = rows_grad
+            seen = normed[j * count : (j + 1) * count, :].astype(jnp.float32)
+            term = jnp.sum(rows_grad * seen, axis=0, keepdims=True)
+            gain_sum = term if j == 0 else gain_sum + term
+        grad_gain[...] = gain_sum / gain[...]
+
+
+def mixer_backward(blocks, w_in_out, taps, cols, normed, gain, kept, spectra, tables, order, places):
     layer = 0
     proj, long, cond_hat, piece_hat = kept
     pack_len = cols.shape[0]
@@ -505,6 +511,8 @@
         + [
             of_layer(layer, taps.shape[1:]),
             whole(cols.shape),
+            whole(normed.shape),
+            whole(gain.shape),
             whole(proj.shape),
             whole(long.shape),
             freq,
@@ -517,6 +525,7 @@
             whole((nb, count, 3 * width)),
             pl.BlockSpec((2, width, FTILE), lambda i: (0, 0, i)),
             whole(taps.shape[1:]),
+            whole(gain.shape),
         ],
         out_shape=[jax.ShapeDtypeStruct((count, model), f32)] * nb
         + [
@@ -524,6 +533,7 @@
             jax.ShapeDtypeStruct((nb, count, 3 * width), low),
             jax.ShapeDtypeStruct((2, width, size), low),
             jax.ShapeDtypeStruct(taps.shape[1:], f32),
+            jax.ShapeDtypeStruct(gain.shape, f32),
         ],
         scratch_shapes=[
             pltpu.VMEM((size, SEGS * width), low),
@@ -533,20 +543,22 @@
             pltpu.VMEM((pack_len, 3 * width), f32),
         ]
         + part_scratch(w_in_out, spectra),
-        compiler_params=pltpu.CompilerParams(vmem_limit_bytes=37 * MIB),
+        compiler_params=pltpu.CompilerParams(vmem_limit_bytes=40 * MIB),
         cost_estimate=pl.CostEstimate(flops=int(30 * PEAK), bytes_accessed=0, transcendentals=0),
         name="mixer_backward",
     )(
-        order, places, *blocks, *w_in_out, *spectra, taps, cols, proj, long, cond_hat, piece_hat,
+        order, places, *blocks, *w_in_out, *spectra, taps, cols, normed, gain, proj, long, cond_hat,
+        piece_hat,
         *tables, *tables,
     )
-    rows, proj_grad, grad_spectrum, grad_taps = out[nb:]
+    rows, proj_grad, grad_spectrum, grad_taps, grad_gain = out[nb:]
     return (
         out[:nb],
         rows.reshape(pack_len, model),
         proj_grad.reshape(pack_len, 3 * width),
         grad_spectrum.reshape(2 * width, size),
         grad_taps,
+        grad_gain,
     )
 
 
@@ -939,17 +951,20 @@
             )
             if opening:
                 gu_both = by_layer(gu_part, after(gu_other, parts))
-                parts, gu_first, cot_in = tie(parts, gu_both[0], cot_in)
+                parts, gu_first, cot_in, down[0] = tie(parts, gu_both[0], cot_in, down[0])
             if layer == 1:
                 parts, cot_chip = tie(parts, cot_chip)
             if index == 0 and layer == 1:
-                parts, gate_up[1], down[1] = tie(parts, gate_up[1], down[1])
+                parts, gate_up[1] = tie(parts, gate_up[1])
             sums_of = core_sums(parts)
             if opening:
                 gate_up[0] = join_parts(gu_first)
             if layer == 1:
                 cot_blocks = both_cores(cot_chip)
-            hidden = state + chip_sums(sums_of)
+            moved_sums = sent_sums(sums_of)
+            if index == 0 and layer == 1:
+                moved_sums, down[1] = tie(moved_sums, down[1])
+            hidden = state + add_sums(sums_of, moved_sums)
             normed_two, norm_pull_two = jax.vjp(layer_norm, hidden, gains[layer, 1])
             blocks = gather_rows(low(normed_two))
             if opening:
@@ -1009,16 +1024,24 @@
         }
         collect(layer, terms, last)
 
-    def mix_terms(layer, kept, sums_of, mix_rows, proj_grad, spectrum_grad, last):
+    def small_rows(tap_grad, gain_one, gain_two):
+        rows_of = jnp.pad(tap_grad, ((0, 0), (0, width - channels)))
+        filled = rows_of.shape[0] + 2
+        return jnp.concatenate(
+            [rows_of, gain_one, gain_two[None], jnp.zeros((-filled % 64, width), jnp.float32)], axis=0
+        )
+
+    def mix_terms(layer, kept, sums_of, mix_rows, proj_grad, spectrum_grad, small, last):
         mix, mix_rows, proj_grad, rows_one = after((kept[2], mix_rows, proj_grad, kept[1]), sums_of)
         terms = {
             "w_in": dot32("lc,ld->cd", proj_grad, rows_one),
             "w_out": dot32("lc,ld->cd", mix, mix_rows),
             "spectrum": spectrum_grad,
+            "small": small,
         }
         collect(layer, terms, last)
 
-    contents = (("down", "gate_a"), ("gate_b", "up"), ("w_in", "w_out", "spectrum"))
+    contents = (("down", "gate_a"), ("gate_b", "up"), ("w_in", "w_out", "spectrum", "small"))
     own = [{}, {}]
     moved = [{}, {}]
     crossed = [{}, {}]
@@ -1049,8 +1072,6 @@
     def hold(m):
         held[m] = [to_holder(t) for t in total[m]]
 
-    small_sum = [None, None]
-    gain_sum = [None, None]
     grads_in = [[], []]
     for index in range(packs):
         last = index == packs - 1
@@ -1071,8 +1092,9 @@
         late_sums = core_sums(after(late_parts, hidden_grad))
         blocks, late_sums = tie(blocks, late_sums)
         late_moved = sent_sums(late_sums)
-        parts, mix_rows, proj_grad, spectrum_grad, tap_grad = mixer_backward(
-            blocks, w_io[1], taps[1:2], cols[index], kept[3], spectra[1], tables, order, places
+        parts, mix_rows, proj_grad, spectrum_grad, tap_grad, gain_one = mixer_backward(
+            blocks, w_io[1], taps[1:2], cols[index], kept[1], gains[1, 0:1], kept[3], spectra[1],
+            tables, order, places,
         )
         parts, late_moved = tie(parts, late_moved)
         if last:
@@ -1089,12 +1111,10 @@
             cross(1, 0)
             cross(1, 1)
             out_sent = deliver(low(jnp.stack(results[0])), low(jnp.stack(results[1])))
-        grad_part, gain_one = kept[0](add_sums(sums_of, moved_sums))
-        state = hidden_grad + grad_part
-        small_sum[1] = add(small_sum[1], tap_grad)
-        gain_sum[1] = add(gain_sum[1], jnp.stack([gain_one, gain_two]))
+        state = hidden_grad + kept[0](add_sums(sums_of, moved_sums))[0]
         grads_in[1].append(state)
-        mix_terms(1, kept, state, mix_rows, proj_grad, spectrum_grad, last)
+        small = small_rows(tap_grad, gain_one, gain_two)
+        mix_terms(1, kept, state, mix_rows, proj_grad, spectrum_grad, small, last)
         if last:
             send_dq(1, 2)
         kept = saved[0][index]
@@ -1121,9 +1141,11 @@
             add_own(1, 2, blocks)
             blocks, own[0][1], own[1][2] = tie(blocks, own[0][1], own[1][2])
             cross(1, 2)
-        parts, mix_rows, proj_grad, spectrum_grad, tap_grad = mixer_backward(
-            blocks, w_io[0], taps[0:1], cols[index], kept[3], spectra[0], tables, order, places
+        parts, mix_rows, proj_grad, spectrum_grad, tap_grad, gain_one = mixer_backward(
+            blocks, w_io[0], taps[0:1], cols[index], kept[1], gains[0, 0:1], kept[3], spectra[0],
+            tables, order, places,
         )
+        small = small_rows(tap_grad, gain_one, gain_two)
         if last:
             parts, moved[0][0], moved[0][1], crossed[1][2] = tie(
                 parts, moved[0][0], moved[0][1], crossed[1][2]
@@ -1131,21 +1153,18 @@
             add_own(0, 0, parts)
             parts, own[0][0] = tie(parts, own[0][0])
             cross(0, 0)
-            mix_terms(0, kept, parts, mix_rows, proj_grad, spectrum_grad, last)
+            mix_terms(0, kept, parts, mix_rows, proj_grad, spectrum_grad, small, last)
             send_dq(0, 2)
             parts, own[0][2] = tie(parts, own[0][2])
         sums_of = core_sums(parts)
         if last:
             add_own(0, 1, sums_of)
         else:
-            mix_terms(0, kept, sums_of, mix_rows, proj_grad, spectrum_grad, last)
+            mix_terms(0, kept, sums_of, mix_rows, proj_grad, spectrum_grad, small, last)
         moved_sums = sent_sums(sums_of)
-        small_sum[0] = add(small_sum[0], tap_grad)
         if last:
             break
-        grad_part, gain_one = kept[0](add_sums(sums_of, moved_sums))
-        grads_in[0].append(hidden_grad + grad_part)
-        gain_sum[0] = add(gain_sum[0], jnp.stack([gain_one, gain_two]))
+        grads_in[0].append(hidden_grad + kept[0](add_sums(sums_of, moved_sums))[0])
 
     line.mark(own[0][1])
     add_total(0, line.events)
@@ -1160,55 +1179,29 @@
         line.mark(terms)
         joined[m] = [join_holders(t) for t in terms]
 
-    grad_part, gain_one = kept[0](add_sums(sums_of, line.take(moved_sums)))
-    state = hidden_grad + grad_part
+    state = hidden_grad + kept[0](add_sums(sums_of, line.take(moved_sums)))[0]
     grads_in[0].append(state)
-    gain_sum[0] = add(gain_sum[0], jnp.stack([gain_one, gain_two]))
     line.mark(state)
-    small = [
-        jnp.concatenate(
-            [jnp.pad(small_sum[k], ((0, 0), (0, width - channels))), gain_sum[k]], axis=0
-        )
-        for k in range(2)
-    ]
-    small_other = swap_section(jnp.where(first, small[1], small[0]))
     add_own(0, 2, line.events)
     cross(0, 2)
     line.mark(own[0][2])
+    grad_sent = deliver(low(jnp.stack(grads_in[0])), low(jnp.stack(grads_in[1])))
+    crossed[0][1], grad_sent = tie(crossed[0][1], grad_sent)
     add_total(1, line.events)
     hold(1)
     line.mark(total[1])
     send_joined(0)
-    mine = jnp.where(first, small[0], small[1]) + line.take(small_other)
-    moved_small = [shift(mine, "dq", k) for k in range(1, lax.axis_size("dq"))]
-    line.mark(mine)
-    add_total(2, line.events)
+    crossed[0][2], held[1] = tie(crossed[0][2], held[1])
+    add_total(2)
     hold(2)
     line.mark(total[2])
-    grad_sent = deliver(
-        *line.take((low(jnp.stack(grads_in[0])), low(jnp.stack(grads_in[1]))))
-    )
-    sum_dq = mine
-    for term in line.take(moved_small):
-        sum_dq = sum_dq + term
-    moved_small = permute(sum_dq, ("th",), lambda h: (1 - h,))
-    line.mark(sum_dq)
-    mine = sum_dq + line.take(moved_small)
-    rows_of = own_taps.shape[0]
-    tap_grads = transposed(mine[:rows_of, :channels])
-    gain_grads = mine[rows_of:]
-    gain_other = swap_core(gain_grads)
-    line.mark(mine)
     send_joined(1)
-    gain_grads = gain_grads + line.take(gain_other)
-    gain_moved = [shift(gain_grads, "tl", k) for k in range(1, peers)]
-    line.mark(gain_grads)
+    held[2], joined[0], joined[1] = tie(held[2], joined[0], joined[1])
+    line.mark(held[2])
+    send_joined(2)
     grad_in = ordered(*line.take(grad_sent))
-    line.mark(grad_in)
-    gain_total = gain_grads
-    for term in line.take(gain_moved):
-        gain_total = gain_total + term
-    line.mark(gain_total)
+
+    small_count = small.shape[0]
 
     def finish_wide(buffers, outs):
         take = row_reader(buffers)
@@ -1222,6 +1215,7 @@
         outs[0][...] = take(3 * channels)
         outs[1][...] = take(channels)
         outs[2][...] = take(2 * channels)[:, :freqs]
+        outs[3][...] = take(small_count)
 
     grad_down, grad_gate_up = assemble(
         line.take(joined[0] + joined[1]),
@@ -1229,15 +1223,27 @@
         finish_wide,
         [(hidden_cols, width), (width, 2, hidden_cols)],
     )
-    line.mark(grad_down)
+    grad_down, joined[2] = tie(grad_down, joined[2])
     send_joined(2)
-    grad_w_in, grad_w_out, grad_spectrum = assemble(
+    grad_w_in, grad_w_out, grad_spectrum, small_total = assemble(
         joined[2],
         places,
         finish_rest,
-        [(3 * channels, width), (channels, width), (2 * channels, freqs)],
+        [
+            (3 * channels, width),
+            (channels, width),
+            (2 * channels, freqs),
+            (small_count, width),
+        ],
     )
     grad_spectrum = grad_spectrum.reshape(2, channels, freqs)
+    rows_of = own_taps.shape[0]
+    tap_grads = small_total[:rows_of, :channels]
+    gain_total = small_total[rows_of : rows_of + 2]
+    gain_total = gain_total + permute(gain_total, ("th",), lambda h: (1 - h,))
+    gain_moved = [shift(gain_total, "tl", k) for k in range(1, peers)]
+    for term in gain_moved:
+        gain_total = gain_total + term
     return (
         layer_out[None],
         grad_in[None],

time: 651 us -> 616 us (0.946)
  waiting for transfers between devices: 248 us -> 226 us
  starting transfers between devices: 150 us -> 137 us
    ppermute x104 -> x100, waiting for transfers between devices: 248 us -> 226 us  [permute(): return lax.ppermute(values, axes if len(axes) > 1 else axes[0], pairs)]
    ppermute x104 -> x100, starting transfers between devices: 150 us -> 137 us  [permute(): return lax.ppermute(values, axes if len(axes) > 1 else axes[0], pairs)]
    unnamed x345 -> x303, local copies, waits for them, and re-layouts: 37.4 us -> 45.7 us
  transfers between devices with their start and end apart: 104 -> 100, of which waited for: 35 -> 37; matrix products, arithmetic and copies ran while one was open for 9% -> 9% of each run, Pallas kernels for 19% -> 19%
where the time goes in v4:
time: 616 us; the launch traced here: 609 us
  waiting for transfers between devices  226 us (37%)
  starting transfers between devices  137 us (22%)
  Pallas kernels  136 us (22%)
  local copies, waits for them, and re-layouts  58 us (9%)
  other arithmetic  38.5 us (6%)
  matrix products  9.75 us (2%)
    ppermute x100, waiting for transfers between devices, permute(): return lax.ppermute(values, axes if len(axes) > 1 else axes[0], pairs)  226 us
    ppermute x100, starting transfers between devices, permute(): return lax.ppermute(values, axes if len(axes) > 1 else axes[0], pairs)  137 us
    pallas_call x2, Pallas kernels, mixer_backward(): pl.pallas_call(partial(mixer_grad_kernel, nb, len(w_in_out)), grid=(size...  55.8 us
    unnamed x303, local copies, waits for them, and re-layouts  45.7 us
    pallas_call x2, Pallas kernels, mixer_forward(): pl.pallas_call(partial(mixer_kernel, nb, len(w_in_out)), grid=(size // FT...  44.4 us
    pallas_call x2, Pallas kernels, glu_backward(): pl.pallas_call(partial(glu_grad_kernel, nb, len(down)), grid=(hidden // t...  12.9 us
    pallas_call x2, Pallas kernels, glu_forward(): pl.pallas_call(partial(glu_kernel, nb, len(down)), grid=(hidden // tile,)...  12.4 us
  transfers between devices with their start and end apart: 100, of which 37 were waited for; matrix products, arithmetic and copies ran while one was open for 9% of the time, Pallas kernels for 19%

profile of v4, /device:TPU:0, one launch (start us, length us, event | category | flops | bytes accessed | tf_op | source)
XLA Modules:
  0.0 608.8 jit_solution(2177109990596214832)
XLA Ops:
  9.7 6.0 collective-permute-start.1
  36.0 12.3 %collective-permute-start.5 = (bf16[176,768]{1,0:T(8,128)(2,1)S(1)}, bf16[176,768]{1,0:T(8,128)(2,1)S(1)}, u32[]{:S(2)}, u32[]{:S(2)}) collective-permute-start(bf16[176,768]{1,0:T(8,128)(2,1)S(1)} %fusion.9.refs_0_), channel_id=1, source_target_pairs={{0,4},{4,0},{1,5},{5,1},{2,6},{6,2},{3,7},{7,3},{8,12},{12,8},{9,1... | collective-permute-start | bytes 811016 | tf_op jit(solution)/shard_map/ppermute | solution.py:41
  56.1 10.4 %collective-permute-start.9 = (bf16[768,768]{1,0:T(8,128)(2,1)}, bf16[768,768]{1,0:T(8,128)(2,1)}, u32[]{:S(2)}, u32[]{:S(2)}) collective-permute-start(bf16[768,768]{1,0:T(8,128)(2,1)} %bitcast.169), channel_id=1, source_target_pairs={{0,0},{2,4},{4,2},{6,6},{1,1},{3,5},{5,3},{7,7},{8,8},{10,12},{12,... | collective-permute-start | bytes 3538952 | tf_op jit(solution)/shard_map/ppermute | solution.py:41
  74.5 5.7 collective-permute-done.15
  96.1 22.2 %mixer_forward.2 = (f32[176,768]{1,0:T(8,128)S(1)}, f32[176,768]{1,0:T(8,128)S(1)}, f32[176,768]{1,0:T(8,128)S(1)}, f32[176,768]{1,0:T(8,128)S(1)}, bf16[4,176,7...) custom-call(s32[4]{0:T(128)S(1)} %pad_add_fusion.1.order, ...), custom_call_target="tpu_custom_call" | custom-call | flops 25999998976 | tf_op jit(solution)/shard_map/mixer_forward/pallas_call | solution.py:332
  121.9 18.7 %collective-permute-start.21 = (f32[176,768]{1,0:T(8,128)S(1)}, f32[176,768]{1,0:T(8,128)S(1)}, u32[]{:S(2)}, u32[]{:S(2)}) collective-permute-start(f32[176,768]{1,0:T(8,128)S(1)} %get-tuple-element.317), channel_id=1, source_target_pairs={{0,4},{4,0},{1,5},{5,1},{2,6},{6,2},{3,7},{7,3},{8,12},{12,8},{9,1... | collective-permute-start | bytes 1622024 | tf_op jit(solution)/shard_map/ppermute | solution.py:41
  145.7 12.4 %collective-permute-done.22 = f32[176,768]{1,0:T(8,128)S(1)} collective-permute-done((f32[176,768]{1,0:T(8,128)S(1)}, f32[176,768]{1,0:T(8,128)S(1)}, u32[]{:S(2)}, u32[]{:S(2)}) %collective-permute-start.22) | collective-permute-done | bytes 540704 | tf_op jit(solution)/shard_map/ppermute | solution.py:41
  160.5 6.4 %collective-permute-done.23.refs_1_ = bf16[176,768]{1,0:T(8,128)(2,1)S(1)} collective-permute-done((bf16[176,768]{1,0:T(8,128)(2,1)S(1)}, bf16[176,768]{1,0:T(8,128)(2,1)S(1)}, u32[]{:S(2)}, u32[]{:S(2)}) %collective-permute-start.23) | collective-permute-done | bytes 270368 | tf_op jit(solution)/shard_map/ppermute | solution.py:41
  167.0 6.3 %collective-permute-done.26.refs_5_.refs_7_ = bf16[768,768]{1,0:T(8,128)(2,1)S(1)} collective-permute-done((bf16[768,768]{1,0:T(8,128)(2,1)S(1)}, bf16[768,768]{1,0:T(8,128)(2,1)S(1)}, u32[]{:S(2)}, u32[]{:S(2)}) %collective-permute-start.26) | collective-permute-done | bytes 1179680 | tf_op jit(solution)/shard_map/ppermute | solution.py:41
  173.3 6.3 %glu_forward.2 = (f32[176,768]{1,0:T(8,128)S(1)}, f32[176,768]{1,0:T(8,128)S(1)}, f32[176,768]{1,0:T(8,128)S(1)}, f32[176,768]{1,0:T(8,128)S(1)}, bf16[704,768]{...) custom-call(s32[2]{0:T(128)S(1)} %pad_add_fusion.places, ...), custom_call_target="tpu_custom_call" | custom-call | flops 8999999488 | tf_op jit(solution)/shard_map/glu_forward/pallas_call | solution.py:626
  186.6 11.8 %collective-permute-done.29 = f32[176,768]{1,0:T(8,128)S(1)} collective-permute-done((f32[176,768]{1,0:T(8,128)S(1)}, f32[176,768]{1,0:T(8,128)S(1)}, u32[]{:S(2)}, u32[]{:S(2)}) %collective-permute-start.29) | collective-permute-done | bytes 540704 | tf_op jit(solution)/shard_map/ppermute | solution.py:41
  199.5 7.3 %collective-permute-done.30.refs_1_ = bf16[176,768]{1,0:T(8,128)(2,1)S(1)} collective-permute-done((bf16[176,768]{1,0:T(8,128)(2,1)S(1)}, bf16[176,768]{1,0:T(8,128)(2,1)S(1)}, u32[]{:S(2)}, u32[]{:S(2)}) %collective-permute-start.30) | collective-permute-done | bytes 270368 | tf_op jit(solution)/shard_map/ppermute | solution.py:41
  212.8 22.2 %mixer_forward.3 = (f32[176,768]{1,0:T(8,128)S(1)}, f32[176,768]{1,0:T(8,128)S(1)}, f32[176,768]{1,0:T(8,128)S(1)}, f32[176,768]{1,0:T(8,128)S(1)}, bf16[4,176,7...) custom-call(s32[4]{0:T(128)S(1)} %pad_add_fusion.1.order, ...), custom_call_target="tpu_custom_call" | custom-call | flops 25999998976 | tf_op jit(solution)/shard_map/mixer_forward/pallas_call | solution.py:332
  242.9 12.0 %collective-permute-done.42.refs_7_.refs_9_ = bf16[384,768]{1,0:T(8,128)(2,1)S(1)} collective-permute-done((bf16[384,768]{1,0:T(8,128)(2,1)S(1)}, bf16[384,768]{1,0:T(8,128)(2,1)S(1)}, u32[]{:S(2)}, u32[]{:S(2)}) %collective-permute-start.42) | collective-permute-done | bytes 589856 | tf_op jit(solution)/shard_map/ppermute | solution.py:41
  257.9 6.0 collective-permute-done.43.refs_1_
  265.5 6.1 glu_forward.3
  274.1 6.8 %glu_backward.2 = (f32[176,768]{1,0:T(8,128)S(1)}, f32[176,768]{1,0:T(8,128)S(1)}, f32[176,768]{1,0:T(8,128)}, f32[176,768]{1,0:T(8,128)S(1)}, bf16[704,768]{1,0...) custom-call(s32[2]{0:T(128)S(1)} %pad_add_fusion.places, bf16[176,768]{1,0:T(8,128)(2,1)S(1)} %bitcast.179, ...), custom_call_target="tpu_custom_call" | custom-call | flops 9500000256 | tf_op jit(solution)/shard_map/glu_backward/pallas_call | solution.py:695
  287.3 13.0 %collective-permute-done.48 = f32[176,768]{1,0:T(8,128)} collective-permute-done((f32[176,768]{1,0:T(8,128)}, f32[176,768]{1,0:T(8,128)}, u32[]{:S(2)}, u32[]{:S(2)}) %collective-permute-start.48) | collective-permute-done | bytes 540704 | tf_op jit(solution)/shard_map/ppermute | solution.py:41
  318.1 28.5 %mixer_backward.2 = (f32[176,768]{1,0:T(8,128)S(1)}, f32[176,768]{1,0:T(8,128)S(1)}, f32[176,768]{1,0:T(8,128)}, f32[176,768]{1,0:T(8,128)}, bf16[4,176,768]{2,1...) custom-call(s32[4]{0:T(128)S(1)} %pad_add_fusion.1.order, ...), custom_call_target="tpu_custom_call" | custom-call | flops 30000001024 | tf_op jit(solution)/shard_map/mixer_backward/pallas_call | solution.py:505
  360.6 9.7 %collective-permute-done.59 = f32[176,768]{1,0:T(8,128)S(1)} collective-permute-done((f32[176,768]{1,0:T(8,128)S(1)}, f32[176,768]{1,0:T(8,128)S(1)}, u32[]{:S(2)}, u32[]{:S(2)}) %collective-permute-start.59) | collective-permute-done | bytes 540704 | tf_op jit(solution)/shard_map/ppermute | solution.py:41
  375.7 7.9 %collective-permute-done.60.refs_1_ = bf16[176,768]{1,0:T(8,128)(2,1)S(1)} collective-permute-done((bf16[176,768]{1,0:T(8,128)(2,1)S(1)}, bf16[176,768]{1,0:T(8,128)(2,1)S(1)}, u32[]{:S(2)}, u32[]{:S(2)}) %collective-permute-start.60) | collective-permute-done | bytes 270368 | tf_op jit(solution)/shard_map/ppermute | solution.py:41
  386.6 6.1 %glu_backward.3 = (f32[176,768]{1,0:T(8,128)S(1)}, f32[176,768]{1,0:T(8,128)S(1)}, f32[176,768]{1,0:T(8,128)S(1)}, f32[176,768]{1,0:T(8,128)S(1)}, bf16[704,768]...) custom-call(s32[2]{0:T(128)S(1)} %pad_add_fusion.places, ...), custom_call_target="tpu_custom_call" | custom-call | flops 9500000256 | tf_op jit(solution)/shard_map/glu_backward/pallas_call | solution.py:695
  394.4 5.4 collective-permute-start.76
  407.4 6.9 %collective-permute-done.66 = f32[176,768]{1,0:T(8,128)S(1)} collective-permute-done((f32[176,768]{1,0:T(8,128)S(1)}, f32[176,768]{1,0:T(8,128)S(1)}, u32[]{:S(2)}, u32[]{:S(2)}) %collective-permute-start.66) | collective-permute-done | bytes 540704 | tf_op jit(solution)/shard_map/ppermute | solution.py:41
  416.2 6.7 %collective-permute-done.68.refs_1_ = bf16[176,768]{1,0:T(8,128)(2,1)S(1)} collective-permute-done((bf16[176,768]{1,0:T(8,128)(2,1)S(1)}, bf16[176,768]{1,0:T(8,128)(2,1)S(1)}, u32[]{:S(2)}, u32[]{:S(2)}) %collective-permute-start.68) | collective-permute-done | bytes 270368 | tf_op jit(solution)/shard_map/ppermute | solution.py:41
  428.3 27.3 %mixer_backward.3 = (f32[176,768]{1,0:T(8,128)S(1)}, f32[176,768]{1,0:T(8,128)S(1)}, f32[176,768]{1,0:T(8,128)S(1)}, f32[176,768]{1,0:T(8,128)S(1)}, bf16[4,176,...) custom-call(s32[4]{0:T(128)S(1)} %pad_add_fusion.1.order, ...), custom_call_target="tpu_custom_call" | custom-call | flops 30000001024 | tf_op jit(solution)/shard_map/mixer_backward/pallas_call | solution.py:505
  471.1 14.0 %collective-permute-done.75 = bf16[576,768]{1,0:T(8,128)(2,1)S(1)} collective-permute-done((bf16[576,768]{1,0:T(8,128)(2,1)S(1)}, bf16[576,768]{1,0:T(8,128)(2,1)S(1)}, u32[]{:S(2)}, u32[]{:S(2)}) %collective-permute-start.75) | collective-permute-done | bytes 884768 | tf_op jit(solution)/shard_map/ppermute | solution.py:41
  494.2 17.6 %collective-permute-done.82 = bf16[1,176,768]{2,1,0:T(8,128)(2,1)S(1)} collective-permute-done((bf16[1,176,768]{2,1,0:T(8,128)(2,1)S(1)}, bf16[1,176,768]{2,1,0:T(8,128)(2,1)S(1)}, u32[]{:S(2)}, u32[]{:S(2)}) %collective-permute-start.82) | collective-permute-done | bytes 270368 | tf_op jit(solution)/shard_map/ppermute | solution.py:41
  518.5 7.8 %collective-permute-done.84 = bf16[608,768]{1,0:T(8,128)(2,1)S(1)} collective-permute-done((bf16[608,768]{1,0:T(8,128)(2,1)S(1)}, bf16[608,768]{1,0:T(8,128)(2,1)S(1)}, u32[]{:S(2)}, u32[]{:S(2)}) %collective-permute-start.84) | collective-permute-done | bytes 933920 | tf_op jit(solution)/shard_map/ppermute | solution.py:41
  526.3 16.2 %collective-permute-done.86 = bf16[576,768]{1,0:T(8,128)(2,1)S(1)} collective-permute-done((bf16[576,768]{1,0:T(8,128)(2,1)S(1)}, bf16[576,768]{1,0:T(8,128)(2,1)S(1)}, u32[]{:S(2)}, u32[]{:S(2)}) %collective-permute-start.86) | collective-permute-done | bytes 884768 | tf_op jit(solution)/shard_map/ppermute | solution.py:41
  551.2 7.2 %collective-permute-done.92.refs_5_ = bf16[576,768]{1,0:T(8,128)(2,1)S(1)} collective-permute-done((bf16[576,768]{1,0:T(8,128)(2,1)S(1)}, bf16[576,768]{1,0:T(8,128)(2,1)S(1)}, u32[]{:S(2)}, u32[]{:S(2)}) %collective-permute-start.92) | collective-permute-done | bytes 884768 | tf_op jit(solution)/shard_map/ppermute | solution.py:41
  569.8 10.4 %collective-permute-done.95.refs_1_ = bf16[608,768]{1,0:T(8,128)(2,1)} collective-permute-done((bf16[608,768]{1,0:T(8,128)(2,1)S(1)}, bf16[608,768]{1,0:T(8,128)(2,1)}, u32[]{:S(2)}, u32[]{:S(2)}) %collective-permute-start.95) | collective-permute-done | bytes 933920 | tf_op jit(solution)/shard_map/ppermute | solution.py:41
  (634 shorter events, 242.0 us)
Async XLA Ops:
  1.5 28.1 %collective-permute-start.3 = (f32[2,768]{1,0:T(2,128)S(1)}, f32[2,768]{1,0:T(2,128)}, u32[]{:S(2)}, u32[]{:S(2)}) collective-permute-start(f32[2,768]{1,0:T(2,128)S(1)} %pad_maximum_fusion.6), channel_id=1, source_target_pairs={{0,16},{16,0},{1,17},{17,1},{2,18},{18,2},{3,19},{19,3},{4,20},{20... | collective-permute-start | bytes 18440 | tf_op jit(solution)/shard_map/ppermute | solution.py:41
  5.8 46.0 %collective-permute-start.16 = (f32[2,704]{1,0:T(2,128)}, f32[2,704]{1,0:T(2,128)}, u32[]{:S(2)}, u32[]{:S(2)}) collective-permute-start(f32[2,704]{1,0:T(2,128)} %convert_element_type.269), channel_id=1, source_target_pairs={{0,4},{4,0},{1,5},{5,1},{2,6},{6,2},{3,7},{7,3},{8,12},{12,8},{9,1... | collective-permute-start | bytes 16904 | tf_op jit(solution)/shard_map/ppermute | solution.py:41
  6.8 23.6 %collective-permute-start = (bf16[1,176,768]{2,1,0:T(8,128)(2,1)S(1)}, bf16[1,176,768]{2,1,0:T(8,128)(2,1)S(1)}, u32[]{:S(2)}, u32[]{:S(2)}) collective-permute-start(bf16[1,176,768]{2,1,0:T(8,128)(2,1)S(1)} %constant_dynamic-slice_fusion.3), channel_id=1, source_target_pairs={{0,0},{2,4},{4,2},{6,6},{1,1},{3,5},{5,3},{7,7},{8,8},{10,12},{12,... | collective-permute-start | bytes 811016 | tf_op jit(solution)/shard_map/ppermute | solution.py:41
  9.7 20.8 %collective-permute-start.1 = (bf16[384,768]{1,0:T(8,128)(2,1)}, bf16[384,768]{1,0:T(8,128)(2,1)}, u32[]{:S(2)}, u32[]{:S(2)}) collective-permute-start(bf16[384,768]{1,0:T(8,128)(2,1)} %fusion.6), channel_id=1, source_target_pairs={{0,0},{2,4},{4,2},{6,6},{1,1},{3,5},{5,3},{7,7},{8,8},{10,12},{12,... | collective-permute-start | bytes 1769480 | tf_op jit(solution)/shard_map/ppermute | solution.py:41
  33.0 33.5 %collective-permute-start.7 = (bf16[384,768]{1,0:T(8,128)(2,1)}, bf16[384,768]{1,0:T(8,128)(2,1)S(1)}, u32[]{:S(2)}, u32[]{:S(2)}) collective-permute-start(bf16[384,768]{1,0:T(8,128)(2,1)} %collective-permute-done.1), channel_id=1, source_target_pairs={{0,16},{16,0},{1,17},{17,1},{2,18},{18,2},{3,19},{19,3},{4,20},{20... | collective-permute-start | bytes 1769480 | tf_op jit(solution)/shard_map/ppermute | solution.py:41
  34.3 32.2 %collective-permute-start.8 = (f32[192,705]{1,0:T(8,128)}, f32[192,705]{1,0:T(8,128)S(1)}, u32[]{:S(2)}, u32[]{:S(2)}) collective-permute-start(f32[192,705]{1,0:T(8,128)} %collective-permute-done.2), channel_id=1, source_target_pairs={{0,16},{16,0},{1,17},{17,1},{2,18},{18,2},{3,19},{19,3},{4,20},{20... | collective-permute-start | bytes 1624328 | tf_op jit(solution)/shard_map/ppermute | solution.py:41
  56.1 24.0 %collective-permute-start.9 = (bf16[768,768]{1,0:T(8,128)(2,1)}, bf16[768,768]{1,0:T(8,128)(2,1)}, u32[]{:S(2)}, u32[]{:S(2)}) collective-permute-start(bf16[768,768]{1,0:T(8,128)(2,1)} %bitcast.169), channel_id=1, source_target_pairs={{0,0},{2,4},{4,2},{6,6},{1,1},{3,5},{5,3},{7,7},{8,8},{10,12},{12,... | collective-permute-start | bytes 3538952 | tf_op jit(solution)/shard_map/ppermute | solution.py:41
  81.5 40.3 %collective-permute-start.18 = (bf16[1,176,768]{2,1,0:T(8,128)(2,1)S(1)}, bf16[1,176,768]{2,1,0:T(8,128)(2,1)S(1)}, u32[]{:S(2)}, u32[]{:S(2)}) collective-permute-start(bf16[1,176,768]{2,1,0:T(8,128)(2,1)S(1)} %copy-done.134), channel_id=1, source_target_pairs={{0,0},{2,4},{4,2},{6,6},{1,1},{3,5},{5,3},{7,7},{8,8},{10,12},{12,... | collective-permute-start | bytes 811016 | tf_op jit(solution)/shard_map/ppermute | solution.py:41
  82.4 39.5 %collective-permute-start.19 = (bf16[384,768]{1,0:T(8,128)(2,1)S(1)}, bf16[384,768]{1,0:T(8,128)(2,1)S(1)}, u32[]{:S(2)}, u32[]{:S(2)}) collective-permute-start(bf16[384,768]{1,0:T(8,128)(2,1)S(1)} %get-tuple-element.319.refs_6_.refs_8_), channel_id=1, source_target_pairs={{0,8},{8,0},{1,9},{9,1},{2,10},{10,2},{3,11},{11,3},{4,12},{12,4},... | collective-permute-start | bytes 1769480 | tf_op jit(solution)/shard_map/ppermute | solution.py:41
  84.0 35.5 %collective-permute-start.17 = (bf16[768,768]{1,0:T(8,128)(2,1)}, bf16[768,768]{1,0:T(8,128)(2,1)S(1)}, u32[]{:S(2)}, u32[]{:S(2)}) collective-permute-start(bf16[768,768]{1,0:T(8,128)(2,1)} %collective-permute-done.9), channel_id=1, source_target_pairs={{0,16},{16,0},{1,17},{17,1},{2,18},{18,2},{3,19},{19,3},{4,20},{20... | collective-permute-start | bytes 3538952 | tf_op jit(solution)/shard_map/ppermute | solution.py:41
  145.3 28.0 %collective-permute-start.26 = (bf16[768,768]{1,0:T(8,128)(2,1)S(1)}, bf16[768,768]{1,0:T(8,128)(2,1)S(1)}, u32[]{:S(2)}, u32[]{:S(2)}) collective-permute-start(bf16[768,768]{1,0:T(8,128)(2,1)S(1)} %get-tuple-element.318.refs_4_.refs_6_), channel_id=1, source_target_pairs={{0,8},{8,0},{1,9},{9,1},{2,10},{10,2},{3,11},{11,3},{4,12},{12,4},... | collective-permute-start | bytes 3538952 | tf_op jit(solution)/shard_map/ppermute | solution.py:41
  184.5 28.2 %collective-permute-start.33 = (bf16[384,768]{1,0:T(8,128)(2,1)S(1)}, bf16[384,768]{1,0:T(8,128)(2,1)S(1)}, u32[]{:S(2)}, u32[]{:S(2)}) collective-permute-start(bf16[384,768]{1,0:T(8,128)(2,1)S(1)} %get-tuple-element.325.refs_4_), channel_id=1, source_target_pairs={{0,8},{8,0},{1,9},{9,1},{2,10},{10,2},{3,11},{11,3},{4,12},{12,4},... | collective-permute-start | bytes 1769480 | tf_op jit(solution)/shard_map/ppermute | solution.py:41
  185.0 27.3 %collective-permute-start.34 = (f32[192,705]{1,0:T(8,128)S(1)}, f32[192,705]{1,0:T(8,128)S(1)}, u32[]{:S(2)}, u32[]{:S(2)}) collective-permute-start(f32[192,705]{1,0:T(8,128)S(1)} %copy-done.6), channel_id=1, source_target_pairs={{0,8},{8,0},{1,9},{9,1},{2,10},{10,2},{3,11},{11,3},{4,12},{12,4},... | collective-permute-start | bytes 1624328 | tf_op jit(solution)/shard_map/ppermute | solution.py:41
  206.8 29.4 %collective-permute-start.35 = (bf16[176,768]{1,0:T(8,128)(2,1)S(1)}, bf16[176,768]{1,0:T(8,128)(2,1)S(1)}, u32[]{:S(2)}, u32[]{:S(2)}) collective-permute-start(bf16[176,768]{1,0:T(8,128)(2,1)S(1)} %bitcast.177), channel_id=1, source_target_pairs={{0,1},{1,0},{2,3},{3,2},{4,5},{5,4},{6,7},{7,6},{8,9},{9,8},{10,11... | collective-permute-start | bytes 811016 | tf_op jit(solution)/shard_map/ppermute | solution.py:41
  212.3 26.9 %collective-permute-start.38 = (bf16[768,768]{1,0:T(8,128)(2,1)S(1)}, bf16[768,768]{1,0:T(8,128)(2,1)S(1)}, u32[]{:S(2)}, u32[]{:S(2)}) collective-permute-start(bf16[768,768]{1,0:T(8,128)(2,1)S(1)} %get-tuple-element.345.refs_4_.refs_6_), channel_id=1, source_target_pairs={{0,8},{8,0},{1,9},{9,1},{2,10},{10,2},{3,11},{11,3},{4,12},{12,4},... | collective-permute-start | bytes 3538952 | tf_op jit(solution)/shard_map/ppermute | solution.py:41
  311.3 38.6 %collective-permute-start.56 = (bf16[576,768]{1,0:T(8,128)(2,1)S(1)}, bf16[576,768]{1,0:T(8,128)(2,1)}, u32[]{:S(2)}, u32[]{:S(2)}) collective-permute-start(bf16[576,768]{1,0:T(8,128)(2,1)S(1)} %dynamic-slice_bitcast_fusion.8), channel_id=1, source_target_pairs={{0,8},{8,0},{1,9},{9,1},{2,10},{10,2},{3,11},{11,3},{4,12},{12,4},... | collective-permute-start | bytes 2654216 | tf_op jit(solution)/shard_map/ppermute | solution.py:41
  314.8 37.4 %collective-permute-start.55 = (bf16[576,768]{1,0:T(8,128)(2,1)S(1)}, bf16[576,768]{1,0:T(8,128)(2,1)}, u32[]{:S(2)}, u32[]{:S(2)}) collective-permute-start(bf16[576,768]{1,0:T(8,128)(2,1)S(1)} %dynamic-slice_bitcast_fusion.9), channel_id=1, source_target_pairs={{0,8},{8,0},{1,9},{9,1},{2,10},{10,2},{3,11},{11,3},{4,12},{12,4},... | collective-permute-start | bytes 2654216 | tf_op jit(solution)/shard_map/ppermute | solution.py:41
  316.3 33.7 %collective-permute-start.54 = (f32[176,768]{1,0:T(8,128)S(1)}, f32[176,768]{1,0:T(8,128)}, u32[]{:S(2)}, u32[]{:S(2)}) collective-permute-start(f32[176,768]{1,0:T(8,128)S(1)} %add.304), channel_id=1, source_target_pairs={{0,1},{1,0},{2,3},{3,2},{4,5},{5,4},{6,7},{7,6},{8,9},{9,8},{10,11... | collective-permute-start | bytes 1622024 | tf_op jit(solution)/shard_map/ppermute | solution.py:41
  394.4 76.7 %collective-permute-start.76 = (bf16[576,768]{1,0:T(8,128)(2,1)}, bf16[576,768]{1,0:T(8,128)(2,1)}, u32[]{:S(2)}, u32[]{:S(2)}) collective-permute-start(bf16[576,768]{1,0:T(8,128)(2,1)} %convert_element_type.313), channel_id=1, source_target_pairs={{0,16},{1,17},{2,18},{3,19},{4,20},{5,21},{6,22},{7,23},{8,24},{9,... | collective-permute-start | bytes 2654216 | tf_op jit(solution)/shard_map/ppermute | solution.py:41
  399.8 24.2 %collective-permute-start.71 = (bf16[608,768]{1,0:T(8,128)(2,1)S(1)}, bf16[608,768]{1,0:T(8,128)(2,1)S(1)}, u32[]{:S(2)}, u32[]{:S(2)}) collective-permute-start(bf16[608,768]{1,0:T(8,128)(2,1)S(1)} %get-tuple-element.632), channel_id=1, source_target_pairs={{0,8},{8,0},{1,9},{9,1},{2,10},{10,2},{3,11},{11,3},{4,12},{12,4},... | collective-permute-start | bytes 2801672 | tf_op jit(solution)/shard_map/ppermute | solution.py:41
  403.2 52.6 %collective-permute-start.72 = (bf16[576,768]{1,0:T(8,128)(2,1)}, bf16[576,768]{1,0:T(8,128)(2,1)S(1)}, u32[]{:S(2)}, u32[]{:S(2)}) collective-permute-start(bf16[576,768]{1,0:T(8,128)(2,1)} %get-tuple-element.636), channel_id=1, source_target_pairs={{0,8},{8,0},{1,9},{9,1},{2,10},{10,2},{3,11},{11,3},{4,12},{12,4},... | collective-permute-start | bytes 2654216 | tf_op jit(solution)/shard_map/ppermute | solution.py:41
  424.0 36.6 %collective-permute-start.73 = (bf16[576,768]{1,0:T(8,128)(2,1)}, bf16[576,768]{1,0:T(8,128)(2,1)}, u32[]{:S(2)}, u32[]{:S(2)}) collective-permute-start(bf16[576,768]{1,0:T(8,128)(2,1)} %get-tuple-element.634), channel_id=1, source_target_pairs={{0,8},{8,0},{1,9},{9,1},{2,10},{10,2},{3,11},{11,3},{4,12},{12,4},... | collective-permute-start | bytes 2654216 | tf_op jit(solution)/shard_map/ppermute | solution.py:41
  425.8 34.8 %collective-permute-start.74 = (bf16[608,768]{1,0:T(8,128)(2,1)S(1)}, bf16[608,768]{1,0:T(8,128)(2,1)S(1)}, u32[]{:S(2)}, u32[]{:S(2)}) collective-permute-start(bf16[608,768]{1,0:T(8,128)(2,1)S(1)} %convert_element_type.309), channel_id=1, source_target_pairs={{0,16},{1,17},{2,18},{3,19},{4,20},{5,21},{6,22},{7,23},{8,24},{9,... | collective-permute-start | bytes 2801672 | tf_op jit(solution)/shard_map/ppermute | solution.py:41
  462.3 22.8 %collective-permute-start.75 = (bf16[576,768]{1,0:T(8,128)(2,1)S(1)}, bf16[576,768]{1,0:T(8,128)(2,1)S(1)}, u32[]{:S(2)}, u32[]{:S(2)}) collective-permute-start(bf16[576,768]{1,0:T(8,128)(2,1)S(1)} %convert_element_type.312), channel_id=1, source_target_pairs={{16,0},{17,1},{18,2},{19,3},{20,4},{21,5},{22,6},{23,7},{24,8},{25... | collective-permute-start | bytes 2654216 | tf_op jit(solution)/shard_map/ppermute | solution.py:41
  464.5 47.3 %collective-permute-start.85 = (bf16[576,768]{1,0:T(8,128)(2,1)S(1)}, bf16[576,768]{1,0:T(8,128)(2,1)S(1)}, u32[]{:S(2)}, u32[]{:S(2)}) collective-permute-start(bf16[576,768]{1,0:T(8,128)(2,1)S(1)} %convert_element_type.324), channel_id=1, source_target_pairs={{0,16},{1,17},{2,18},{3,19},{4,20},{5,21},{6,22},{7,23},{8,24},{9,... | collective-permute-start | bytes 2654216 | tf_op jit(solution)/shard_map/ppermute | solution.py:41
  469.2 22.5 %collective-permute-start.83 = (bf16[608,768]{1,0:T(8,128)(2,1)S(1)}, bf16[608,768]{1,0:T(8,128)(2,1)S(1)}, u32[]{:S(2)}, u32[]{:S(2)}) collective-permute-start(bf16[608,768]{1,0:T(8,128)(2,1)S(1)} %get-tuple-element.630), channel_id=1, source_target_pairs={{0,8},{8,0},{1,9},{9,1},{2,10},{10,2},{3,11},{11,3},{4,12},{12,4},... | collective-permute-start | bytes 2801672 | tf_op jit(solution)/shard_map/ppermute | solution.py:41
  485.7 30.1 %collective-permute-start.88 = (bf16[576,768]{1,0:T(8,128)(2,1)S(1)}, bf16[576,768]{1,0:T(8,128)(2,1)S(1)}, u32[]{:S(2)}, u32[]{:S(2)}) collective-permute-start(bf16[576,768]{1,0:T(8,128)(2,1)S(1)} %convert_element_type.329), channel_id=1, source_target_pairs={{2,0},{4,6},{3,1},{5,7},{10,8},{12,14},{11,9},{13,15},{18,16},{20,... | collective-permute-start | bytes 2654216 | tf_op jit(solution)/shard_map/ppermute | solution.py:41
  487.0 24.8 %collective-permute-start.79 = (bf16[576,768]{1,0:T(8,128)(2,1)S(1)}, bf16[576,768]{1,0:T(8,128)(2,1)S(1)}, u32[]{:S(2)}, u32[]{:S(2)}) collective-permute-start(bf16[576,768]{1,0:T(8,128)(2,1)S(1)} %convert_element_type.319), channel_id=1, source_target_pairs={{16,0},{17,1},{18,2},{19,3},{20,4},{21,5},{22,6},{23,7},{24,8},{25... | collective-permute-start | bytes 2654216 | tf_op jit(solution)/shard_map/ppermute | solution.py:41
  492.9 33.5 %collective-permute-start.84 = (bf16[608,768]{1,0:T(8,128)(2,1)S(1)}, bf16[608,768]{1,0:T(8,128)(2,1)S(1)}, u32[]{:S(2)}, u32[]{:S(2)}) collective-permute-start(bf16[608,768]{1,0:T(8,128)(2,1)S(1)} %fusion.33), channel_id=1, source_target_pairs={{16,0},{17,1},{18,2},{19,3},{20,4},{21,5},{22,6},{23,7},{24,8},{25... | collective-permute-start | bytes 2801672 | tf_op jit(solution)/shard_map/ppermute | solution.py:41
  512.3 30.3 %collective-permute-start.86 = (bf16[576,768]{1,0:T(8,128)(2,1)S(1)}, bf16[576,768]{1,0:T(8,128)(2,1)S(1)}, u32[]{:S(2)}, u32[]{:S(2)}) collective-permute-start(bf16[576,768]{1,0:T(8,128)(2,1)S(1)} %get-tuple-element.600), channel_id=1, source_target_pairs={{2,0},{4,6},{3,1},{5,7},{10,8},{12,14},{11,9},{13,15},{18,16},{20,... | collective-permute-start | bytes 2654216 | tf_op jit(solution)/shard_map/ppermute | solution.py:41
  516.0 32.5 %collective-permute-start.89 = (bf16[576,768]{1,0:T(8,128)(2,1)S(1)}, bf16[576,768]{1,0:T(8,128)(2,1)S(1)}, u32[]{:S(2)}, u32[]{:S(2)}) collective-permute-start(bf16[576,768]{1,0:T(8,128)(2,1)S(1)} %add_convert_fusion.3.refs_0_), channel_id=1, source_target_pairs={{0,8},{6,14},{8,0},{14,6},{1,9},{7,15},{9,1},{15,7},{16,24},{22,30... | collective-permute-start | bytes 2654216 | tf_op jit(solution)/shard_map/ppermute | solution.py:41
  567.5 27.9 %collective-permute-start.96 = (bf16[608,768]{1,0:T(8,128)(2,1)S(1)}, bf16[608,768]{1,0:T(8,128)(2,1)}, u32[]{:S(2)}, u32[]{:S(2)}) collective-permute-start(bf16[608,768]{1,0:T(8,128)(2,1)S(1)} %add_convert_fusion.refs_0_), channel_id=1, source_target_pairs={{0,4},{6,2},{1,5},{7,3},{8,12},{14,10},{9,13},{15,11},{16,20},{22,... | collective-permute-start | bytes 2801672 | tf_op jit(solution)/shard_map/ppermute | solution.py:41
  (218 other events, 2265.1 us)

commit v5 on v4

--- a/solution.py
+++ b/solution.py
@@ -321,7 +321,7 @@
     ]
 
 
-def mixer_forward(blocks, w_in_out, taps, cols, spectra, tables, order, places):
+def mixer_forward(blocks, w_in_out, taps, cols, spectra, tables, order, places, mib):
     layer = 0
     pack_len = cols.shape[0]
     nb = len(blocks)
@@ -362,7 +362,7 @@
             pltpu.VMEM((pack_len, width), f32),
         ]
         + part_scratch(w_in_out, spectra),
-        compiler_params=pltpu.CompilerParams(vmem_limit_bytes=36 * MIB),
+        compiler_params=pltpu.CompilerParams(vmem_limit_bytes=mib * MIB),
         cost_estimate=pl.CostEstimate(flops=int(26 * PEAK), bytes_accessed=0, transcendentals=0),
         name="mixer_forward",
     )(order, places, *blocks, *w_in_out, *spectra, taps, cols, *tables, *tables)
@@ -947,7 +947,7 @@
                 down[0] = join_parts(dn_first)
             parts, gathered, mix, kept = mixer_forward(
                 blocks, w_io[layer], taps[layer : layer + 1], cols[index], spectra[layer], tables,
-                order, places,
+                order, places, 56 if opening else 36,
             )
             if opening:
                 gu_both = by_layer(gu_part, after(gu_other, parts))

time: 616 us -> 613 us (level)
  local copies, waits for them, and re-layouts: 58 us -> 48.2 us
    unnamed x303 -> x299, local copies, waits for them, and re-layouts: 45.7 us -> 34.4 us
  transfers between devices with their start and end apart: 100 -> 100, of which waited for: 37 -> 37; matrix products, arithmetic and copies ran while one was open for 9% -> 10% of each run, Pallas kernels for 19% -> 20%
where the time goes in v5:
time: 613 us; the launch traced here: 606 us
  waiting for transfers between devices  223 us (36%)
  starting transfers between devices  141 us (23%)
  Pallas kernels  140 us (23%)
  local copies, waits for them, and re-layouts  48.2 us (8%)
  other arithmetic  40.1 us (7%)
  matrix products  9.79 us (2%)
    ppermute x100, waiting for transfers between devices, permute(): return lax.ppermute(values, axes if len(axes) > 1 else axes[0], pairs)  223 us
    ppermute x100, starting transfers between devices, permute(): return lax.ppermute(values, axes if len(axes) > 1 else axes[0], pairs)  141 us
    pallas_call x2, Pallas kernels, mixer_backward(): pl.pallas_call(partial(mixer_grad_kernel, nb, len(w_in_out)), grid=(size...  55.6 us
    pallas_call x2, Pallas kernels, mixer_forward(): pl.pallas_call(partial(mixer_kernel, nb, len(w_in_out)), grid=(size // FT...  48.8 us
    unnamed x299, local copies, waits for them, and re-layouts  34.4 us
    pallas_call x2, Pallas kernels, glu_backward(): pl.pallas_call(partial(glu_grad_kernel, nb, len(down)), grid=(hidden // t...  12.9 us
    pallas_call x2, Pallas kernels, glu_forward(): pl.pallas_call(partial(glu_kernel, nb, len(down)), grid=(hidden // tile,)...  12.4 us
  transfers between devices with their start and end apart: 100, of which 37 were waited for; matrix products, arithmetic and copies ran while one was open for 10% of the time, Pallas kernels for 20%

profile of v5, /device:TPU:0, one launch (start us, length us, event | category | flops | bytes accessed | tf_op | source)
XLA Modules:
  0.0 605.9 jit_solution(18081771758790011642)
XLA Ops:
  14.4 6.0 collective-permute-start.2
  37.8 11.1 %collective-permute-start.5 = (bf16[176,768]{1,0:T(8,128)(2,1)S(1)}, bf16[176,768]{1,0:T(8,128)(2,1)S(1)}, u32[]{:S(2)}, u32[]{:S(2)}) collective-permute-start(bf16[176,768]{1,0:T(8,128)(2,1)S(1)} %fusion.9.refs_0_), channel_id=1, source_target_pairs={{0,4},{4,0},{1,5},{5,1},{2,6},{6,2},{3,7},{7,3},{8,12},{12,8},{9,1... | collective-permute-start | bytes 811016 | tf_op jit(solution)/shard_map/ppermute | solution.py:41
  53.8 10.4 %collective-permute-start.9 = (bf16[768,768]{1,0:T(8,128)(2,1)}, bf16[768,768]{1,0:T(8,128)(2,1)}, u32[]{:S(2)}, u32[]{:S(2)}) collective-permute-start(bf16[768,768]{1,0:T(8,128)(2,1)} %bitcast.169), channel_id=1, source_target_pairs={{0,0},{2,4},{4,2},{6,6},{1,1},{3,5},{5,3},{7,7},{8,8},{10,12},{12,... | collective-permute-start | bytes 3538952 | tf_op jit(solution)/shard_map/ppermute | solution.py:41
  86.5 26.6 %mixer_forward.2 = (f32[176,768]{1,0:T(8,128)}, f32[176,768]{1,0:T(8,128)}, f32[176,768]{1,0:T(8,128)}, f32[176,768]{1,0:T(8,128)}, bf16[4,176,768]{2,1,0:T(8,12...) custom-call(s32[4]{0:T(128)} %pad_add_fusion.1.order, ...), custom_call_target="tpu_custom_call" | custom-call | flops 25999998976 | tf_op jit(solution)/shard_map/mixer_forward/pallas_call | solution.py:332
  114.8 19.6 %collective-permute-start.21 = (f32[176,768]{1,0:T(8,128)S(1)}, f32[176,768]{1,0:T(8,128)S(1)}, u32[]{:S(2)}, u32[]{:S(2)}) collective-permute-start(f32[176,768]{1,0:T(8,128)S(1)} %copy-done.145), channel_id=1, source_target_pairs={{0,4},{4,0},{1,5},{5,1},{2,6},{6,2},{3,7},{7,3},{8,12},{12,8},{9,1... | collective-permute-start | bytes 1622024 | tf_op jit(solution)/shard_map/ppermute | solution.py:41
  140.5 12.3 %collective-permute-done.22 = f32[176,768]{1,0:T(8,128)S(1)} collective-permute-done((f32[176,768]{1,0:T(8,128)S(1)}, f32[176,768]{1,0:T(8,128)S(1)}, u32[]{:S(2)}, u32[]{:S(2)}) %collective-permute-start.22) | collective-permute-done | bytes 540704 | tf_op jit(solution)/shard_map/ppermute | solution.py:41
  155.2 6.4 %collective-permute-done.23.refs_1_ = bf16[176,768]{1,0:T(8,128)(2,1)S(1)} collective-permute-done((bf16[176,768]{1,0:T(8,128)(2,1)S(1)}, bf16[176,768]{1,0:T(8,128)(2,1)S(1)}, u32[]{:S(2)}, u32[]{:S(2)}) %collective-permute-start.23) | collective-permute-done | bytes 270368 | tf_op jit(solution)/shard_map/ppermute | solution.py:41
  161.7 6.3 %collective-permute-done.26.refs_5_.refs_7_ = bf16[768,768]{1,0:T(8,128)(2,1)S(1)} collective-permute-done((bf16[768,768]{1,0:T(8,128)(2,1)S(1)}, bf16[768,768]{1,0:T(8,128)(2,1)S(1)}, u32[]{:S(2)}, u32[]{:S(2)}) %collective-permute-start.26) | collective-permute-done | bytes 1179680 | tf_op jit(solution)/shard_map/ppermute | solution.py:41
  168.0 6.3 %glu_forward.2 = (f32[176,768]{1,0:T(8,128)S(1)}, f32[176,768]{1,0:T(8,128)S(1)}, f32[176,768]{1,0:T(8,128)S(1)}, f32[176,768]{1,0:T(8,128)S(1)}, bf16[704,768]{...) custom-call(s32[2]{0:T(128)S(1)} %copy-done.64, ...), custom_call_target="tpu_custom_call" | custom-call | flops 8999999488 | tf_op jit(solution)/shard_map/glu_forward/pallas_call | solution.py:626
  180.2 11.8 %collective-permute-done.29 = f32[176,768]{1,0:T(8,128)S(1)} collective-permute-done((f32[176,768]{1,0:T(8,128)S(1)}, f32[176,768]{1,0:T(8,128)S(1)}, u32[]{:S(2)}, u32[]{:S(2)}) %collective-permute-start.29) | collective-permute-done | bytes 540704 | tf_op jit(solution)/shard_map/ppermute | solution.py:41
  193.2 7.3 %collective-permute-done.30.refs_1_ = bf16[176,768]{1,0:T(8,128)(2,1)S(1)} collective-permute-done((bf16[176,768]{1,0:T(8,128)(2,1)S(1)}, bf16[176,768]{1,0:T(8,128)(2,1)S(1)}, u32[]{:S(2)}, u32[]{:S(2)}) %collective-permute-start.30) | collective-permute-done | bytes 270368 | tf_op jit(solution)/shard_map/ppermute | solution.py:41
  206.5 22.2 %mixer_forward.3 = (f32[176,768]{1,0:T(8,128)S(1)}, f32[176,768]{1,0:T(8,128)S(1)}, f32[176,768]{1,0:T(8,128)S(1)}, f32[176,768]{1,0:T(8,128)S(1)}, bf16[4,176,7...) custom-call(s32[4]{0:T(128)S(1)} %copy-done.25, ...), custom_call_target="tpu_custom_call" | custom-call | flops 25999998976 | tf_op jit(solution)/shard_map/mixer_forward/pallas_call | solution.py:332
  236.6 12.0 %collective-permute-done.42.refs_7_.refs_9_ = bf16[384,768]{1,0:T(8,128)(2,1)S(1)} collective-permute-done((bf16[384,768]{1,0:T(8,128)(2,1)S(1)}, bf16[384,768]{1,0:T(8,128)(2,1)S(1)}, u32[]{:S(2)}, u32[]{:S(2)}) %collective-permute-start.42) | collective-permute-done | bytes 589856 | tf_op jit(solution)/shard_map/ppermute | solution.py:41
  251.6 6.0 collective-permute-done.43.refs_1_
  259.1 6.1 %glu_forward.3 = (f32[176,768]{1,0:T(8,128)S(1)}, f32[176,768]{1,0:T(8,128)S(1)}, f32[176,768]{1,0:T(8,128)S(1)}, f32[176,768]{1,0:T(8,128)S(1)}, bf16[704,768]{...) custom-call(s32[2]{0:T(128)S(1)} %copy-done.64, ...), custom_call_target="tpu_custom_call" | custom-call | flops 8999999488 | tf_op jit(solution)/shard_map/glu_forward/pallas_call | solution.py:626
  267.9 6.8 %glu_backward.2 = (f32[176,768]{1,0:T(8,128)S(1)}, f32[176,768]{1,0:T(8,128)S(1)}, f32[176,768]{1,0:T(8,128)}, f32[176,768]{1,0:T(8,128)S(1)}, bf16[704,768]{1,0...) custom-call(s32[2]{0:T(128)S(1)} %copy-done.64, bf16[176,768]{1,0:T(8,128)(2,1)S(1)} %bitcast.178, ...), custom_call_target="tpu_custom_call" | custom-call | flops 9500000256 | tf_op jit(solution)/shard_map/glu_backward/pallas_call | solution.py:695
  281.2 13.0 %collective-permute-done.48 = f32[176,768]{1,0:T(8,128)} collective-permute-done((f32[176,768]{1,0:T(8,128)}, f32[176,768]{1,0:T(8,128)}, u32[]{:S(2)}, u32[]{:S(2)}) %collective-permute-start.48) | collective-permute-done | bytes 540704 | tf_op jit(solution)/shard_map/ppermute | solution.py:41
  311.8 28.5 %mixer_backward.2 = (f32[176,768]{1,0:T(8,128)S(1)}, f32[176,768]{1,0:T(8,128)S(1)}, f32[176,768]{1,0:T(8,128)}, f32[176,768]{1,0:T(8,128)}, bf16[4,176,768]{2,1...) custom-call(s32[4]{0:T(128)S(1)} %copy-done.25, ...), custom_call_target="tpu_custom_call" | custom-call | flops 30000001024 | tf_op jit(solution)/shard_map/mixer_backward/pallas_call | solution.py:505
  354.5 9.6 %collective-permute-done.59 = f32[176,768]{1,0:T(8,128)S(1)} collective-permute-done((f32[176,768]{1,0:T(8,128)S(1)}, f32[176,768]{1,0:T(8,128)S(1)}, u32[]{:S(2)}, u32[]{:S(2)}) %collective-permute-start.59) | collective-permute-done | bytes 540704 | tf_op jit(solution)/shard_map/ppermute | solution.py:41
  369.6 7.9 %collective-permute-done.60.refs_1_ = bf16[176,768]{1,0:T(8,128)(2,1)S(1)} collective-permute-done((bf16[176,768]{1,0:T(8,128)(2,1)S(1)}, bf16[176,768]{1,0:T(8,128)(2,1)S(1)}, u32[]{:S(2)}, u32[]{:S(2)}) %collective-permute-start.60) | collective-permute-done | bytes 270368 | tf_op jit(solution)/shard_map/ppermute | solution.py:41
  380.5 6.1 %glu_backward.3 = (f32[176,768]{1,0:T(8,128)S(1)}, f32[176,768]{1,0:T(8,128)S(1)}, f32[176,768]{1,0:T(8,128)S(1)}, f32[176,768]{1,0:T(8,128)S(1)}, bf16[704,768]...) custom-call(s32[2]{0:T(128)S(1)} %copy-done.64, ...), custom_call_target="tpu_custom_call" | custom-call | flops 9500000256 | tf_op jit(solution)/shard_map/glu_backward/pallas_call | solution.py:695
  388.3 5.4 collective-permute-start.76
  401.3 7.2 %collective-permute-done.66 = f32[176,768]{1,0:T(8,128)S(1)} collective-permute-done((f32[176,768]{1,0:T(8,128)S(1)}, f32[176,768]{1,0:T(8,128)S(1)}, u32[]{:S(2)}, u32[]{:S(2)}) %collective-permute-start.66) | collective-permute-done | bytes 540704 | tf_op jit(solution)/shard_map/ppermute | solution.py:41
  410.3 6.4 %collective-permute-done.68.refs_1_ = bf16[176,768]{1,0:T(8,128)(2,1)S(1)} collective-permute-done((bf16[176,768]{1,0:T(8,128)(2,1)S(1)}, bf16[176,768]{1,0:T(8,128)(2,1)S(1)}, u32[]{:S(2)}, u32[]{:S(2)}) %collective-permute-start.68) | collective-permute-done | bytes 270368 | tf_op jit(solution)/shard_map/ppermute | solution.py:41
  422.2 27.0 %mixer_backward.3 = (f32[176,768]{1,0:T(8,128)S(1)}, f32[176,768]{1,0:T(8,128)S(1)}, f32[176,768]{1,0:T(8,128)S(1)}, f32[176,768]{1,0:T(8,128)S(1)}, bf16[4,176,...) custom-call(s32[4]{0:T(128)S(1)} %copy-done.25, ...), custom_call_target="tpu_custom_call" | custom-call | flops 30000001024 | tf_op jit(solution)/shard_map/mixer_backward/pallas_call | solution.py:505
  449.4 5.1 collective-permute-done.73
  466.8 13.7 %collective-permute-done.75 = bf16[576,768]{1,0:T(8,128)(2,1)S(1)} collective-permute-done((bf16[576,768]{1,0:T(8,128)(2,1)S(1)}, bf16[576,768]{1,0:T(8,128)(2,1)S(1)}, u32[]{:S(2)}, u32[]{:S(2)}) %collective-permute-start.75) | collective-permute-done | bytes 884768 | tf_op jit(solution)/shard_map/ppermute | solution.py:41
  490.4 17.0 %collective-permute-done.82 = bf16[1,176,768]{2,1,0:T(8,128)(2,1)S(1)} collective-permute-done((bf16[1,176,768]{2,1,0:T(8,128)(2,1)S(1)}, bf16[1,176,768]{2,1,0:T(8,128)(2,1)S(1)}, u32[]{:S(2)}, u32[]{:S(2)}) %collective-permute-start.82) | collective-permute-done | bytes 270368 | tf_op jit(solution)/shard_map/ppermute | solution.py:41
  514.0 7.8 %collective-permute-done.84 = bf16[608,768]{1,0:T(8,128)(2,1)S(1)} collective-permute-done((bf16[608,768]{1,0:T(8,128)(2,1)S(1)}, bf16[608,768]{1,0:T(8,128)(2,1)S(1)}, u32[]{:S(2)}, u32[]{:S(2)}) %collective-permute-start.84) | collective-permute-done | bytes 933920 | tf_op jit(solution)/shard_map/ppermute | solution.py:41
  521.8 17.1 %collective-permute-done.86 = bf16[576,768]{1,0:T(8,128)(2,1)S(1)} collective-permute-done((bf16[576,768]{1,0:T(8,128)(2,1)S(1)}, bf16[576,768]{1,0:T(8,128)(2,1)S(1)}, u32[]{:S(2)}, u32[]{:S(2)}) %collective-permute-start.86) | collective-permute-done | bytes 884768 | tf_op jit(solution)/shard_map/ppermute | solution.py:41
  547.5 7.1 %collective-permute-done.92.refs_5_ = bf16[576,768]{1,0:T(8,128)(2,1)S(1)} collective-permute-done((bf16[576,768]{1,0:T(8,128)(2,1)S(1)}, bf16[576,768]{1,0:T(8,128)(2,1)S(1)}, u32[]{:S(2)}, u32[]{:S(2)}) %collective-permute-start.92) | collective-permute-done | bytes 884768 | tf_op jit(solution)/shard_map/ppermute | solution.py:41
  566.0 10.4 %collective-permute-done.95.refs_1_ = bf16[608,768]{1,0:T(8,128)(2,1)} collective-permute-done((bf16[608,768]{1,0:T(8,128)(2,1)S(1)}, bf16[608,768]{1,0:T(8,128)(2,1)}, u32[]{:S(2)}, u32[]{:S(2)}) %collective-permute-start.95) | collective-permute-done | bytes 933920 | tf_op jit(solution)/shard_map/ppermute | solution.py:41
  (630 shorter events, 236.2 us)
Async XLA Ops:
  1.5 30.4 %collective-permute-start.3 = (f32[2,768]{1,0:T(2,128)S(1)}, f32[2,768]{1,0:T(2,128)S(1)}, u32[]{:S(2)}, u32[]{:S(2)}) collective-permute-start(f32[2,768]{1,0:T(2,128)S(1)} %pad_maximum_fusion.6), channel_id=1, source_target_pairs={{0,16},{16,0},{1,17},{17,1},{2,18},{18,2},{3,19},{19,3},{4,20},{20... | collective-permute-start | bytes 18440 | tf_op jit(solution)/shard_map/ppermute | solution.py:41
  5.2 46.3 %collective-permute-start.16 = (f32[2,704]{1,0:T(2,128)S(1)}, f32[2,704]{1,0:T(2,128)S(1)}, u32[]{:S(2)}, u32[]{:S(2)}) collective-permute-start(f32[2,704]{1,0:T(2,128)S(1)} %convert_element_type.269), channel_id=1, source_target_pairs={{0,4},{4,0},{1,5},{5,1},{2,6},{6,2},{3,7},{7,3},{8,12},{12,8},{9,1... | collective-permute-start | bytes 16904 | tf_op jit(solution)/shard_map/ppermute | solution.py:41
  6.9 25.1 %collective-permute-start = (bf16[1,176,768]{2,1,0:T(8,128)(2,1)}, bf16[1,176,768]{2,1,0:T(8,128)(2,1)S(1)}, u32[]{:S(2)}, u32[]{:S(2)}) collective-permute-start(bf16[1,176,768]{2,1,0:T(8,128)(2,1)} %constant_dynamic-slice_fusion.3), channel_id=1, source_target_pairs={{0,0},{2,4},{4,2},{6,6},{1,1},{3,5},{5,3},{7,7},{8,8},{10,12},{12,... | collective-permute-start | bytes 811016 | tf_op jit(solution)/shard_map/ppermute | solution.py:41
  10.7 21.3 %collective-permute-start.1 = (bf16[384,768]{1,0:T(8,128)(2,1)}, bf16[384,768]{1,0:T(8,128)(2,1)S(1)}, u32[]{:S(2)}, u32[]{:S(2)}) collective-permute-start(bf16[384,768]{1,0:T(8,128)(2,1)} %fusion.6), channel_id=1, source_target_pairs={{0,0},{2,4},{4,2},{6,6},{1,1},{3,5},{5,3},{7,7},{8,8},{10,12},{12,... | collective-permute-start | bytes 1769480 | tf_op jit(solution)/shard_map/ppermute | solution.py:41
  34.3 29.9 %collective-permute-start.7 = (bf16[384,768]{1,0:T(8,128)(2,1)S(1)}, bf16[384,768]{1,0:T(8,128)(2,1)S(1)}, u32[]{:S(2)}, u32[]{:S(2)}) collective-permute-start(bf16[384,768]{1,0:T(8,128)(2,1)S(1)} %collective-permute-done.1), channel_id=1, source_target_pairs={{0,16},{16,0},{1,17},{17,1},{2,18},{18,2},{3,19},{19,3},{4,20},{20... | collective-permute-start | bytes 1769480 | tf_op jit(solution)/shard_map/ppermute | solution.py:41
  34.9 29.2 %collective-permute-start.8 = (f32[192,705]{1,0:T(8,128)}, f32[192,705]{1,0:T(8,128)S(1)}, u32[]{:S(2)}, u32[]{:S(2)}) collective-permute-start(f32[192,705]{1,0:T(8,128)} %collective-permute-done.2), channel_id=1, source_target_pairs={{0,16},{16,0},{1,17},{17,1},{2,18},{18,2},{3,19},{19,3},{4,20},{20... | collective-permute-start | bytes 1624328 | tf_op jit(solution)/shard_map/ppermute | solution.py:41
  53.8 24.4 %collective-permute-start.9 = (bf16[768,768]{1,0:T(8,128)(2,1)}, bf16[768,768]{1,0:T(8,128)(2,1)}, u32[]{:S(2)}, u32[]{:S(2)}) collective-permute-start(bf16[768,768]{1,0:T(8,128)(2,1)} %bitcast.169), channel_id=1, source_target_pairs={{0,0},{2,4},{4,2},{6,6},{1,1},{3,5},{5,3},{7,7},{8,8},{10,12},{12,... | collective-permute-start | bytes 3538952 | tf_op jit(solution)/shard_map/ppermute | solution.py:41
  79.5 35.2 %collective-permute-start.18 = (bf16[1,176,768]{2,1,0:T(8,128)(2,1)S(1)}, bf16[1,176,768]{2,1,0:T(8,128)(2,1)S(1)}, u32[]{:S(2)}, u32[]{:S(2)}) collective-permute-start(bf16[1,176,768]{2,1,0:T(8,128)(2,1)S(1)} %constant_dynamic-slice_fusion), channel_id=1, source_target_pairs={{0,0},{2,4},{4,2},{6,6},{1,1},{3,5},{5,3},{7,7},{8,8},{10,12},{12,... | collective-permute-start | bytes 811016 | tf_op jit(solution)/shard_map/ppermute | solution.py:41
  80.4 34.4 %collective-permute-start.19 = (bf16[384,768]{1,0:T(8,128)(2,1)S(1)}, bf16[384,768]{1,0:T(8,128)(2,1)S(1)}, u32[]{:S(2)}, u32[]{:S(2)}) collective-permute-start(bf16[384,768]{1,0:T(8,128)(2,1)S(1)} %get-tuple-element.319.refs_6_.refs_8_), channel_id=1, source_target_pairs={{0,8},{8,0},{1,9},{9,1},{2,10},{10,2},{3,11},{11,3},{4,12},{12,4},... | collective-permute-start | bytes 1769480 | tf_op jit(solution)/shard_map/ppermute | solution.py:41
  82.0 31.2 %collective-permute-start.17 = (bf16[768,768]{1,0:T(8,128)(2,1)}, bf16[768,768]{1,0:T(8,128)(2,1)S(1)}, u32[]{:S(2)}, u32[]{:S(2)}) collective-permute-start(bf16[768,768]{1,0:T(8,128)(2,1)} %collective-permute-done.9), channel_id=1, source_target_pairs={{0,16},{16,0},{1,17},{17,1},{2,18},{18,2},{3,19},{19,3},{4,20},{20... | collective-permute-start | bytes 3538952 | tf_op jit(solution)/shard_map/ppermute | solution.py:41
  140.0 28.0 %collective-permute-start.26 = (bf16[768,768]{1,0:T(8,128)(2,1)S(1)}, bf16[768,768]{1,0:T(8,128)(2,1)S(1)}, u32[]{:S(2)}, u32[]{:S(2)}) collective-permute-start(bf16[768,768]{1,0:T(8,128)(2,1)S(1)} %get-tuple-element.318.refs_4_.refs_6_), channel_id=1, source_target_pairs={{0,8},{8,0},{1,9},{9,1},{2,10},{10,2},{3,11},{11,3},{4,12},{12,4},... | collective-permute-start | bytes 3538952 | tf_op jit(solution)/shard_map/ppermute | solution.py:41
  178.2 28.3 %collective-permute-start.33 = (bf16[384,768]{1,0:T(8,128)(2,1)S(1)}, bf16[384,768]{1,0:T(8,128)(2,1)S(1)}, u32[]{:S(2)}, u32[]{:S(2)}) collective-permute-start(bf16[384,768]{1,0:T(8,128)(2,1)S(1)} %copy-done.8), channel_id=1, source_target_pairs={{0,8},{8,0},{1,9},{9,1},{2,10},{10,2},{3,11},{11,3},{4,12},{12,4},... | collective-permute-start | bytes 1769480 | tf_op jit(solution)/shard_map/ppermute | solution.py:41
  178.7 27.2 %collective-permute-start.34 = (f32[192,705]{1,0:T(8,128)S(1)}, f32[192,705]{1,0:T(8,128)S(1)}, u32[]{:S(2)}, u32[]{:S(2)}) collective-permute-start(f32[192,705]{1,0:T(8,128)S(1)} %copy-done.9), channel_id=1, source_target_pairs={{0,8},{8,0},{1,9},{9,1},{2,10},{10,2},{3,11},{11,3},{4,12},{12,4},... | collective-permute-start | bytes 1624328 | tf_op jit(solution)/shard_map/ppermute | solution.py:41
  200.6 29.4 %collective-permute-start.35 = (bf16[176,768]{1,0:T(8,128)(2,1)S(1)}, bf16[176,768]{1,0:T(8,128)(2,1)S(1)}, u32[]{:S(2)}, u32[]{:S(2)}) collective-permute-start(bf16[176,768]{1,0:T(8,128)(2,1)S(1)} %bitcast.176), channel_id=1, source_target_pairs={{0,1},{1,0},{2,3},{3,2},{4,5},{5,4},{6,7},{7,6},{8,9},{9,8},{10,11... | collective-permute-start | bytes 811016 | tf_op jit(solution)/shard_map/ppermute | solution.py:41
  205.9 26.9 %collective-permute-start.38 = (bf16[768,768]{1,0:T(8,128)(2,1)S(1)}, bf16[768,768]{1,0:T(8,128)(2,1)S(1)}, u32[]{:S(2)}, u32[]{:S(2)}) collective-permute-start(bf16[768,768]{1,0:T(8,128)(2,1)S(1)} %get-tuple-element.345.refs_4_.refs_6_), channel_id=1, source_target_pairs={{0,8},{8,0},{1,9},{9,1},{2,10},{10,2},{3,11},{11,3},{4,12},{12,4},... | collective-permute-start | bytes 3538952 | tf_op jit(solution)/shard_map/ppermute | solution.py:41
  305.2 38.5 %collective-permute-start.56 = (bf16[576,768]{1,0:T(8,128)(2,1)S(1)}, bf16[576,768]{1,0:T(8,128)(2,1)}, u32[]{:S(2)}, u32[]{:S(2)}) collective-permute-start(bf16[576,768]{1,0:T(8,128)(2,1)S(1)} %dynamic-slice_bitcast_fusion.8), channel_id=1, source_target_pairs={{0,8},{8,0},{1,9},{9,1},{2,10},{10,2},{3,11},{11,3},{4,12},{12,4},... | collective-permute-start | bytes 2654216 | tf_op jit(solution)/shard_map/ppermute | solution.py:41
  307.5 38.5 %collective-permute-start.55 = (bf16[576,768]{1,0:T(8,128)(2,1)S(1)}, bf16[576,768]{1,0:T(8,128)(2,1)}, u32[]{:S(2)}, u32[]{:S(2)}) collective-permute-start(bf16[576,768]{1,0:T(8,128)(2,1)S(1)} %dynamic-slice_bitcast_fusion.9), channel_id=1, source_target_pairs={{0,8},{8,0},{1,9},{9,1},{2,10},{10,2},{3,11},{11,3},{4,12},{12,4},... | collective-permute-start | bytes 2654216 | tf_op jit(solution)/shard_map/ppermute | solution.py:41
  310.0 33.7 %collective-permute-start.54 = (f32[176,768]{1,0:T(8,128)S(1)}, f32[176,768]{1,0:T(8,128)}, u32[]{:S(2)}, u32[]{:S(2)}) collective-permute-start(f32[176,768]{1,0:T(8,128)S(1)} %add.304), channel_id=1, source_target_pairs={{0,1},{1,0},{2,3},{3,2},{4,5},{5,4},{6,7},{7,6},{8,9},{9,8},{10,11... | collective-permute-start | bytes 1622024 | tf_op jit(solution)/shard_map/ppermute | solution.py:41
  388.3 78.5 %collective-permute-start.76 = (bf16[576,768]{1,0:T(8,128)(2,1)}, bf16[576,768]{1,0:T(8,128)(2,1)}, u32[]{:S(2)}, u32[]{:S(2)}) collective-permute-start(bf16[576,768]{1,0:T(8,128)(2,1)} %convert_element_type.313), channel_id=1, source_target_pairs={{0,16},{1,17},{2,18},{3,19},{4,20},{5,21},{6,22},{7,23},{8,24},{9,... | collective-permute-start | bytes 2654216 | tf_op jit(solution)/shard_map/ppermute | solution.py:41
  393.7 24.2 %collective-permute-start.71 = (bf16[608,768]{1,0:T(8,128)(2,1)S(1)}, bf16[608,768]{1,0:T(8,128)(2,1)S(1)}, u32[]{:S(2)}, u32[]{:S(2)}) collective-permute-start(bf16[608,768]{1,0:T(8,128)(2,1)S(1)} %get-tuple-element.632), channel_id=1, source_target_pairs={{0,8},{8,0},{1,9},{9,1},{2,10},{10,2},{3,11},{11,3},{4,12},{12,4},... | collective-permute-start | bytes 2801672 | tf_op jit(solution)/shard_map/ppermute | solution.py:41
  397.5 51.8 %collective-permute-start.72 = (bf16[576,768]{1,0:T(8,128)(2,1)}, bf16[576,768]{1,0:T(8,128)(2,1)}, u32[]{:S(2)}, u32[]{:S(2)}) collective-permute-start(bf16[576,768]{1,0:T(8,128)(2,1)} %get-tuple-element.636), channel_id=1, source_target_pairs={{0,8},{8,0},{1,9},{9,1},{2,10},{10,2},{3,11},{11,3},{4,12},{12,4},... | collective-permute-start | bytes 2654216 | tf_op jit(solution)/shard_map/ppermute | solution.py:41
  417.9 36.6 %collective-permute-start.73 = (bf16[576,768]{1,0:T(8,128)(2,1)}, bf16[576,768]{1,0:T(8,128)(2,1)}, u32[]{:S(2)}, u32[]{:S(2)}) collective-permute-start(bf16[576,768]{1,0:T(8,128)(2,1)} %get-tuple-element.634), channel_id=1, source_target_pairs={{0,8},{8,0},{1,9},{9,1},{2,10},{10,2},{3,11},{11,3},{4,12},{12,4},... | collective-permute-start | bytes 2654216 | tf_op jit(solution)/shard_map/ppermute | solution.py:41
  419.8 34.7 %collective-permute-start.74 = (bf16[608,768]{1,0:T(8,128)(2,1)S(1)}, bf16[608,768]{1,0:T(8,128)(2,1)S(1)}, u32[]{:S(2)}, u32[]{:S(2)}) collective-permute-start(bf16[608,768]{1,0:T(8,128)(2,1)S(1)} %convert_element_type.309), channel_id=1, source_target_pairs={{0,16},{1,17},{2,18},{3,19},{4,20},{5,21},{6,22},{7,23},{8,24},{9,... | collective-permute-start | bytes 2801672 | tf_op jit(solution)/shard_map/ppermute | solution.py:41
  457.8 22.8 %collective-permute-start.75 = (bf16[576,768]{1,0:T(8,128)(2,1)S(1)}, bf16[576,768]{1,0:T(8,128)(2,1)S(1)}, u32[]{:S(2)}, u32[]{:S(2)}) collective-permute-start(bf16[576,768]{1,0:T(8,128)(2,1)S(1)} %convert_element_type.312), channel_id=1, source_target_pairs={{16,0},{17,1},{18,2},{19,3},{20,4},{21,5},{22,6},{23,7},{24,8},{25... | collective-permute-start | bytes 2654216 | tf_op jit(solution)/shard_map/ppermute | solution.py:41
  460.0 48.1 %collective-permute-start.85 = (bf16[576,768]{1,0:T(8,128)(2,1)S(1)}, bf16[576,768]{1,0:T(8,128)(2,1)S(1)}, u32[]{:S(2)}, u32[]{:S(2)}) collective-permute-start(bf16[576,768]{1,0:T(8,128)(2,1)S(1)} %convert_element_type.324), channel_id=1, source_target_pairs={{0,16},{1,17},{2,18},{3,19},{4,20},{5,21},{6,22},{7,23},{8,24},{9,... | collective-permute-start | bytes 2654216 | tf_op jit(solution)/shard_map/ppermute | solution.py:41
  464.7 22.5 %collective-permute-start.83 = (bf16[608,768]{1,0:T(8,128)(2,1)S(1)}, bf16[608,768]{1,0:T(8,128)(2,1)S(1)}, u32[]{:S(2)}, u32[]{:S(2)}) collective-permute-start(bf16[608,768]{1,0:T(8,128)(2,1)S(1)} %get-tuple-element.630), channel_id=1, source_target_pairs={{0,8},{8,0},{1,9},{9,1},{2,10},{10,2},{3,11},{11,3},{4,12},{12,4},... | collective-permute-start | bytes 2801672 | tf_op jit(solution)/shard_map/ppermute | solution.py:41
  481.3 30.1 %collective-permute-start.88 = (bf16[576,768]{1,0:T(8,128)(2,1)S(1)}, bf16[576,768]{1,0:T(8,128)(2,1)S(1)}, u32[]{:S(2)}, u32[]{:S(2)}) collective-permute-start(bf16[576,768]{1,0:T(8,128)(2,1)S(1)} %convert_element_type.329), channel_id=1, source_target_pairs={{2,0},{4,6},{3,1},{5,7},{10,8},{12,14},{11,9},{13,15},{18,16},{20,... | collective-permute-start | bytes 2654216 | tf_op jit(solution)/shard_map/ppermute | solution.py:41
  482.6 24.8 %collective-permute-start.79 = (bf16[576,768]{1,0:T(8,128)(2,1)S(1)}, bf16[576,768]{1,0:T(8,128)(2,1)S(1)}, u32[]{:S(2)}, u32[]{:S(2)}) collective-permute-start(bf16[576,768]{1,0:T(8,128)(2,1)S(1)} %convert_element_type.319), channel_id=1, source_target_pairs={{16,0},{17,1},{18,2},{19,3},{20,4},{21,5},{22,6},{23,7},{24,8},{25... | collective-permute-start | bytes 2654216 | tf_op jit(solution)/shard_map/ppermute | solution.py:41
  489.1 32.7 %collective-permute-start.84 = (bf16[608,768]{1,0:T(8,128)(2,1)S(1)}, bf16[608,768]{1,0:T(8,128)(2,1)S(1)}, u32[]{:S(2)}, u32[]{:S(2)}) collective-permute-start(bf16[608,768]{1,0:T(8,128)(2,1)S(1)} %fusion.33), channel_id=1, source_target_pairs={{16,0},{17,1},{18,2},{19,3},{20,4},{21,5},{22,6},{23,7},{24,8},{25... | collective-permute-start | bytes 2801672 | tf_op jit(solution)/shard_map/ppermute | solution.py:41
  508.6 30.2 %collective-permute-start.86 = (bf16[576,768]{1,0:T(8,128)(2,1)S(1)}, bf16[576,768]{1,0:T(8,128)(2,1)S(1)}, u32[]{:S(2)}, u32[]{:S(2)}) collective-permute-start(bf16[576,768]{1,0:T(8,128)(2,1)S(1)} %get-tuple-element.600), channel_id=1, source_target_pairs={{2,0},{4,6},{3,1},{5,7},{10,8},{12,14},{11,9},{13,15},{18,16},{20,... | collective-permute-start | bytes 2654216 | tf_op jit(solution)/shard_map/ppermute | solution.py:41
  511.6 33.2 %collective-permute-start.89 = (bf16[576,768]{1,0:T(8,128)(2,1)S(1)}, bf16[576,768]{1,0:T(8,128)(2,1)S(1)}, u32[]{:S(2)}, u32[]{:S(2)}) collective-permute-start(bf16[576,768]{1,0:T(8,128)(2,1)S(1)} %add_convert_fusion.3.refs_0_), channel_id=1, source_target_pairs={{0,8},{6,14},{8,0},{14,6},{1,9},{7,15},{9,1},{15,7},{16,24},{22,30... | collective-permute-start | bytes 2654216 | tf_op jit(solution)/shard_map/ppermute | solution.py:41
  563.7 28.9 %collective-permute-start.96 = (bf16[608,768]{1,0:T(8,128)(2,1)S(1)}, bf16[608,768]{1,0:T(8,128)(2,1)}, u32[]{:S(2)}, u32[]{:S(2)}) collective-permute-start(bf16[608,768]{1,0:T(8,128)(2,1)S(1)} %add_convert_fusion.refs_0_), channel_id=1, source_target_pairs={{0,4},{6,2},{1,5},{7,3},{8,12},{14,10},{9,13},{15,11},{16,20},{22,... | collective-permute-start | bytes 2801672 | tf_op jit(solution)/shard_map/ppermute | solution.py:41
  (216 other events, 2243.0 us)

commit v6 on v5

--- a/solution.py
+++ b/solution.py
@@ -13,7 +13,7 @@
 SEGS = 4
 
 FTILE = 256
-HTILE = 384
+HTILE = 768
 PEAK = 1.0e9
 MIB = 1024 * 1024
 
@@ -636,7 +636,7 @@
             jax.ShapeDtypeStruct((length, hidden), low),
         ],
         scratch_shapes=[pltpu.VMEM((length, model), f32)] + glu_scratch(gate_up, down, tile),
-        compiler_params=pltpu.CompilerParams(vmem_limit_bytes=28 * MIB),
+        compiler_params=pltpu.CompilerParams(vmem_limit_bytes=34 * MIB),
         cost_estimate=pl.CostEstimate(flops=int(9 * PEAK), bytes_accessed=0, transcendentals=0),
         name="glu_forward",
     )(places, *blocks, *gate_up, *down)
@@ -704,7 +704,7 @@
             jax.ShapeDtypeStruct((length, hidden), low),
         ],
         scratch_shapes=[pltpu.VMEM((length, model), f32)] + glu_scratch(gate_up, down, tile),
-        compiler_params=pltpu.CompilerParams(vmem_limit_bytes=28 * MIB),
+        compiler_params=pltpu.CompilerParams(vmem_limit_bytes=34 * MIB),
         cost_estimate=pl.CostEstimate(flops=int(9.5 * PEAK), bytes_accessed=0, transcendentals=0),
         name="glu_backward",
     )(places, *blocks, gate, up, *gate_up, *down)

time: 613 us -> 607 us (level)
  Pallas kernels: 140 us -> 132 us
    unnamed x299 -> x301, local copies, waits for them, and re-layouts: 34.4 us -> 35.8 us
where the time goes in v6:
time: 607 us; the launch traced here: 599 us
  waiting for transfers between devices  222 us (37%)
  starting transfers between devices  141 us (23%)
  Pallas kernels  132 us (22%)
  local copies, waits for them, and re-layouts  50.3 us (8%)
  other arithmetic  40.2 us (7%)
  matrix products  9.77 us (2%)
    ppermute x100, waiting for transfers between devices, permute(): return lax.ppermute(values, axes if len(axes) > 1 else axes[0], pairs)  222 us
    ppermute x100, starting transfers between devices, permute(): return lax.ppermute(values, axes if len(axes) > 1 else axes[0], pairs)  141 us
    pallas_call x2, Pallas kernels, mixer_backward(): pl.pallas_call(partial(mixer_grad_kernel, nb, len(w_in_out)), grid=(size...  55.3 us
    pallas_call x2, Pallas kernels, mixer_forward(): pl.pallas_call(partial(mixer_kernel, nb, len(w_in_out)), grid=(size // FT...  49.6 us
    unnamed x301, local copies, waits for them, and re-layouts  35.8 us
  transfers between devices with their start and end apart: 100, of which 37 were waited for; matrix products, arithmetic and copies ran while one was open for 10% of the time, Pallas kernels for 20%

profile of v6, /device:TPU:0, one launch (start us, length us, event | category | flops | bytes accessed | tf_op | source)
XLA Modules:
  0.0 599.1 jit_solution(7982559488302339761)
XLA Ops:
  14.4 5.9 collective-permute-start.2
  38.3 11.1 %collective-permute-start.5 = (bf16[176,768]{1,0:T(8,128)(2,1)S(1)}, bf16[176,768]{1,0:T(8,128)(2,1)S(1)}, u32[]{:S(2)}, u32[]{:S(2)}) collective-permute-start(bf16[176,768]{1,0:T(8,128)(2,1)S(1)} %fusion.9.refs_0_), channel_id=1, source_target_pairs={{0,4},{4,0},{1,5},{5,1},{2,6},{6,2},{3,7},{7,3},{8,12},{12,8},{9,1... | collective-permute-start | bytes 811016 | tf_op jit(solution)/shard_map/ppermute | solution.py:41
  53.8 10.3 %collective-permute-start.9 = (bf16[768,768]{1,0:T(8,128)(2,1)}, bf16[768,768]{1,0:T(8,128)(2,1)}, u32[]{:S(2)}, u32[]{:S(2)}) collective-permute-start(bf16[768,768]{1,0:T(8,128)(2,1)} %bitcast.169), channel_id=1, source_target_pairs={{0,0},{2,4},{4,2},{6,6},{1,1},{3,5},{5,3},{7,7},{8,8},{10,12},{12,... | collective-permute-start | bytes 3538952 | tf_op jit(solution)/shard_map/ppermute | solution.py:41
  72.6 5.0 collective-permute-done.15
  86.5 26.8 %mixer_forward.2 = (f32[176,768]{1,0:T(8,128)}, f32[176,768]{1,0:T(8,128)}, f32[176,768]{1,0:T(8,128)}, f32[176,768]{1,0:T(8,128)}, bf16[4,176,768]{2,1,0:T(8,12...) custom-call(s32[4]{0:T(128)} %pad_add_fusion.1.order, ...), custom_call_target="tpu_custom_call" | custom-call | flops 25999998976 | tf_op jit(solution)/shard_map/mixer_forward/pallas_call | solution.py:332
  115.0 19.5 %collective-permute-start.21 = (f32[176,768]{1,0:T(8,128)S(1)}, f32[176,768]{1,0:T(8,128)S(1)}, u32[]{:S(2)}, u32[]{:S(2)}) collective-permute-start(f32[176,768]{1,0:T(8,128)S(1)} %copy-done.145), channel_id=1, source_target_pairs={{0,4},{4,0},{1,5},{5,1},{2,6},{6,2},{3,7},{7,3},{8,12},{12,8},{9,1... | collective-permute-start | bytes 1622024 | tf_op jit(solution)/shard_map/ppermute | solution.py:41
  140.6 12.4 %collective-permute-done.22 = f32[176,768]{1,0:T(8,128)S(1)} collective-permute-done((f32[176,768]{1,0:T(8,128)S(1)}, f32[176,768]{1,0:T(8,128)S(1)}, u32[]{:S(2)}, u32[]{:S(2)}) %collective-permute-start.22) | collective-permute-done | bytes 540704 | tf_op jit(solution)/shard_map/ppermute | solution.py:41
  155.4 6.4 %collective-permute-done.23.refs_1_ = bf16[176,768]{1,0:T(8,128)(2,1)S(1)} collective-permute-done((bf16[176,768]{1,0:T(8,128)(2,1)S(1)}, bf16[176,768]{1,0:T(8,128)(2,1)S(1)}, u32[]{:S(2)}, u32[]{:S(2)}) %collective-permute-start.23) | collective-permute-done | bytes 270368 | tf_op jit(solution)/shard_map/ppermute | solution.py:41
  161.9 6.2 %collective-permute-done.26.refs_5_.refs_7_ = bf16[768,768]{1,0:T(8,128)(2,1)S(1)} collective-permute-done((bf16[768,768]{1,0:T(8,128)(2,1)S(1)}, bf16[768,768]{1,0:T(8,128)(2,1)S(1)}, u32[]{:S(2)}, u32[]{:S(2)}) %collective-permute-start.26) | collective-permute-done | bytes 1179680 | tf_op jit(solution)/shard_map/ppermute | solution.py:41
  179.1 11.8 %collective-permute-done.29 = f32[176,768]{1,0:T(8,128)S(1)} collective-permute-done((f32[176,768]{1,0:T(8,128)S(1)}, f32[176,768]{1,0:T(8,128)S(1)}, u32[]{:S(2)}, u32[]{:S(2)}) %collective-permute-start.29) | collective-permute-done | bytes 540704 | tf_op jit(solution)/shard_map/ppermute | solution.py:41
  192.0 7.3 %collective-permute-done.30.refs_1_ = bf16[176,768]{1,0:T(8,128)(2,1)S(1)} collective-permute-done((bf16[176,768]{1,0:T(8,128)(2,1)S(1)}, bf16[176,768]{1,0:T(8,128)(2,1)S(1)}, u32[]{:S(2)}, u32[]{:S(2)}) %collective-permute-start.30) | collective-permute-done | bytes 270368 | tf_op jit(solution)/shard_map/ppermute | solution.py:41
  199.7 5.1 collective-permute-done.34.refs_7_
  205.3 22.8 %mixer_forward.3 = (f32[176,768]{1,0:T(8,128)S(1)}, f32[176,768]{1,0:T(8,128)S(1)}, f32[176,768]{1,0:T(8,128)S(1)}, f32[176,768]{1,0:T(8,128)S(1)}, bf16[4,176,7...) custom-call(s32[4]{0:T(128)S(1)} %copy-done.25, ...), custom_call_target="tpu_custom_call" | custom-call | flops 25999998976 | tf_op jit(solution)/shard_map/mixer_forward/pallas_call | solution.py:332
  235.4 12.0 %collective-permute-done.42.refs_7_.refs_9_ = bf16[384,768]{1,0:T(8,128)(2,1)S(1)} collective-permute-done((bf16[384,768]{1,0:T(8,128)(2,1)S(1)}, bf16[384,768]{1,0:T(8,128)(2,1)S(1)}, u32[]{:S(2)}, u32[]{:S(2)}) %collective-permute-start.42) | collective-permute-done | bytes 589856 | tf_op jit(solution)/shard_map/ppermute | solution.py:41
  250.4 6.0 %collective-permute-done.43.refs_1_ = bf16[176,768]{1,0:T(8,128)(2,1)S(1)} collective-permute-done((bf16[176,768]{1,0:T(8,128)(2,1)S(1)}, bf16[176,768]{1,0:T(8,128)(2,1)S(1)}, u32[]{:S(2)}, u32[]{:S(2)}) %collective-permute-start.43) | collective-permute-done | bytes 270368 | tf_op jit(solution)/shard_map/ppermute | solution.py:41
  264.4 5.2 glu_backward.2
  276.0 13.0 %collective-permute-done.48 = f32[176,768]{1,0:T(8,128)} collective-permute-done((f32[176,768]{1,0:T(8,128)}, f32[176,768]{1,0:T(8,128)}, u32[]{:S(2)}, u32[]{:S(2)}) %collective-permute-start.48) | collective-permute-done | bytes 540704 | tf_op jit(solution)/shard_map/ppermute | solution.py:41
  306.8 28.3 %mixer_backward.2 = (f32[176,768]{1,0:T(8,128)S(1)}, f32[176,768]{1,0:T(8,128)S(1)}, f32[176,768]{1,0:T(8,128)}, f32[176,768]{1,0:T(8,128)}, bf16[4,176,768]{2,1...) custom-call(s32[4]{0:T(128)S(1)} %copy-done.25, ...), custom_call_target="tpu_custom_call" | custom-call | flops 30000001024 | tf_op jit(solution)/shard_map/mixer_backward/pallas_call | solution.py:505
  349.4 9.6 %collective-permute-done.59 = f32[176,768]{1,0:T(8,128)S(1)} collective-permute-done((f32[176,768]{1,0:T(8,128)S(1)}, f32[176,768]{1,0:T(8,128)S(1)}, u32[]{:S(2)}, u32[]{:S(2)}) %collective-permute-start.59) | collective-permute-done | bytes 540704 | tf_op jit(solution)/shard_map/ppermute | solution.py:41
  364.4 7.9 %collective-permute-done.60.refs_1_ = bf16[176,768]{1,0:T(8,128)(2,1)S(1)} collective-permute-done((bf16[176,768]{1,0:T(8,128)(2,1)S(1)}, bf16[176,768]{1,0:T(8,128)(2,1)S(1)}, u32[]{:S(2)}, u32[]{:S(2)}) %collective-permute-start.60) | collective-permute-done | bytes 270368 | tf_op jit(solution)/shard_map/ppermute | solution.py:41
  381.5 5.4 collective-permute-start.76
  394.4 7.1 %collective-permute-done.66 = f32[176,768]{1,0:T(8,128)S(1)} collective-permute-done((f32[176,768]{1,0:T(8,128)S(1)}, f32[176,768]{1,0:T(8,128)S(1)}, u32[]{:S(2)}, u32[]{:S(2)}) %collective-permute-start.66) | collective-permute-done | bytes 540704 | tf_op jit(solution)/shard_map/ppermute | solution.py:41
  403.4 6.4 %collective-permute-done.68.refs_1_ = bf16[176,768]{1,0:T(8,128)(2,1)S(1)} collective-permute-done((bf16[176,768]{1,0:T(8,128)(2,1)S(1)}, bf16[176,768]{1,0:T(8,128)(2,1)S(1)}, u32[]{:S(2)}, u32[]{:S(2)}) %collective-permute-start.68) | collective-permute-done | bytes 270368 | tf_op jit(solution)/shard_map/ppermute | solution.py:41
  415.4 27.0 %mixer_backward.3 = (f32[176,768]{1,0:T(8,128)S(1)}, f32[176,768]{1,0:T(8,128)S(1)}, f32[176,768]{1,0:T(8,128)S(1)}, f32[176,768]{1,0:T(8,128)S(1)}, bf16[4,176,...) custom-call(s32[4]{0:T(128)S(1)} %copy-done.25, ...), custom_call_target="tpu_custom_call" | custom-call | flops 30000001024 | tf_op jit(solution)/shard_map/mixer_backward/pallas_call | solution.py:505
  442.5 5.1 collective-permute-done.73
  459.9 13.8 %collective-permute-done.75 = bf16[576,768]{1,0:T(8,128)(2,1)S(1)} collective-permute-done((bf16[576,768]{1,0:T(8,128)(2,1)S(1)}, bf16[576,768]{1,0:T(8,128)(2,1)S(1)}, u32[]{:S(2)}, u32[]{:S(2)}) %collective-permute-start.75) | collective-permute-done | bytes 884768 | tf_op jit(solution)/shard_map/ppermute | solution.py:41
  483.5 17.0 %collective-permute-done.82 = bf16[1,176,768]{2,1,0:T(8,128)(2,1)S(1)} collective-permute-done((bf16[1,176,768]{2,1,0:T(8,128)(2,1)S(1)}, bf16[1,176,768]{2,1,0:T(8,128)(2,1)S(1)}, u32[]{:S(2)}, u32[]{:S(2)}) %collective-permute-start.82) | collective-permute-done | bytes 270368 | tf_op jit(solution)/shard_map/ppermute | solution.py:41
  507.1 7.9 %collective-permute-done.84 = bf16[608,768]{1,0:T(8,128)(2,1)S(1)} collective-permute-done((bf16[608,768]{1,0:T(8,128)(2,1)S(1)}, bf16[608,768]{1,0:T(8,128)(2,1)S(1)}, u32[]{:S(2)}, u32[]{:S(2)}) %collective-permute-start.84) | collective-permute-done | bytes 933920 | tf_op jit(solution)/shard_map/ppermute | solution.py:41
  515.0 17.0 %collective-permute-done.86 = bf16[576,768]{1,0:T(8,128)(2,1)S(1)} collective-permute-done((bf16[576,768]{1,0:T(8,128)(2,1)S(1)}, bf16[576,768]{1,0:T(8,128)(2,1)S(1)}, u32[]{:S(2)}, u32[]{:S(2)}) %collective-permute-start.86) | collective-permute-done | bytes 884768 | tf_op jit(solution)/shard_map/ppermute | solution.py:41
  540.6 7.2 %collective-permute-done.92.refs_5_ = bf16[576,768]{1,0:T(8,128)(2,1)S(1)} collective-permute-done((bf16[576,768]{1,0:T(8,128)(2,1)S(1)}, bf16[576,768]{1,0:T(8,128)(2,1)S(1)}, u32[]{:S(2)}, u32[]{:S(2)}) %collective-permute-start.92) | collective-permute-done | bytes 884768 | tf_op jit(solution)/shard_map/ppermute | solution.py:41
  559.1 10.4 %collective-permute-done.95.refs_1_ = bf16[608,768]{1,0:T(8,128)(2,1)} collective-permute-done((bf16[608,768]{1,0:T(8,128)(2,1)S(1)}, bf16[608,768]{1,0:T(8,128)(2,1)}, u32[]{:S(2)}, u32[]{:S(2)}) %collective-permute-start.95) | collective-permute-done | bytes 933920 | tf_op jit(solution)/shard_map/ppermute | solution.py:41
  578.9 4.8 assemble.3
  (632 shorter events, 234.2 us)
Async XLA Ops:
  1.5 30.4 %collective-permute-start.3 = (f32[2,768]{1,0:T(2,128)S(1)}, f32[2,768]{1,0:T(2,128)S(1)}, u32[]{:S(2)}, u32[]{:S(2)}) collective-permute-start(f32[2,768]{1,0:T(2,128)S(1)} %pad_maximum_fusion.6), channel_id=1, source_target_pairs={{0,16},{16,0},{1,17},{17,1},{2,18},{18,2},{3,19},{19,3},{4,20},{20... | collective-permute-start | bytes 18440 | tf_op jit(solution)/shard_map/ppermute | solution.py:41
  5.2 46.3 %collective-permute-start.16 = (f32[2,704]{1,0:T(2,128)S(1)}, f32[2,704]{1,0:T(2,128)S(1)}, u32[]{:S(2)}, u32[]{:S(2)}) collective-permute-start(f32[2,704]{1,0:T(2,128)S(1)} %convert_element_type.269), channel_id=1, source_target_pairs={{0,4},{4,0},{1,5},{5,1},{2,6},{6,2},{3,7},{7,3},{8,12},{12,8},{9,1... | collective-permute-start | bytes 16904 | tf_op jit(solution)/shard_map/ppermute | solution.py:41
  6.9 25.1 %collective-permute-start = (bf16[1,176,768]{2,1,0:T(8,128)(2,1)}, bf16[1,176,768]{2,1,0:T(8,128)(2,1)S(1)}, u32[]{:S(2)}, u32[]{:S(2)}) collective-permute-start(bf16[1,176,768]{2,1,0:T(8,128)(2,1)} %constant_dynamic-slice_fusion.3), channel_id=1, source_target_pairs={{0,0},{2,4},{4,2},{6,6},{1,1},{3,5},{5,3},{7,7},{8,8},{10,12},{12,... | collective-permute-start | bytes 811016 | tf_op jit(solution)/shard_map/ppermute | solution.py:41
  10.7 21.3 %collective-permute-start.1 = (bf16[384,768]{1,0:T(8,128)(2,1)}, bf16[384,768]{1,0:T(8,128)(2,1)S(1)}, u32[]{:S(2)}, u32[]{:S(2)}) collective-permute-start(bf16[384,768]{1,0:T(8,128)(2,1)} %fusion.6), channel_id=1, source_target_pairs={{0,0},{2,4},{4,2},{6,6},{1,1},{3,5},{5,3},{7,7},{8,8},{10,12},{12,... | collective-permute-start | bytes 1769480 | tf_op jit(solution)/shard_map/ppermute | solution.py:41
  34.3 29.9 %collective-permute-start.7 = (bf16[384,768]{1,0:T(8,128)(2,1)S(1)}, bf16[384,768]{1,0:T(8,128)(2,1)S(1)}, u32[]{:S(2)}, u32[]{:S(2)}) collective-permute-start(bf16[384,768]{1,0:T(8,128)(2,1)S(1)} %collective-permute-done.1), channel_id=1, source_target_pairs={{0,16},{16,0},{1,17},{17,1},{2,18},{18,2},{3,19},{19,3},{4,20},{20... | collective-permute-start | bytes 1769480 | tf_op jit(solution)/shard_map/ppermute | solution.py:41
  35.5 28.6 %collective-permute-start.8 = (f32[192,705]{1,0:T(8,128)}, f32[192,705]{1,0:T(8,128)S(1)}, u32[]{:S(2)}, u32[]{:S(2)}) collective-permute-start(f32[192,705]{1,0:T(8,128)} %collective-permute-done.2), channel_id=1, source_target_pairs={{0,16},{16,0},{1,17},{17,1},{2,18},{18,2},{3,19},{19,3},{4,20},{20... | collective-permute-start | bytes 1624328 | tf_op jit(solution)/shard_map/ppermute | solution.py:41
  53.8 24.4 %collective-permute-start.9 = (bf16[768,768]{1,0:T(8,128)(2,1)}, bf16[768,768]{1,0:T(8,128)(2,1)}, u32[]{:S(2)}, u32[]{:S(2)}) collective-permute-start(bf16[768,768]{1,0:T(8,128)(2,1)} %bitcast.169), channel_id=1, source_target_pairs={{0,0},{2,4},{4,2},{6,6},{1,1},{3,5},{5,3},{7,7},{8,8},{10,12},{12,... | collective-permute-start | bytes 3538952 | tf_op jit(solution)/shard_map/ppermute | solution.py:41
  79.5 35.4 %collective-permute-start.18 = (bf16[1,176,768]{2,1,0:T(8,128)(2,1)}, bf16[1,176,768]{2,1,0:T(8,128)(2,1)S(1)}, u32[]{:S(2)}, u32[]{:S(2)}) collective-permute-start(bf16[1,176,768]{2,1,0:T(8,128)(2,1)} %constant_dynamic-slice_fusion), channel_id=1, source_target_pairs={{0,0},{2,4},{4,2},{6,6},{1,1},{3,5},{5,3},{7,7},{8,8},{10,12},{12,... | collective-permute-start | bytes 811016 | tf_op jit(solution)/shard_map/ppermute | solution.py:41
  81.3 33.7 %collective-permute-start.19 = (bf16[384,768]{1,0:T(8,128)(2,1)S(1)}, bf16[384,768]{1,0:T(8,128)(2,1)S(1)}, u32[]{:S(2)}, u32[]{:S(2)}) collective-permute-start(bf16[384,768]{1,0:T(8,128)(2,1)S(1)} %get-tuple-element.319.refs_6_.refs_8_), channel_id=1, source_target_pairs={{0,8},{8,0},{1,9},{9,1},{2,10},{10,2},{3,11},{11,3},{4,12},{12,4},... | collective-permute-start | bytes 1769480 | tf_op jit(solution)/shard_map/ppermute | solution.py:41
  82.9 30.5 %collective-permute-start.17 = (bf16[768,768]{1,0:T(8,128)(2,1)}, bf16[768,768]{1,0:T(8,128)(2,1)S(1)}, u32[]{:S(2)}, u32[]{:S(2)}) collective-permute-start(bf16[768,768]{1,0:T(8,128)(2,1)} %collective-permute-done.9), channel_id=1, source_target_pairs={{0,16},{16,0},{1,17},{17,1},{2,18},{18,2},{3,19},{19,3},{4,20},{20... | collective-permute-start | bytes 3538952 | tf_op jit(solution)/shard_map/ppermute | solution.py:41
  140.1 28.0 %collective-permute-start.26 = (bf16[768,768]{1,0:T(8,128)(2,1)S(1)}, bf16[768,768]{1,0:T(8,128)(2,1)S(1)}, u32[]{:S(2)}, u32[]{:S(2)}) collective-permute-start(bf16[768,768]{1,0:T(8,128)(2,1)S(1)} %get-tuple-element.318.refs_4_.refs_6_), channel_id=1, source_target_pairs={{0,8},{8,0},{1,9},{9,1},{2,10},{10,2},{3,11},{11,3},{4,12},{12,4},... | collective-permute-start | bytes 3538952 | tf_op jit(solution)/shard_map/ppermute | solution.py:41
  177.0 28.2 %collective-permute-start.33 = (bf16[384,768]{1,0:T(8,128)(2,1)S(1)}, bf16[384,768]{1,0:T(8,128)(2,1)S(1)}, u32[]{:S(2)}, u32[]{:S(2)}) collective-permute-start(bf16[384,768]{1,0:T(8,128)(2,1)S(1)} %copy-done.8), channel_id=1, source_target_pairs={{0,8},{8,0},{1,9},{9,1},{2,10},{10,2},{3,11},{11,3},{4,12},{12,4},... | collective-permute-start | bytes 1769480 | tf_op jit(solution)/shard_map/ppermute | solution.py:41
  177.5 27.3 %collective-permute-start.34 = (f32[192,705]{1,0:T(8,128)S(1)}, f32[192,705]{1,0:T(8,128)S(1)}, u32[]{:S(2)}, u32[]{:S(2)}) collective-permute-start(f32[192,705]{1,0:T(8,128)S(1)} %copy-done.9), channel_id=1, source_target_pairs={{0,8},{8,0},{1,9},{9,1},{2,10},{10,2},{3,11},{11,3},{4,12},{12,4},... | collective-permute-start | bytes 1624328 | tf_op jit(solution)/shard_map/ppermute | solution.py:41
  199.4 30.0 %collective-permute-start.35 = (bf16[176,768]{1,0:T(8,128)(2,1)S(1)}, bf16[176,768]{1,0:T(8,128)(2,1)S(1)}, u32[]{:S(2)}, u32[]{:S(2)}) collective-permute-start(bf16[176,768]{1,0:T(8,128)(2,1)S(1)} %bitcast.176), channel_id=1, source_target_pairs={{0,1},{1,0},{2,3},{3,2},{4,5},{5,4},{6,7},{7,6},{8,9},{9,8},{10,11... | collective-permute-start | bytes 811016 | tf_op jit(solution)/shard_map/ppermute | solution.py:41
  204.8 26.9 %collective-permute-start.38 = (bf16[768,768]{1,0:T(8,128)(2,1)S(1)}, bf16[768,768]{1,0:T(8,128)(2,1)S(1)}, u32[]{:S(2)}, u32[]{:S(2)}) collective-permute-start(bf16[768,768]{1,0:T(8,128)(2,1)S(1)} %get-tuple-element.345.refs_4_.refs_6_), channel_id=1, source_target_pairs={{0,8},{8,0},{1,9},{9,1},{2,10},{10,2},{3,11},{11,3},{4,12},{12,4},... | collective-permute-start | bytes 3538952 | tf_op jit(solution)/shard_map/ppermute | solution.py:41
  300.0 38.4 %collective-permute-start.56 = (bf16[576,768]{1,0:T(8,128)(2,1)S(1)}, bf16[576,768]{1,0:T(8,128)(2,1)}, u32[]{:S(2)}, u32[]{:S(2)}) collective-permute-start(bf16[576,768]{1,0:T(8,128)(2,1)S(1)} %dynamic-slice_bitcast_fusion.8), channel_id=1, source_target_pairs={{0,8},{8,0},{1,9},{9,1},{2,10},{10,2},{3,11},{11,3},{4,12},{12,4},... | collective-permute-start | bytes 2654216 | tf_op jit(solution)/shard_map/ppermute | solution.py:41
  302.3 38.5 %collective-permute-start.55 = (bf16[576,768]{1,0:T(8,128)(2,1)S(1)}, bf16[576,768]{1,0:T(8,128)(2,1)}, u32[]{:S(2)}, u32[]{:S(2)}) collective-permute-start(bf16[576,768]{1,0:T(8,128)(2,1)S(1)} %dynamic-slice_bitcast_fusion.9), channel_id=1, source_target_pairs={{0,8},{8,0},{1,9},{9,1},{2,10},{10,2},{3,11},{11,3},{4,12},{12,4},... | collective-permute-start | bytes 2654216 | tf_op jit(solution)/shard_map/ppermute | solution.py:41
  305.0 33.5 %collective-permute-start.54 = (f32[176,768]{1,0:T(8,128)S(1)}, f32[176,768]{1,0:T(8,128)}, u32[]{:S(2)}, u32[]{:S(2)}) collective-permute-start(f32[176,768]{1,0:T(8,128)S(1)} %add.304), channel_id=1, source_target_pairs={{0,1},{1,0},{2,3},{3,2},{4,5},{5,4},{6,7},{7,6},{8,9},{9,8},{10,11... | collective-permute-start | bytes 1622024 | tf_op jit(solution)/shard_map/ppermute | solution.py:41
  381.5 78.5 %collective-permute-start.76 = (bf16[576,768]{1,0:T(8,128)(2,1)}, bf16[576,768]{1,0:T(8,128)(2,1)}, u32[]{:S(2)}, u32[]{:S(2)}) collective-permute-start(bf16[576,768]{1,0:T(8,128)(2,1)} %convert_element_type.313), channel_id=1, source_target_pairs={{0,16},{1,17},{2,18},{3,19},{4,20},{5,21},{6,22},{7,23},{8,24},{9,... | collective-permute-start | bytes 2654216 | tf_op jit(solution)/shard_map/ppermute | solution.py:41
  386.8 24.1 %collective-permute-start.71 = (bf16[608,768]{1,0:T(8,128)(2,1)S(1)}, bf16[608,768]{1,0:T(8,128)(2,1)S(1)}, u32[]{:S(2)}, u32[]{:S(2)}) collective-permute-start(bf16[608,768]{1,0:T(8,128)(2,1)S(1)} %get-tuple-element.632), channel_id=1, source_target_pairs={{0,8},{8,0},{1,9},{9,1},{2,10},{10,2},{3,11},{11,3},{4,12},{12,4},... | collective-permute-start | bytes 2801672 | tf_op jit(solution)/shard_map/ppermute | solution.py:41
  390.6 51.9 %collective-permute-start.72 = (bf16[576,768]{1,0:T(8,128)(2,1)}, bf16[576,768]{1,0:T(8,128)(2,1)}, u32[]{:S(2)}, u32[]{:S(2)}) collective-permute-start(bf16[576,768]{1,0:T(8,128)(2,1)} %get-tuple-element.636), channel_id=1, source_target_pairs={{0,8},{8,0},{1,9},{9,1},{2,10},{10,2},{3,11},{11,3},{4,12},{12,4},... | collective-permute-start | bytes 2654216 | tf_op jit(solution)/shard_map/ppermute | solution.py:41
  411.0 36.7 %collective-permute-start.73 = (bf16[576,768]{1,0:T(8,128)(2,1)}, bf16[576,768]{1,0:T(8,128)(2,1)}, u32[]{:S(2)}, u32[]{:S(2)}) collective-permute-start(bf16[576,768]{1,0:T(8,128)(2,1)} %get-tuple-element.634), channel_id=1, source_target_pairs={{0,8},{8,0},{1,9},{9,1},{2,10},{10,2},{3,11},{11,3},{4,12},{12,4},... | collective-permute-start | bytes 2654216 | tf_op jit(solution)/shard_map/ppermute | solution.py:41
  413.0 34.7 %collective-permute-start.74 = (bf16[608,768]{1,0:T(8,128)(2,1)S(1)}, bf16[608,768]{1,0:T(8,128)(2,1)S(1)}, u32[]{:S(2)}, u32[]{:S(2)}) collective-permute-start(bf16[608,768]{1,0:T(8,128)(2,1)S(1)} %convert_element_type.309), channel_id=1, source_target_pairs={{0,16},{1,17},{2,18},{3,19},{4,20},{5,21},{6,22},{7,23},{8,24},{9,... | collective-permute-start | bytes 2801672 | tf_op jit(solution)/shard_map/ppermute | solution.py:41
  450.9 22.8 %collective-permute-start.75 = (bf16[576,768]{1,0:T(8,128)(2,1)S(1)}, bf16[576,768]{1,0:T(8,128)(2,1)S(1)}, u32[]{:S(2)}, u32[]{:S(2)}) collective-permute-start(bf16[576,768]{1,0:T(8,128)(2,1)S(1)} %convert_element_type.312), channel_id=1, source_target_pairs={{16,0},{17,1},{18,2},{19,3},{20,4},{21,5},{22,6},{23,7},{24,8},{25... | collective-permute-start | bytes 2654216 | tf_op jit(solution)/shard_map/ppermute | solution.py:41
  453.1 48.1 %collective-permute-start.85 = (bf16[576,768]{1,0:T(8,128)(2,1)S(1)}, bf16[576,768]{1,0:T(8,128)(2,1)S(1)}, u32[]{:S(2)}, u32[]{:S(2)}) collective-permute-start(bf16[576,768]{1,0:T(8,128)(2,1)S(1)} %convert_element_type.324), channel_id=1, source_target_pairs={{0,16},{1,17},{2,18},{3,19},{4,20},{5,21},{6,22},{7,23},{8,24},{9,... | collective-permute-start | bytes 2654216 | tf_op jit(solution)/shard_map/ppermute | solution.py:41
  457.8 22.5 %collective-permute-start.83 = (bf16[608,768]{1,0:T(8,128)(2,1)S(1)}, bf16[608,768]{1,0:T(8,128)(2,1)S(1)}, u32[]{:S(2)}, u32[]{:S(2)}) collective-permute-start(bf16[608,768]{1,0:T(8,128)(2,1)S(1)} %get-tuple-element.630), channel_id=1, source_target_pairs={{0,8},{8,0},{1,9},{9,1},{2,10},{10,2},{3,11},{11,3},{4,12},{12,4},... | collective-permute-start | bytes 2801672 | tf_op jit(solution)/shard_map/ppermute | solution.py:41
  474.4 30.1 %collective-permute-start.88 = (bf16[576,768]{1,0:T(8,128)(2,1)S(1)}, bf16[576,768]{1,0:T(8,128)(2,1)S(1)}, u32[]{:S(2)}, u32[]{:S(2)}) collective-permute-start(bf16[576,768]{1,0:T(8,128)(2,1)S(1)} %convert_element_type.329), channel_id=1, source_target_pairs={{2,0},{4,6},{3,1},{5,7},{10,8},{12,14},{11,9},{13,15},{18,16},{20,... | collective-permute-start | bytes 2654216 | tf_op jit(solution)/shard_map/ppermute | solution.py:41
  475.7 24.8 %collective-permute-start.79 = (bf16[576,768]{1,0:T(8,128)(2,1)S(1)}, bf16[576,768]{1,0:T(8,128)(2,1)S(1)}, u32[]{:S(2)}, u32[]{:S(2)}) collective-permute-start(bf16[576,768]{1,0:T(8,128)(2,1)S(1)} %convert_element_type.319), channel_id=1, source_target_pairs={{16,0},{17,1},{18,2},{19,3},{20,4},{21,5},{22,6},{23,7},{24,8},{25... | collective-permute-start | bytes 2654216 | tf_op jit(solution)/shard_map/ppermute | solution.py:41
  482.2 32.8 %collective-permute-start.84 = (bf16[608,768]{1,0:T(8,128)(2,1)S(1)}, bf16[608,768]{1,0:T(8,128)(2,1)S(1)}, u32[]{:S(2)}, u32[]{:S(2)}) collective-permute-start(bf16[608,768]{1,0:T(8,128)(2,1)S(1)} %fusion.33), channel_id=1, source_target_pairs={{16,0},{17,1},{18,2},{19,3},{20,4},{21,5},{22,6},{23,7},{24,8},{25... | collective-permute-start | bytes 2801672 | tf_op jit(solution)/shard_map/ppermute | solution.py:41
  501.8 30.2 %collective-permute-start.86 = (bf16[576,768]{1,0:T(8,128)(2,1)S(1)}, bf16[576,768]{1,0:T(8,128)(2,1)S(1)}, u32[]{:S(2)}, u32[]{:S(2)}) collective-permute-start(bf16[576,768]{1,0:T(8,128)(2,1)S(1)} %get-tuple-element.600), channel_id=1, source_target_pairs={{2,0},{4,6},{3,1},{5,7},{10,8},{12,14},{11,9},{13,15},{18,16},{20,... | collective-permute-start | bytes 2654216 | tf_op jit(solution)/shard_map/ppermute | solution.py:41
  504.8 33.1 %collective-permute-start.89 = (bf16[576,768]{1,0:T(8,128)(2,1)S(1)}, bf16[576,768]{1,0:T(8,128)(2,1)S(1)}, u32[]{:S(2)}, u32[]{:S(2)}) collective-permute-start(bf16[576,768]{1,0:T(8,128)(2,1)S(1)} %add_convert_fusion.3.refs_0_), channel_id=1, source_target_pairs={{0,8},{6,14},{8,0},{14,6},{1,9},{7,15},{9,1},{15,7},{16,24},{22,30... | collective-permute-start | bytes 2654216 | tf_op jit(solution)/shard_map/ppermute | solution.py:41
  556.9 28.9 %collective-permute-start.96 = (bf16[608,768]{1,0:T(8,128)(2,1)S(1)}, bf16[608,768]{1,0:T(8,128)(2,1)}, u32[]{:S(2)}, u32[]{:S(2)}) collective-permute-start(bf16[608,768]{1,0:T(8,128)(2,1)S(1)} %add_convert_fusion.refs_0_), channel_id=1, source_target_pairs={{0,4},{6,2},{1,5},{7,3},{8,12},{14,10},{9,13},{15,11},{16,20},{22,... | collective-permute-start | bytes 2801672 | tf_op jit(solution)/shard_map/ppermute | solution.py:41
  (217 other events, 2223.9 us)
